TPU v7x, 32 devices: a whole 2x2x4 slice. The times are simulated.
32 devices in a mesh: groups: 2 (over x), blk: 16 (over z, y, core).
Axes of the slice: x: 2, y: 2, z: 4, core: 2. Of those that a mesh axis runs over, the one named last changes fastest.
Arguments:
- rows: bfloat16 [131072, 768], P(('groups', 'blk')), parts along dimension 0, may hold values from -8 to 8, as said below
- centroids: bfloat16 [8192, 768], P(('groups', 'blk')), parts along dimension 0, may hold values from -4 to 4, as said below
- lists: int32 [512, 6], P(('groups', 'blk')), parts along dimension 0, may hold values from 0 to 15, as said below
Outputs:
- new_centroids: float32 [8192, 768], P(('groups', 'blk')), parts along dimension 0
- log_totals: float32 [131072], P(('groups', 'blk')), parts along dimension 0
There are 2 independent parts, one for each index of `groups`. A program takes and returns all parts, laid end to end along the dimension named above; each array names one. Nothing has to cross between parts.
Inputs may be any that keep to these rules, and one draw needn't show every extreme that they name: `rows`: embeddings of order one. `centroids`: centroids of order one half. `lists`: the 6 entries of a block are distinct panel numbers. Block b is held by device q = b // 16 along blk; every listed panel lies within cycle distance 6 of panel q (indices taken modulo 16), panel q itself is always listed, and distance 6 is reached. Panels are listed unevenly.
All inputs are finite; a program needn't handle non-finite values.
Results may differ from a plain program's by a relative error of at most 0.00056.
Values may be sent and summed in bfloat16 or wider, within the bound.
No kernel may reach another device: no remote copies, remote signals or barrier semaphores. Data moves between devices by JAX's collectives and lax.ppermute only.
A program may use at most 128 MiB of HBM per device.

v0:
```python
import functools
import math

import jax
import jax.numpy as jnp
from jax import lax
from jax.experimental import pallas as pl
from jax.experimental.pallas import tpu as pltpu
from jax.sharding import PartitionSpec as P

BLOCK = 256
SPAN = 6
LOGIT_SCALE = 0.25
PRIOR_MASS = 8.0
LOG2E = math.log2(math.e)
LINK_SCALE = 1.0 / 16.0
EXTRA = 8
DEPTH = 4


def grid_plan():
    return 0, (
        ((2, 0, 4), (1, 0, None)),
        ((6, 0, -4), (3, 2, None)),
        ((5, 3, 4), (7, 6, None)),
    )


def ring_plan():
    reach = (SPAN + 1) // 2
    return reach, tuple(
        ((reach + hop + 1, reach + hop, 2), (reach - hop - 1, reach - hop, -2)) for hop in range(reach)
    )


def plan_of(count):
    return grid_plan() if count == 16 else ring_plan()


def chip_place(panel, device, count):
    if count == 16:
        return (device // 4 - panel // 4) % 4 * 2 + ((panel ^ device) >> 1 & 1)
    return (device // 2 - panel // 2 + (SPAN + 1) // 2) % (count // 2)


def moved(value, shift):
    count = lax.axis_size("blk")
    if shift is None:
        return lax.ppermute(value, "blk", [(i, i ^ 2) for i in range(count)])
    return lax.ppermute(value, "blk", [(i, (i + shift) % count) for i in range(count)])


def other_core(value):
    count = lax.axis_size("blk")
    return lax.ppermute(value, "blk", [(i, i ^ 1) for i in range(count)])


def collect(slots_ref, members, ids_ref, blocks, listed):
    def one_block(b, found):
        for l in range(listed):
            chip = slots_ref[b * listed + l] >> 1
            hit = functools.reduce(jnp.logical_or, [chip == m for m in members])
            ids_ref[found] = 8 * b + l
            found = found + hit.astype(jnp.int32)
        return found

    return lax.fori_loop(0, blocks, one_block, jnp.int32(0))


def local_place(slot, members):
    if len(members) == 1:
        return slot & 1
    return (slot & 1) + 2 * ((slot >> 1) == members[1]).astype(jnp.int32)


def start_rows(rows_ref, x, sem):
    for b in range(x.shape[0]):
        pltpu.make_async_copy(rows_ref.at[pl.ds(b * BLOCK, BLOCK)], x.at[b], sem.at[b]).start()


def await_rows(rows_ref, x, sem, ready, upto):
    def one(b, _):
        pltpu.make_async_copy(rows_ref.at[pl.ds(0, BLOCK)], x.at[b], sem.at[b]).wait()
        return 0

    lax.fori_loop(ready, upto, one, 0)
    return jnp.maximum(ready, upto)


def load_panels(piece_refs, panels, norms, sem):
    copies = [
        pltpu.make_async_copy(ref, panels.at[p], sem.at[p]) for p, ref in enumerate(piece_refs)
    ]
    for copy in copies:
        copy.start()

    def finish():
        for copy in copies:
            copy.wait()
        for p in range(len(copies)):
            wide = panels[p].astype(jnp.float32)
            norm = jnp.sum(wide * wide, axis=1, keepdims=True)
            norms[p] = jnp.broadcast_to(norm * (0.5 * LOGIT_SCALE * LOG2E), norms.shape[1:])

    return finish


def tile_of(panel, norm, block):
    scores = lax.dot_general(
        panel, block, (((1,), (1,)), ((), ())), preferred_element_type=jnp.float32
    )
    scores = scores * (LOGIT_SCALE * LOG2E) - jnp.concatenate([norm, norm], axis=1)
    top = jnp.max(scores, axis=0, keepdims=True)
    powers = jnp.exp2(scores - top)
    return powers, top, jnp.sum(powers, axis=0, keepdims=True)


def score_loop(members, slots_ref, ids, found, listed, x, panels, norms, tops, masses, wait_rows, put):
    blocks = x.shape[0]
    tops[...] = jnp.full_like(tops, -jnp.inf)
    masses[...] = jnp.zeros_like(masses)

    def two(half, ready):
        work = []
        for side in range(2):
            j = 2 * half + side
            code = ids[jnp.minimum(j, found - 1)]
            b, l = code >> 3, code & 7
            work.append((j, b, l, local_place(slots_ref[b * listed + l], members)))
        ready = wait_rows(ready, work[1][1] + 1)
        tiles = [tile_of(panels[p], norms[p], x[b]) for _, b, _, p in work]
        for (j, b, l, _), (powers, top, mass) in zip(work, tiles):
            put(j, powers)
            tops[pl.ds(l * blocks + b, 1)] = top
            masses[pl.ds(l * blocks + b, 1)] = mass
        return ready

    return lax.fori_loop(0, (found + 1) // 2, two, jnp.int32(0))


def sum_loop(members, slots_ref, ids, found, listed, x, shares, acc, totals, wait_rows, ready, get):
    blocks = x.shape[0]
    cent = totals.shape[1]

    def two(half, ready):
        work = []
        for side in range(2):
            j = 2 * half + side
            code = ids[jnp.minimum(j, found - 1)]
            b, l = code >> 3, code & 7
            work.append((j, b, l, local_place(slots_ref[b * listed + l], members)))
        ready = wait_rows(ready, work[1][1] + 1)
        live = (work[1][0] < found).astype(jnp.float32)
        for side, (j, b, l, p) in enumerate(work):
            share = shares[pl.ds(l * blocks + b, 1)]
            if side:
                share = share * live
            weights = (get(j) * share).astype(jnp.bfloat16)
            wide = weights.astype(jnp.float32)
            totals[p] += wide[:, :128] + wide[:, 128:]
            acc[p, pl.ds(0, cent)] += jnp.dot(weights, x[b], preferred_element_type=jnp.float32)
        return ready

    return lax.fori_loop(0, (found + 1) // 2, two, ready)


def clear_sums(acc, totals):
    acc[...] = jnp.zeros_like(acc)
    totals[...] = jnp.zeros_like(totals)


def store_sums(acc, totals, out_refs, sem):
    cent = totals.shape[1]
    copies = []
    for p, ref in enumerate(out_refs):
        row = jnp.sum(totals[p].T, axis=0, keepdims=True)
        acc[p, pl.ds(cent, EXTRA), pl.ds(0, cent)] = jnp.broadcast_to(row, (EXTRA, cent))
        copies.append(pltpu.make_async_copy(acc.at[p], ref, sem.at[p]))
        copies[-1].start()
    for copy in copies:
        copy.wait()


def score_kernel(members, listed, slots_ref, rows_ref, *refs):
    pieces = 2 * len(members)
    piece_refs = refs[:pieces]
    tiles_ref, tops, masses, x, panels, norms, ring, ids, row_sem, panel_sem, ring_sem = refs[pieces:]
    blocks = x.shape[0]
    finish_panels = load_panels(piece_refs, panels, norms, panel_sem)
    start_rows(rows_ref, x, row_sem)
    found = collect(slots_ref, members, ids, blocks, listed)
    finish_panels()

    def outgoing(j):
        slot = j % DEPTH
        return pltpu.make_async_copy(ring.at[slot], tiles_ref.at[j], ring_sem.at[slot])

    def put(j, powers):
        @pl.when(j >= DEPTH)
        def _():
            outgoing(j - DEPTH).wait()

        ring[j % DEPTH] = powers
        outgoing(j).start()

    wait_rows = functools.partial(await_rows, rows_ref, x, row_sem)
    ready = score_loop(
        members, slots_ref, ids, found, listed, x, panels, norms, tops, masses, wait_rows, put
    )
    written = (found + 1) // 2 * 2
    lax.fori_loop(jnp.maximum(written - DEPTH, 0), written, lambda j, _: (outgoing(j).wait(), 0)[1], 0)
    wait_rows(ready, blocks)


def sum_kernel(members, listed, slots_ref, rows_ref, tiles_ref, shares, *refs):
    pieces = 2 * len(members)
    out_refs = refs[:pieces]
    x, acc, totals, ring, ids, row_sem, ring_sem, out_sem = refs[pieces:]
    blocks = x.shape[0]
    start_rows(rows_ref, x, row_sem)
    found = collect(slots_ref, members, ids, blocks, listed)
    held = (found + 1) // 2 * 2

    def incoming(j):
        slot = j % DEPTH
        return pltpu.make_async_copy(tiles_ref.at[j], ring.at[slot], ring_sem.at[slot])

    lax.fori_loop(0, jnp.minimum(held, DEPTH), lambda j, _: (incoming(j).start(), 0)[1], 0)
    clear_sums(acc, totals)

    def get(j):
        incoming(j).wait()
        return ring[j % DEPTH]

    def wait_rows(ready, upto):
        return await_rows(rows_ref, x, row_sem, ready, upto)

    cent = totals.shape[1]

    def two(half, ready):
        work = []
        for side in range(2):
            j = 2 * half + side
            code = ids[jnp.minimum(j, found - 1)]
            b, l = code >> 3, code & 7
            work.append((j, b, l, local_place(slots_ref[b * listed + l], members)))
        ready = wait_rows(ready, work[1][1] + 1)
        live = (work[1][0] < found).astype(jnp.float32)
        for side, (j, b, l, p) in enumerate(work):
            share = shares[pl.ds(l * blocks + b, 1)]
            if side:
                share = share * live
            weights = (get(j) * share).astype(jnp.bfloat16)
            wide = weights.astype(jnp.float32)
            totals[p] += wide[:, :128] + wide[:, 128:]
            acc[p, pl.ds(0, cent)] += jnp.dot(weights, x[b], preferred_element_type=jnp.float32)
        for j, _, _, _ in work:

            @pl.when(j + DEPTH < held)
            def _(j=j):
                incoming(j + DEPTH).start()

        return ready

    ready = lax.fori_loop(0, held // 2, two, jnp.int32(0))
    store_sums(acc, totals, out_refs, out_sem)
    wait_rows(ready, blocks)


def middle_kernel(members, listed, earlier, slots_ref, rows_ref, *refs):
    pieces = 2 * len(members)
    stat_refs = refs[: 2 * earlier]
    piece_refs = refs[2 * earlier : 2 * earlier + pieces]
    refs = refs[2 * earlier + pieces :]
    logs_ref, shares = refs[:2]
    out_refs = refs[2 : 2 + pieces]
    refs = refs[2 + pieces :]
    x, panels, norms, tiles, tops, masses, acc, totals, ids, row_sem, panel_sem, out_sem = refs
    blocks = x.shape[0]
    finish_panels = load_panels(piece_refs, panels, norms, panel_sem)
    start_rows(rows_ref, x, row_sem)
    found = collect(slots_ref, members, ids, blocks, listed)
    finish_panels()

    def put(j, powers):
        tiles[j] = powers

    def get(j):
        return tiles[j]

    wait_rows = functools.partial(await_rows, rows_ref, x, row_sem)
    ready = score_loop(
        members, slots_ref, ids, found, listed, x, panels, norms, tops, masses, wait_rows, put
    )
    clear_sums(acc, totals)
    width = tops.shape[1]
    top = functools.reduce(jnp.maximum, [ref[...] for ref in stat_refs[:earlier]], tops[...])
    mass = functools.reduce(jnp.add, [ref[...] for ref in stat_refs[earlier:]], masses[...])
    top = top.reshape(listed, blocks, width)
    mass = mass.reshape(listed, blocks, width)
    highest = jnp.max(top, axis=0)
    factor = jnp.exp2(top - highest[None])
    whole = jnp.sum(factor * mass, axis=0)
    logs_ref[...] = (highest + jnp.log2(whole)) * (1.0 / LOG2E)
    shares[...] = (factor / whole[None]).reshape(listed * blocks, width)
    ready = sum_loop(
        members, slots_ref, ids, found, listed, x, shares, acc, totals, wait_rows, ready, get
    )
    store_sums(acc, totals, out_refs, out_sem)
    wait_rows(ready, blocks)


SMEM = pl.BlockSpec(memory_space=pltpu.SMEM)
ANY = pl.BlockSpec(memory_space=pl.ANY)
HBM = pl.BlockSpec(memory_space=pltpu.HBM)
VMEM = pl.BlockSpec(memory_space=pltpu.VMEM)


class Sizes:
    def __init__(self, rows, slots, cent):
        self.blocks, self.listed = slots.shape
        self.width = rows.shape[1]
        self.cent = cent
        self.stats = jax.ShapeDtypeStruct((self.listed * self.blocks, BLOCK), jnp.float32)
        self.sums = jax.ShapeDtypeStruct((cent + EXTRA, self.width), jnp.float32)

    def tiles(self, members):
        return self.blocks * 4 + 2

    def cost(self, members, products):
        share = 2 * len(members) / 14
        pairs = self.blocks * self.listed * share
        return pl.CostEstimate(
            flops=int(2 * products * pairs * self.cent * BLOCK * self.width),
            bytes_accessed=int(2 * self.blocks * BLOCK * self.width + 4 * pairs * self.cent * BLOCK),
            transcendentals=int(pairs * self.cent * BLOCK),
        )

    def rows_scratch(self):
        return pltpu.VMEM((self.blocks, BLOCK, self.width), jnp.bfloat16)

    def panel_scratch(self, pieces):
        return [
            pltpu.VMEM((pieces, self.cent, self.width), jnp.bfloat16),
            pltpu.VMEM((pieces, self.cent, 128), jnp.float32),
        ]

    def sum_scratch(self, pieces):
        return [
            pltpu.VMEM((pieces, self.cent + EXTRA, self.width), jnp.float32),
            pltpu.VMEM((pieces, self.cent, 128), jnp.float32),
        ]

    def ids_scratch(self):
        return pltpu.SMEM((self.blocks * self.listed + 8,), jnp.int32)


def score_group(sizes, members, slots, rows, pieces):
    count = len(pieces)
    return pl.pallas_call(
        functools.partial(score_kernel, members, sizes.listed),
        out_shape=(
            jax.ShapeDtypeStruct((sizes.tiles(members), sizes.cent, BLOCK), jnp.float32),
            sizes.stats,
            sizes.stats,
        ),
        in_specs=[SMEM, HBM] + [ANY] * count,
        out_specs=(HBM, VMEM, VMEM),
        scratch_shapes=[sizes.rows_scratch()]
        + sizes.panel_scratch(count)
        + [
            pltpu.VMEM((DEPTH, sizes.cent, BLOCK), jnp.float32),
            sizes.ids_scratch(),
            pltpu.SemaphoreType.DMA((sizes.blocks,)),
            pltpu.SemaphoreType.DMA((count,)),
            pltpu.SemaphoreType.DMA((DEPTH,)),
        ],
        compiler_params=pltpu.CompilerParams(vmem_limit_bytes=48 << 20),
        cost_estimate=sizes.cost(members, 1),
        name="score_group",
    )(slots, rows, *pieces)


def sum_group(sizes, members, slots, rows, tiles, shares):
    count = 2 * len(members)
    return pl.pallas_call(
        functools.partial(sum_kernel, members, sizes.listed),
        out_shape=(sizes.sums,) * count,
        in_specs=[SMEM, HBM, HBM, VMEM],
        out_specs=(ANY,) * count,
        scratch_shapes=[sizes.rows_scratch()]
        + sizes.sum_scratch(count)
        + [
            pltpu.VMEM((DEPTH, sizes.cent, BLOCK), jnp.float32),
            sizes.ids_scratch(),
            pltpu.SemaphoreType.DMA((sizes.blocks,)),
            pltpu.SemaphoreType.DMA((DEPTH,)),
            pltpu.SemaphoreType.DMA((count,)),
        ],
        compiler_params=pltpu.CompilerParams(vmem_limit_bytes=48 << 20),
        cost_estimate=sizes.cost(members, 1),
        name="sum_group",
    )(slots, rows, tiles, shares)


def middle_group(sizes, members, slots, rows, tops, masses, pieces):
    count = len(pieces)
    earlier = len(tops)
    return pl.pallas_call(
        functools.partial(middle_kernel, members, sizes.listed, earlier),
        out_shape=(jax.ShapeDtypeStruct((sizes.blocks, BLOCK), jnp.float32), sizes.stats)
        + (sizes.sums,) * count,
        in_specs=[SMEM, HBM] + [VMEM] * (2 * earlier) + [ANY] * count,
        out_specs=(VMEM, VMEM) + (ANY,) * count,
        scratch_shapes=[sizes.rows_scratch()]
        + sizes.panel_scratch(count)
        + [
            pltpu.VMEM((sizes.tiles(members), sizes.cent, BLOCK), jnp.float32),
            pltpu.VMEM(sizes.stats.shape, jnp.float32),
            pltpu.VMEM(sizes.stats.shape, jnp.float32),
        ]
        + sizes.sum_scratch(count)
        + [
            sizes.ids_scratch(),
            pltpu.SemaphoreType.DMA((sizes.blocks,)),
            pltpu.SemaphoreType.DMA((count,)),
            pltpu.SemaphoreType.DMA((count,)),
        ],
        compiler_params=pltpu.CompilerParams(vmem_limit_bytes=48 << 20),
        cost_estimate=sizes.cost(members, 2),
        name="middle_group",
    )(slots, rows, *tops, *masses, *pieces)


def on_device(rows, centroids, lists):
    count = lax.axis_size("blk")
    device = lax.axis_index("blk")
    cent = centroids.shape[0]
    own, stages = plan_of(count)
    groups = [(own,)] + [tuple(q for q, _, _ in stage) for stage in stages]
    slots = (2 * chip_place(lists, device, count) + ((lists ^ device) & 1)).astype(jnp.int32)
    sizes = Sizes(rows, slots, cent)
    slots = slots.reshape(-1)

    near = {own: centroids}
    tiles, tops, masses = [], [], []
    for members, stage in zip(groups, stages):
        arriving = [moved(near[source], shift) for _, source, shift in stage]
        pieces = [v for q in members for v in (near[q], other_core(near[q]))]
        scored = score_group(sizes, members, slots, rows, pieces)
        arriving, scored, near = lax.optimization_barrier((arriving, scored, near))
        tiles.append(scored[0])
        tops.append(scored[1])
        masses.append(scored[2])
        for (q, _, _), value in zip(stage, arriving):
            near[q] = value
    members = groups[-1]
    pieces = [v for q in members for v in (near[q], other_core(near[q]))]
    log_totals, shares, *sums = middle_group(sizes, members, slots, rows, tops, masses, pieces)

    back = {q: [] for members in groups for q in members}
    sums = {q: pair for q, pair in zip(groups[-1], zip(sums[::2], sums[1::2]))}
    arriving = []
    for at in reversed(range(len(groups))):
        crossed = {q: other_core(theirs) for q, (_, theirs) in sums.items()}
        ahead = []
        if at:
            ahead = sum_group(sizes, groups[at - 1], slots, rows, tiles[at - 1], shares)
        crossed, ahead, arriving, shares = lax.optimization_barrier((crossed, ahead, arriving, shares))
        if arriving:
            for value, (_, source, _) in zip(arriving, stages[at]):
                back[source].append(value)
        total = {}
        for q, (mine, _) in sums.items():
            total[q] = (mine + crossed[q]) * LINK_SCALE
            for value in back[q]:
                total[q] = total[q] + value.astype(jnp.float32)
        if at:
            arriving = [
                moved(total[q].astype(jnp.float16), shift if shift is None else -shift)
                for q, _, shift in stages[at - 1]
            ]
            sums = {q: pair for q, pair in zip(groups[at - 1], zip(ahead[::2], ahead[1::2]))}
    own_sums = total[own] * (1.0 / LINK_SCALE)
    updated = (own_sums[:cent] + PRIOR_MASS * centroids.astype(jnp.float32)) / (
        own_sums[cent, :cent][:, None] + PRIOR_MASS
    )
    return updated, log_totals.reshape(-1)


def solution(mesh):
    placed = P(("groups", "blk"), None)
    return jax.shard_map(
        on_device,
        mesh=mesh,
        in_specs=(placed, placed, placed),
        out_specs=(placed, P(("groups", "blk"))),
        check_vma=False,
    )
```

profile of v0, /device:TPU:0, one launch (start us, length us, event | category | flops | bytes accessed | tf_op | source)
XLA Modules:
  0.0 150.9 jit_solution(12193576721316968662)
XLA Ops:
  0.6 0.5 collective-permute-start.2
  1.1 2.6 %collective-permute-start.1 = (bf16[256,768]{1,0:T(8,128)(2,1)}, bf16[256,768]{1,0:T(8,128)(2,1)S(1)}, u32[]{:S(2)}, u32[]{:S(2)}) collective-permute-start(bf16[256,768]{1,0:T(8,128)(2,1)} %refs_0_.1), channel_id=1, source_target_pairs={{0,2},{1,3},{2,0},{3,1},{4,6},{5,7},{6,4},{7,5},{8,10},{9,11},{10,... | collective-permute-start | bytes 1179656 | tf_op jit(solution)/shard_map/ppermute | solution.py:49
  3.7 1.6 %collective-permute-start = (bf16[256,768]{1,0:T(8,128)(2,1)}, bf16[256,768]{1,0:T(8,128)(2,1)S(1)}, u32[]{:S(2)}, u32[]{:S(2)}) collective-permute-start(bf16[256,768]{1,0:T(8,128)(2,1)} %refs_0_.1), channel_id=1, source_target_pairs={{0,4},{1,5},{2,6},{3,7},{4,8},{5,9},{6,10},{7,11},{8,12},{9,13},{1... | collective-permute-start | bytes 1179656 | tf_op jit(solution)/shard_map/ppermute | solution.py:50
  5.3 0.7 fusion.7
  6.2 7.4 %score_group.3 = (f32[66,256,256]{2,1,0:T(8,128)}, f32[96,256]{1,0:T(8,128)S(1)}, f32[96,256]{1,0:T(8,128)S(1)}) custom-call(s32[96]{0:T(128)S(1)} %reshape.19.slots_ref, bf16[4096,768]{1,0:T(8,128)(2,1)} %rows_ref.13, bf16[256,768]{1,0:T(8,128)(2,1)} %refs_0_.1, bf16[256,768]{1,0:T(8,128)(2,1)S(1)} %collective-permute-done.2.refs_1_), custom_call_target="tpu_custom_call" | custom-call | flops 1380525184 | bytes 9886573 | tf_op jit(solution)/shard_map/score_group/pallas_call | solution.py:360
  13.7 3.4 %collective-permute-done.refs_0_ = bf16[256,768]{1,0:T(8,128)(2,1)S(1)} collective-permute-done((bf16[256,768]{1,0:T(8,128)(2,1)}, bf16[256,768]{1,0:T(8,128)(2,1)S(1)}, u32[]{:S(2)}, u32[]{:S(2)}) %collective-permute-start) | collective-permute-done | bytes 393248 | tf_op jit(solution)/shard_map/ppermute | solution.py:50
  17.0 0.5 collective-permute-start.5
  17.5 3.3 %collective-permute-start.3 = (bf16[256,768]{1,0:T(8,128)(2,1)}, bf16[256,768]{1,0:T(8,128)(2,1)S(1)}, u32[]{:S(2)}, u32[]{:S(2)}) collective-permute-start(bf16[256,768]{1,0:T(8,128)(2,1)} %refs_0_.1), channel_id=1, source_target_pairs={{0,12},{1,13},{2,14},{3,15},{4,0},{5,1},{6,2},{7,3},{8,4},{9,5},{1... | collective-permute-start | bytes 1179656 | tf_op jit(solution)/shard_map/ppermute | solution.py:50
  20.9 12.4 %score_group.4 = (f32[66,256,256]{2,1,0:T(8,128)}, f32[96,256]{1,0:T(8,128)S(1)}, f32[96,256]{1,0:T(8,128)S(1)}) custom-call(s32[96]{0:T(128)S(1)} %reshape.19.slots_ref, bf16[4096,768]{1,0:T(8,128)(2,1)} %rows_ref.13, bf16[256,768]{1,0:T(8,128)(2,1)S(1)} %collective-permute-done.refs_0_, bf16[256,768]{1,0:T(8,128)(2,1)S(1)} %collective-permute-done.5.refs_1_, ...), custom_call_target="tpu_custom_call" | custom-call | flops 2761050368 | bytes 13481691 | tf_op jit(solution)/shard_map/score_group/pallas_call | solution.py:360
  33.4 0.5 collective-permute-start.9
  33.9 3.0 %collective-permute-start.7 = (bf16[256,768]{1,0:T(8,128)(2,1)S(1)}, bf16[256,768]{1,0:T(8,128)(2,1)S(1)}, u32[]{:S(2)}, u32[]{:S(2)}) collective-permute-start(bf16[256,768]{1,0:T(8,128)(2,1)S(1)} %collective-permute-done.4.refs_2_), channel_id=1, source_target_pairs={{0,4},{1,5},{2,6},{3,7},{4,8},{5,9},{6,10},{7,11},{8,12},{9,13},{1... | collective-permute-start | bytes 1179656 | tf_op jit(solution)/shard_map/ppermute | solution.py:50
  37.0 7.9 %score_group.5 = (f32[66,256,256]{2,1,0:T(8,128)}, f32[96,256]{1,0:T(8,128)S(1)}, f32[96,256]{1,0:T(8,128)S(1)}) custom-call(s32[96]{0:T(128)S(1)} %reshape.19.slots_ref, bf16[4096,768]{1,0:T(8,128)(2,1)} %rows_ref.13, bf16[256,768]{1,0:T(8,128)(2,1)S(1)} %collective-permute-done.3.refs_0_, bf16[256,768]{1,0:T(8,128)(2,1)S(1)} %collective-permute-done.9.refs_1_, ...), custom_call_target="tpu_custom_call" | custom-call | flops 2761050368 | bytes 13481691 | tf_op jit(solution)/shard_map/score_group/pallas_call | solution.py:360
  44.9 1.9 %collective-permute-done.7.refs_6_ = bf16[256,768]{1,0:T(8,128)(2,1)S(1)} collective-permute-done((bf16[256,768]{1,0:T(8,128)(2,1)S(1)}, bf16[256,768]{1,0:T(8,128)(2,1)S(1)}, u32[]{:S(2)}, u32[]{:S(2)}) %collective-permute-start.7) | collective-permute-done | bytes 393248 | tf_op jit(solution)/shard_map/ppermute | solution.py:50
  46.8 1.3 collective-permute-done.8.refs_8_
  48.1 0.5 collective-permute-start.12
  48.6 1.2 collective-permute-done.11.refs_7_
  49.9 0.6 collective-permute-done.12.refs_9_
  50.4 18.5 %middle_group.1 = (f32[16,256]{1,0:T(8,128)S(1)}, f32[96,256]{1,0:T(8,128)S(1)}, f32[264,768]{1,0:T(8,128)S(1)}, f32[264,768]{1,0:T(8,128)S(1)}, f32[264,768]{1,0:T(8,128)S(1)}, /*index=5*/f32[264,768]{1,0:T(8,128)S(1)}) custom-call(s32[96]{0:T(128)S(1)} %reshape.19.slots_ref, bf16[4096,768]{1,0:T(8,128)(2,1)} %rows_ref.13, ...), custom_call_target="tpu_custom_call" | custom-call | flops 5522100736 | bytes 13481691 | tf_op jit(solution)/shard_map/middle_group/pallas_call | solution.py:409
  69.0 1.1 collective-permute-start.13
  70.2 9.7 %sum_group.3 = (f32[264,768]{1,0:T(8,128)S(1)}, f32[264,768]{1,0:T(8,128)S(1)}, f32[264,768]{1,0:T(8,128)S(1)}, f32[264,768]{1,0:T(8,128)S(1)}) custom-call(s32[96]{0:T(128)S(1)} %reshape.19.slots_ref, bf16[4096,768]{1,0:T(8,128)(2,1)} %rows_ref.13, f32[66,256,256]{2,1,0:T(8,128)} %get-tuple-element.92.tiles_ref, f32[96,256]{1,0:T(8,128)S(1)} %get-tuple-element.113.shares), custom_call_target="tpu_custom_call" | custom-call | flops 2761050368 | bytes 13481691 | tf_op jit(solution)/shard_map/sum_group/pallas_call | solution.py:386
  80.6 3.6 %collective-permute-start.17 = (f16[264,768]{1,0:T(8,128)(2,1)S(1)}, f16[264,768]{1,0:T(8,128)(2,1)S(1)}, u32[]{:S(2)}, u32[]{:S(2)}) collective-permute-start(f16[264,768]{1,0:T(8,128)(2,1)S(1)} %multiply_convert_fusion.2), channel_id=1, source_target_pairs={{0,12},{1,13},{2,14},{3,15},{4,0},{5,1},{6,2},{7,3},{8,4},{9,5},{1... | collective-permute-start | bytes 1216520 | tf_op jit(solution)/shard_map/ppermute | solution.py:50
  84.5 17.5 %collective-permute-start.18 = (f16[264,768]{1,0:T(8,128)(2,1)S(1)}, f16[264,768]{1,0:T(8,128)(2,1)S(1)}, u32[]{:S(2)}, u32[]{:S(2)}) collective-permute-start(f16[264,768]{1,0:T(8,128)(2,1)S(1)} %multiply_convert_fusion.1), channel_id=1, source_target_pairs={{0,2},{1,3},{2,0},{3,1},{4,6},{5,7},{6,4},{7,5},{8,10},{9,11},{10,... | collective-permute-start | bytes 1216520 | tf_op jit(solution)/shard_map/ppermute | solution.py:49
  101.9 15.0 %sum_group.4 = (f32[264,768]{1,0:T(8,128)S(1)}, f32[264,768]{1,0:T(8,128)S(1)}, f32[264,768]{1,0:T(8,128)S(1)}, f32[264,768]{1,0:T(8,128)S(1)}) custom-call(s32[96]{0:T(128)S(1)} %reshape.19.slots_ref, bf16[4096,768]{1,0:T(8,128)(2,1)} %rows_ref.13, f32[66,256,256]{2,1,0:T(8,128)} %get-tuple-element.100.tiles_ref, f32[96,256]{1,0:T(8,128)S(1)} %get-tuple-element.113.shares), custom_call_target="tpu_custom_call" | custom-call | flops 2761050368 | bytes 13481691 | tf_op jit(solution)/shard_map/sum_group/pallas_call | solution.py:386
  117.1 0.5 collective-permute-start.20
  117.8 3.8 %collective-permute-start.21 = (f16[264,768]{1,0:T(8,128)(2,1)S(1)}, f16[264,768]{1,0:T(8,128)(2,1)S(1)}, u32[]{:S(2)}, u32[]{:S(2)}) collective-permute-start(f16[264,768]{1,0:T(8,128)(2,1)S(1)} %add_convert_fusion.2), channel_id=1, source_target_pairs={{0,4},{1,5},{2,6},{3,7},{4,8},{5,9},{6,10},{7,11},{8,12},{9,13},{1... | collective-permute-start | bytes 1216520 | tf_op jit(solution)/shard_map/ppermute | solution.py:50
  121.9 9.3 %sum_group.5 = (f32[264,768]{1,0:T(8,128)S(1)}, f32[264,768]{1,0:T(8,128)S(1)}) custom-call(s32[96]{0:T(128)S(1)} %reshape.19.slots_ref, bf16[4096,768]{1,0:T(8,128)(2,1)} %rows_ref.13, f32[66,256,256]{2,1,0:T(8,128)} %get-tuple-element.112.tiles_ref, f32[96,256]{1,0:T(8,128)S(1)} %get-tuple-element.113.shares), custom_call_target="tpu_custom_call" | custom-call | flops 1380525184 | bytes 9886573 | tf_op jit(solution)/shard_map/sum_group/pallas_call | solution.py:386
  131.1 2.2 %collective-permute-done.22 = f16[264,768]{1,0:T(8,128)(2,1)S(1)} collective-permute-done((f16[264,768]{1,0:T(8,128)(2,1)S(1)}, f16[264,768]{1,0:T(8,128)(2,1)S(1)}, u32[]{:S(2)}, u32[]{:S(2)}) %collective-permute-start.22) | collective-permute-done | bytes 405536 | tf_op jit(solution)/shard_map/ppermute | solution.py:49
  133.5 3.4 %collective-permute-start.24 = (f16[264,768]{1,0:T(8,128)(2,1)S(1)}, f16[264,768]{1,0:T(8,128)(2,1)S(1)}, u32[]{:S(2)}, u32[]{:S(2)}) collective-permute-start(f16[264,768]{1,0:T(8,128)(2,1)S(1)} %add_convert_fusion), channel_id=1, source_target_pairs={{0,12},{1,13},{2,14},{3,15},{4,0},{5,1},{6,2},{7,3},{8,4},{9,5},{1... | collective-permute-start | bytes 1216520 | tf_op jit(solution)/shard_map/ppermute | solution.py:50
  137.1 0.6 copy.7
  137.7 9.2 %collective-permute-done.24 = f16[264,768]{1,0:T(8,128)(2,1)S(1)} collective-permute-done((f16[264,768]{1,0:T(8,128)(2,1)S(1)}, f16[264,768]{1,0:T(8,128)(2,1)S(1)}, u32[]{:S(2)}, u32[]{:S(2)}) %collective-permute-start.24) | collective-permute-done | bytes 405536 | tf_op jit(solution)/shard_map/ppermute | solution.py:50
  146.9 1.7 %collective-permute-done.25 = f16[264,768]{1,0:T(8,128)(2,1)S(1)} collective-permute-done((f16[264,768]{1,0:T(8,128)(2,1)S(1)}, f16[264,768]{1,0:T(8,128)(2,1)S(1)}, u32[]{:S(2)}, u32[]{:S(2)}) %collective-permute-start.25) | collective-permute-done | bytes 405536 | tf_op jit(solution)/shard_map/ppermute | solution.py:49
  148.9 2.0 %fusion = f32[256,768]{1,0:T(8,128)} fusion(f32[264,768]{1,0:T(8,128)S(1)} %add_multiply_fusion, bf16[256,768]{1,0:T(8,128)(2,1)} %refs_0_.1, f32[256]{0:T(256)S(1)} %bitcast.5), kind=kLoop, calls=%fused_computation.8 | loop fusion | flops 786432 | bytes 1967104 | tf_op jit(solution)/shard_map/div | solution.py:485
  (40 shorter events, 2.6 us)
Async XLA Ops:
  0.6 5.6 %collective-permute-start.2 = (bf16[256,768]{1,0:T(8,128)(2,1)}, bf16[256,768]{1,0:T(8,128)(2,1)S(1)}, u32[]{:S(2)}, u32[]{:S(2)}) collective-permute-start(bf16[256,768]{1,0:T(8,128)(2,1)} %refs_0_.1), channel_id=1, source_target_pairs={{0,1},{1,0},{2,3},{3,2},{4,5},{5,4},{6,7},{7,6},{8,9},{9,8},{10,11... | collective-permute-start | bytes 1179656 | tf_op jit(solution)/shard_map/ppermute | solution.py:55
  1.1 12.5 %collective-permute-start.1 = (bf16[256,768]{1,0:T(8,128)(2,1)}, bf16[256,768]{1,0:T(8,128)(2,1)S(1)}, u32[]{:S(2)}, u32[]{:S(2)}) collective-permute-start(bf16[256,768]{1,0:T(8,128)(2,1)} %refs_0_.1), channel_id=1, source_target_pairs={{0,2},{1,3},{2,0},{3,1},{4,6},{5,7},{6,4},{7,5},{8,10},{9,11},{10,... | collective-permute-start | bytes 1179656 | tf_op jit(solution)/shard_map/ppermute | solution.py:49
  3.7 13.3 %collective-permute-start = (bf16[256,768]{1,0:T(8,128)(2,1)}, bf16[256,768]{1,0:T(8,128)(2,1)S(1)}, u32[]{:S(2)}, u32[]{:S(2)}) collective-permute-start(bf16[256,768]{1,0:T(8,128)(2,1)} %refs_0_.1), channel_id=1, source_target_pairs={{0,4},{1,5},{2,6},{3,7},{4,8},{5,9},{6,10},{7,11},{8,12},{9,13},{1... | collective-permute-start | bytes 1179656 | tf_op jit(solution)/shard_map/ppermute | solution.py:50
  17.0 3.8 %collective-permute-start.6 = (bf16[256,768]{1,0:T(8,128)(2,1)S(1)}, bf16[256,768]{1,0:T(8,128)(2,1)S(1)}, u32[]{:S(2)}, u32[]{:S(2)}) collective-permute-start(bf16[256,768]{1,0:T(8,128)(2,1)S(1)} %collective-permute-done.1.refs_2_), channel_id=1, source_target_pairs={{0,1},{1,0},{2,3},{3,2},{4,5},{5,4},{6,7},{7,6},{8,9},{9,8},{10,11... | collective-permute-start | bytes 1179656 | tf_op jit(solution)/shard_map/ppermute | solution.py:55
  17.0 3.8 %collective-permute-start.5 = (bf16[256,768]{1,0:T(8,128)(2,1)S(1)}, bf16[256,768]{1,0:T(8,128)(2,1)S(1)}, u32[]{:S(2)}, u32[]{:S(2)}) collective-permute-start(bf16[256,768]{1,0:T(8,128)(2,1)S(1)} %collective-permute-done.refs_0_), channel_id=1, source_target_pairs={{0,1},{1,0},{2,3},{3,2},{4,5},{5,4},{6,7},{7,6},{8,9},{9,8},{10,11... | collective-permute-start | bytes 1179656 | tf_op jit(solution)/shard_map/ppermute | solution.py:55
  17.5 15.8 %collective-permute-start.3 = (bf16[256,768]{1,0:T(8,128)(2,1)}, bf16[256,768]{1,0:T(8,128)(2,1)S(1)}, u32[]{:S(2)}, u32[]{:S(2)}) collective-permute-start(bf16[256,768]{1,0:T(8,128)(2,1)} %refs_0_.1), channel_id=1, source_target_pairs={{0,12},{1,13},{2,14},{3,15},{4,0},{5,1},{6,2},{7,3},{8,4},{9,5},{1... | collective-permute-start | bytes 1179656 | tf_op jit(solution)/shard_map/ppermute | solution.py:50
  20.9 12.4 %collective-permute-start.4 = (bf16[256,768]{1,0:T(8,128)(2,1)S(1)}, bf16[256,768]{1,0:T(8,128)(2,1)S(1)}, u32[]{:S(2)}, u32[]{:S(2)}) collective-permute-start(bf16[256,768]{1,0:T(8,128)(2,1)S(1)} %collective-permute-done.refs_0_), channel_id=1, source_target_pairs={{0,2},{1,3},{2,0},{3,1},{4,6},{5,7},{6,4},{7,5},{8,10},{9,11},{10,... | collective-permute-start | bytes 1179656 | tf_op jit(solution)/shard_map/ppermute | solution.py:49
  33.3 3.6 %collective-permute-start.10 = (bf16[256,768]{1,0:T(8,128)(2,1)S(1)}, bf16[256,768]{1,0:T(8,128)(2,1)S(1)}, u32[]{:S(2)}, u32[]{:S(2)}) collective-permute-start(bf16[256,768]{1,0:T(8,128)(2,1)S(1)} %collective-permute-done.4.refs_2_), channel_id=1, source_target_pairs={{0,1},{1,0},{2,3},{3,2},{4,5},{5,4},{6,7},{7,6},{8,9},{9,8},{10,11... | collective-permute-start | bytes 1179656 | tf_op jit(solution)/shard_map/ppermute | solution.py:55
  33.4 3.6 %collective-permute-start.9 = (bf16[256,768]{1,0:T(8,128)(2,1)S(1)}, bf16[256,768]{1,0:T(8,128)(2,1)S(1)}, u32[]{:S(2)}, u32[]{:S(2)}) collective-permute-start(bf16[256,768]{1,0:T(8,128)(2,1)S(1)} %collective-permute-done.3.refs_0_), channel_id=1, source_target_pairs={{0,1},{1,0},{2,3},{3,2},{4,5},{5,4},{6,7},{7,6},{8,9},{9,8},{10,11... | collective-permute-start | bytes 1179656 | tf_op jit(solution)/shard_map/ppermute | solution.py:55
  33.9 12.9 %collective-permute-start.7 = (bf16[256,768]{1,0:T(8,128)(2,1)S(1)}, bf16[256,768]{1,0:T(8,128)(2,1)S(1)}, u32[]{:S(2)}, u32[]{:S(2)}) collective-permute-start(bf16[256,768]{1,0:T(8,128)(2,1)S(1)} %collective-permute-done.4.refs_2_), channel_id=1, source_target_pairs={{0,4},{1,5},{2,6},{3,7},{4,8},{5,9},{6,10},{7,11},{8,12},{9,13},{1... | collective-permute-start | bytes 1179656 | tf_op jit(solution)/shard_map/ppermute | solution.py:50
  36.9 11.2 %collective-permute-start.8 = (bf16[256,768]{1,0:T(8,128)(2,1)S(1)}, bf16[256,768]{1,0:T(8,128)(2,1)S(1)}, u32[]{:S(2)}, u32[]{:S(2)}) collective-permute-start(bf16[256,768]{1,0:T(8,128)(2,1)S(1)} %collective-permute-done.3.refs_0_), channel_id=1, source_target_pairs={{0,2},{1,3},{2,0},{3,1},{4,6},{5,7},{6,4},{7,5},{8,10},{9,11},{10,... | collective-permute-start | bytes 1179656 | tf_op jit(solution)/shard_map/ppermute | solution.py:49
  48.1 1.7 %collective-permute-start.11 = (bf16[256,768]{1,0:T(8,128)(2,1)S(1)}, bf16[256,768]{1,0:T(8,128)(2,1)S(1)}, u32[]{:S(2)}, u32[]{:S(2)}) collective-permute-start(bf16[256,768]{1,0:T(8,128)(2,1)S(1)} %collective-permute-done.7.refs_6_), channel_id=1, source_target_pairs={{0,1},{1,0},{2,3},{3,2},{4,5},{5,4},{6,7},{7,6},{8,9},{9,8},{10,11... | collective-permute-start | bytes 1179656 | tf_op jit(solution)/shard_map/ppermute | solution.py:55
  48.1 2.3 %collective-permute-start.12 = (bf16[256,768]{1,0:T(8,128)(2,1)S(1)}, bf16[256,768]{1,0:T(8,128)(2,1)S(1)}, u32[]{:S(2)}, u32[]{:S(2)}) collective-permute-start(bf16[256,768]{1,0:T(8,128)(2,1)S(1)} %collective-permute-done.8.refs_8_), channel_id=1, source_target_pairs={{0,1},{1,0},{2,3},{3,2},{4,5},{5,4},{6,7},{7,6},{8,9},{9,8},{10,11... | collective-permute-start | bytes 1179656 | tf_op jit(solution)/shard_map/ppermute | solution.py:55
  69.0 10.9 %collective-permute-start.13 = (f32[264,768]{1,0:T(8,128)S(1)}, f32[264,768]{1,0:T(8,128)S(1)}, u32[]{:S(2)}, u32[]{:S(2)}) collective-permute-start(f32[264,768]{1,0:T(8,128)S(1)} %get-tuple-element.90), channel_id=1, source_target_pairs={{0,1},{1,0},{2,3},{3,2},{4,5},{5,4},{6,7},{7,6},{8,9},{9,8},{10,11... | collective-permute-start | bytes 2433032 | tf_op jit(solution)/shard_map/ppermute | solution.py:55
  70.1 9.8 %collective-permute-start.14 = (f32[264,768]{1,0:T(8,128)S(1)}, f32[264,768]{1,0:T(8,128)S(1)}, u32[]{:S(2)}, u32[]{:S(2)}) collective-permute-start(f32[264,768]{1,0:T(8,128)S(1)} %get-tuple-element.91), channel_id=1, source_target_pairs={{0,1},{1,0},{2,3},{3,2},{4,5},{5,4},{6,7},{7,6},{8,9},{9,8},{10,11... | collective-permute-start | bytes 2433032 | tf_op jit(solution)/shard_map/ppermute | solution.py:55
  79.9 37.1 %collective-permute-start.15 = (f32[264,768]{1,0:T(8,128)S(1)}, f32[264,768]{1,0:T(8,128)S(1)}, u32[]{:S(2)}, u32[]{:S(2)}) collective-permute-start(f32[264,768]{1,0:T(8,128)S(1)} %get-tuple-element.98), channel_id=1, source_target_pairs={{0,1},{1,0},{2,3},{3,2},{4,5},{5,4},{6,7},{7,6},{8,9},{9,8},{10,11... | collective-permute-start | bytes 2433032 | tf_op jit(solution)/shard_map/ppermute | solution.py:55
  80.4 36.6 %collective-permute-start.16 = (f32[264,768]{1,0:T(8,128)S(1)}, f32[264,768]{1,0:T(8,128)S(1)}, u32[]{:S(2)}, u32[]{:S(2)}) collective-permute-start(f32[264,768]{1,0:T(8,128)S(1)} %get-tuple-element.99), channel_id=1, source_target_pairs={{0,1},{1,0},{2,3},{3,2},{4,5},{5,4},{6,7},{7,6},{8,9},{9,8},{10,11... | collective-permute-start | bytes 2433032 | tf_op jit(solution)/shard_map/ppermute | solution.py:55
  80.6 36.3 %collective-permute-start.17 = (f16[264,768]{1,0:T(8,128)(2,1)S(1)}, f16[264,768]{1,0:T(8,128)(2,1)S(1)}, u32[]{:S(2)}, u32[]{:S(2)}) collective-permute-start(f16[264,768]{1,0:T(8,128)(2,1)S(1)} %multiply_convert_fusion.2), channel_id=1, source_target_pairs={{0,12},{1,13},{2,14},{3,15},{4,0},{5,1},{6,2},{7,3},{8,4},{9,5},{1... | collective-permute-start | bytes 1216520 | tf_op jit(solution)/shard_map/ppermute | solution.py:50
  84.5 32.5 %collective-permute-start.18 = (f16[264,768]{1,0:T(8,128)(2,1)S(1)}, f16[264,768]{1,0:T(8,128)(2,1)S(1)}, u32[]{:S(2)}, u32[]{:S(2)}) collective-permute-start(f16[264,768]{1,0:T(8,128)(2,1)S(1)} %multiply_convert_fusion.1), channel_id=1, source_target_pairs={{0,2},{1,3},{2,0},{3,1},{4,6},{5,7},{6,4},{7,5},{8,10},{9,11},{10,... | collective-permute-start | bytes 1216520 | tf_op jit(solution)/shard_map/ppermute | solution.py:49
  117.0 16.3 %collective-permute-start.19 = (f32[264,768]{1,0:T(8,128)S(1)}, f32[264,768]{1,0:T(8,128)S(1)}, u32[]{:S(2)}, u32[]{:S(2)}) collective-permute-start(f32[264,768]{1,0:T(8,128)S(1)} %get-tuple-element.110), channel_id=1, source_target_pairs={{0,1},{1,0},{2,3},{3,2},{4,5},{5,4},{6,7},{7,6},{8,9},{9,8},{10,11... | collective-permute-start | bytes 2433032 | tf_op jit(solution)/shard_map/ppermute | solution.py:55
  117.1 16.2 %collective-permute-start.20 = (f32[264,768]{1,0:T(8,128)S(1)}, f32[264,768]{1,0:T(8,128)S(1)}, u32[]{:S(2)}, u32[]{:S(2)}) collective-permute-start(f32[264,768]{1,0:T(8,128)S(1)} %get-tuple-element.111), channel_id=1, source_target_pairs={{0,1},{1,0},{2,3},{3,2},{4,5},{5,4},{6,7},{7,6},{8,9},{9,8},{10,11... | collective-permute-start | bytes 2433032 | tf_op jit(solution)/shard_map/ppermute | solution.py:55
  117.8 13.4 %collective-permute-start.21 = (f16[264,768]{1,0:T(8,128)(2,1)S(1)}, f16[264,768]{1,0:T(8,128)(2,1)S(1)}, u32[]{:S(2)}, u32[]{:S(2)}) collective-permute-start(f16[264,768]{1,0:T(8,128)(2,1)S(1)} %add_convert_fusion.2), channel_id=1, source_target_pairs={{0,4},{1,5},{2,6},{3,7},{4,8},{5,9},{6,10},{7,11},{8,12},{9,13},{1... | collective-permute-start | bytes 1216520 | tf_op jit(solution)/shard_map/ppermute | solution.py:50
  121.8 11.5 %collective-permute-start.22 = (f16[264,768]{1,0:T(8,128)(2,1)S(1)}, f16[264,768]{1,0:T(8,128)(2,1)S(1)}, u32[]{:S(2)}, u32[]{:S(2)}) collective-permute-start(f16[264,768]{1,0:T(8,128)(2,1)S(1)} %add_convert_fusion.1), channel_id=1, source_target_pairs={{0,2},{1,3},{2,0},{3,1},{4,6},{5,7},{6,4},{7,5},{8,10},{9,11},{10,... | collective-permute-start | bytes 1216520 | tf_op jit(solution)/shard_map/ppermute | solution.py:49
  133.3 15.2 %collective-permute-start.23 = (f32[264,768]{1,0:T(8,128)S(1)}, f32[264,768]{1,0:T(8,128)S(1)}, u32[]{:S(2)}, u32[]{:S(2)}) collective-permute-start(f32[264,768]{1,0:T(8,128)S(1)} %get-tuple-element.123), channel_id=1, source_target_pairs={{0,1},{1,0},{2,3},{3,2},{4,5},{5,4},{6,7},{7,6},{8,9},{9,8},{10,11... | collective-permute-start | bytes 2433032 | tf_op jit(solution)/shard_map/ppermute | solution.py:55
  133.5 13.4 %collective-permute-start.24 = (f16[264,768]{1,0:T(8,128)(2,1)S(1)}, f16[264,768]{1,0:T(8,128)(2,1)S(1)}, u32[]{:S(2)}, u32[]{:S(2)}) collective-permute-start(f16[264,768]{1,0:T(8,128)(2,1)S(1)} %add_convert_fusion), channel_id=1, source_target_pairs={{0,12},{1,13},{2,14},{3,15},{4,0},{5,1},{6,2},{7,3},{8,4},{9,5},{1... | collective-permute-start | bytes 1216520 | tf_op jit(solution)/shard_map/ppermute | solution.py:50
  137.0 11.6 %collective-permute-start.25 = (f16[264,768]{1,0:T(8,128)(2,1)S(1)}, f16[264,768]{1,0:T(8,128)(2,1)S(1)}, u32[]{:S(2)}, u32[]{:S(2)}) collective-permute-start(f16[264,768]{1,0:T(8,128)(2,1)S(1)} %multiply_convert_fusion), channel_id=1, source_target_pairs={{0,2},{1,3},{2,0},{3,1},{4,6},{5,7},{6,4},{7,5},{8,10},{9,11},{10,... | collective-permute-start | bytes 1216520 | tf_op jit(solution)/shard_map/ppermute | solution.py:49
where the time goes:
time: 153 us; the launch traced here: 151 us
  Pallas kernels  80.3 us (52%)
  starting transfers between devices  43.5 us (28%)
  waiting for transfers between devices  21.5 us (14%)
  other arithmetic  4.04 us (3%)
    pallas_call x3, Pallas kernels, sum_group(): pl.pallas_call(functools.partial(sum_kernel, members, sizes.listed), out_...  34 us
    pallas_call x3, Pallas kernels, score_group(): pl.pallas_call(functools.partial(score_kernel, members, sizes.listed), ou...  27.7 us
    ppermute x6, starting transfers between devices, moved(): return lax.ppermute(value, 'blk', [(i, i ^ 2) for i in range(count)])  20.2 us
    ppermute x6, starting transfers between devices, moved(): lax.ppermute(value, 'blk', [(i, (i + shift) % count) for i in range(count)])  18.8 us
    pallas_call x1, Pallas kernels, middle_group(): pl.pallas_call(functools.partial(middle_kernel, members, sizes.listed, ea...  18.5 us
    ppermute x6, waiting for transfers between devices, moved(): lax.ppermute(value, 'blk', [(i, (i + shift) % count) for i in range(count)])  14.4 us
    ppermute x6, waiting for transfers between devices, moved(): return lax.ppermute(value, 'blk', [(i, i ^ 2) for i in range(count)])  5.22 us
    ppermute x14, starting transfers between devices, other_core(): return lax.ppermute(value, 'blk', [(i, i ^ 1) for i in range(count)])  4.46 us
  transfers between devices with their start and end apart: 26, of which 8 were waited for; matrix products, arithmetic and copies ran while one was open for 2% of the time, Pallas kernels for 41%

commit v1 on v0

v1 whole, which is shorter than its diff:
```python
import functools
import math

import jax
import jax.numpy as jnp
from jax import lax
from jax.experimental import pallas as pl
from jax.experimental.pallas import tpu as pltpu
from jax.sharding import PartitionSpec as P

BLOCK = 256
SPAN = 6
LOGIT_SCALE = 0.25
PRIOR_MASS = 8.0
LOG2E = math.log2(math.e)
LINK_SCALE = 1.0 / 16.0
EXTRA = 8
VMEM_GRANT = 42 << 20


def grid_plan():
    return 0, (
        ((2, 0, 4), (1, 0, None)),
        ((6, 0, -4), (3, 2, None)),
        ((5, 3, 4), (7, 6, None)),
    )


def ring_plan():
    reach = (SPAN + 1) // 2
    return reach, tuple(
        ((reach + hop + 1, reach + hop, 2), (reach - hop - 1, reach - hop, -2)) for hop in range(reach)
    )


def plan_of(count):
    return grid_plan() if count == 16 else ring_plan()


def chip_place(panel, device, count):
    if count == 16:
        return (device // 4 - panel // 4) % 4 * 2 + ((panel ^ device) >> 1 & 1)
    return (device // 2 - panel // 2 + (SPAN + 1) // 2) % (count // 2)


def moved(value, shift):
    count = lax.axis_size("blk")
    if shift is None:
        return lax.ppermute(value, "blk", [(i, i ^ 2) for i in range(count)])
    return lax.ppermute(value, "blk", [(i, (i + shift) % count) for i in range(count)])


def other_core(value):
    count = lax.axis_size("blk")
    return lax.ppermute(value, "blk", [(i, i ^ 1) for i in range(count)])


def pairs_of(slots, room):
    blocks, listed = slots.shape
    hit = slots[:, :, None] == jnp.arange(room, dtype=jnp.int32)
    listing = jnp.any(hit, axis=1)
    code = 8 * jnp.arange(blocks, dtype=jnp.int32)[:, None] + jnp.sum(
        jnp.where(hit, jnp.arange(listed, dtype=jnp.int32)[None, :, None], 0), axis=1
    )
    before = jnp.arange(blocks)[:, None] > jnp.arange(blocks)[None, :]
    rank = jnp.sum(jnp.where(before[:, :, None] & listing[None], 1, 0), axis=1)
    chosen = listing[:, :, None] & (rank[:, :, None] == jnp.arange(blocks))
    order = jnp.sum(jnp.where(chosen, code[:, :, None], 0), axis=0)
    return order.reshape(-1).astype(jnp.int32), jnp.sum(listing, axis=0).astype(jnp.int32)


def local_slots(members):
    return [2 * q + core for q in members for core in (0, 1)]


def some_pairs(order_ref, counts_ref, slot, blocks, first, number):
    work = []
    for i in range(number):
        code = order_ref[slot * blocks + jnp.minimum(first + i, counts_ref[slot] - 1)]
        work.append((first + i, code >> 3, (code & 7) * blocks + (code >> 3)))
    return work


def by_fours(count, act):
    fours = count // 4
    lax.fori_loop(0, fours, lambda k, _: (act(4 * k, 4), 0)[1], 0)
    lax.fori_loop(2 * fours, (count + 1) // 2, lambda k, _: (act(2 * k, 2), 0)[1], 0)


def rows_of(x, block):
    return x[pl.ds(pl.multiple_of(block * BLOCK, BLOCK), BLOCK)]


def load_panels(piece_refs, panels, norms, sem):
    copies = [
        pltpu.make_async_copy(ref, panels.at[p], sem.at[p]) for p, ref in enumerate(piece_refs)
    ]
    for copy in copies:
        copy.start()

    def finish():
        for copy in copies:
            copy.wait()
        for p in range(len(copies)):
            wide = panels[p].astype(jnp.float32)
            norm = jnp.sum(wide * wide, axis=1, keepdims=True)
            norms[p] = jnp.broadcast_to(norm * (0.5 * LOGIT_SCALE * LOG2E), norms.shape[1:])

    return finish


def tile_of(panel, norm, block):
    scores = lax.dot_general(
        panel, block, (((1,), (1,)), ((), ())), preferred_element_type=jnp.float32
    )
    scores = scores * (LOGIT_SCALE * LOG2E) - jnp.concatenate([norm, norm], axis=1)
    top = jnp.max(scores, axis=0, keepdims=True)
    powers = jnp.exp2(scores - top)
    return powers, top, jnp.sum(powers, axis=0, keepdims=True)


def score_loop(slots, order_ref, counts_ref, x, panels, norms, tops, masses, tiles, done):
    blocks = x.shape[0] // BLOCK
    tops[...] = jnp.full_like(tops, -jnp.inf)
    masses[...] = jnp.zeros_like(masses)
    for p, slot in enumerate(slots):

        def some(first, number):
            work = some_pairs(order_ref, counts_ref, slot, blocks, first, number)
            found = [tile_of(panels[p], norms[p], rows_of(x, b)) for _, b, _ in work]
            for (i, _, at), (powers, top, mass) in zip(work, found):
                tiles[p * blocks + i] = powers
                tops[pl.ds(at, 1)] = top
                masses[pl.ds(at, 1)] = mass
            for i, _, _ in work:
                done(p * blocks + i)

        by_fours(counts_ref[slot], some)


def sum_loop(slots, order_ref, counts_ref, x, shares, acc, totals, tiles, ready):
    blocks = x.shape[0] // BLOCK
    cent = totals.shape[1]
    for p, slot in enumerate(slots):

        def some(first, number):
            work = some_pairs(order_ref, counts_ref, slot, blocks, first, number)
            for i, _, _ in work:
                ready(p * blocks + i)
            partial, count = None, None
            for i, b, at in work:
                share = shares[pl.ds(at, 1)]
                if number == 2:
                    share = share * (i < counts_ref[slot]).astype(jnp.float32)
                weights = (tiles[p * blocks + i] * share).astype(jnp.bfloat16)
                wide = weights.astype(jnp.float32)
                wide = wide[:, :128] + wide[:, 128:]
                product = jnp.dot(weights, rows_of(x, b), preferred_element_type=jnp.float32)
                partial = product if partial is None else partial + product
                count = wide if count is None else count + wide
            totals[p] += count
            acc[p, pl.ds(0, cent)] += partial

        by_fours(counts_ref[slot], some)


def clear_sums(acc, totals):
    acc[...] = jnp.zeros_like(acc)
    totals[...] = jnp.zeros_like(totals)


def store_sums(acc, totals, out_refs, sem):
    cent = totals.shape[1]
    copies = []
    for p, ref in enumerate(out_refs):
        row = jnp.sum(totals[p].T, axis=0, keepdims=True)
        acc[p, pl.ds(cent, EXTRA), pl.ds(0, cent)] = jnp.broadcast_to(row, (EXTRA, cent))
        copies.append(pltpu.make_async_copy(acc.at[p], ref, sem.at[p]))
        copies[-1].start()
    for copy in copies:
        copy.wait()


def over_tiles(slots, counts_ref, blocks, act):
    for p, slot in enumerate(slots):
        held = (counts_ref[slot] + 1) // 2 * 2
        lax.fori_loop(0, held, lambda i, _: (act(p * blocks + i), 0)[1], 0)


def score_kernel(slots, order_ref, counts_ref, x, *refs):
    pieces = len(slots)
    piece_refs = refs[:pieces]
    tiles_ref, tops, masses, panels, norms, tiles, panel_sem, tile_sem = refs[pieces:]
    load_panels(piece_refs, panels, norms, panel_sem)()

    def outgoing(j):
        return pltpu.make_async_copy(tiles.at[j], tiles_ref.at[j], tile_sem.at[j])

    score_loop(
        slots, order_ref, counts_ref, x, panels, norms, tops, masses, tiles,
        lambda j: outgoing(j).start(),
    )
    over_tiles(slots, counts_ref, x.shape[0] // BLOCK, lambda j: outgoing(j).wait())


def sum_kernel(slots, order_ref, counts_ref, x, tiles_ref, shares, *refs):
    pieces = len(slots)
    out_refs = refs[:pieces]
    acc, totals, tiles, tile_sem, out_sem = refs[pieces:]

    def incoming(j):
        return pltpu.make_async_copy(tiles_ref.at[j], tiles.at[j], tile_sem.at[j])

    over_tiles(slots, counts_ref, x.shape[0] // BLOCK, lambda j: incoming(j).start())
    clear_sums(acc, totals)
    sum_loop(
        slots, order_ref, counts_ref, x, shares, acc, totals, tiles, lambda j: incoming(j).wait()
    )
    store_sums(acc, totals, out_refs, out_sem)


def middle_kernel(slots, listed, earlier, order_ref, counts_ref, x, *refs):
    pieces = len(slots)
    stat_refs = refs[: 2 * earlier]
    piece_refs = refs[2 * earlier : 2 * earlier + pieces]
    refs = refs[2 * earlier + pieces :]
    logs_ref, shares = refs[:2]
    out_refs = refs[2 : 2 + pieces]
    panels, norms, tiles, tops, masses, acc, totals, panel_sem, out_sem = refs[2 + pieces :]
    blocks = x.shape[0] // BLOCK
    finish_panels = load_panels(piece_refs, panels, norms, panel_sem)
    clear_sums(acc, totals)
    finish_panels()
    score_loop(
        slots, order_ref, counts_ref, x, panels, norms, tops, masses, tiles, lambda j: None
    )
    width = tops.shape[1]
    top = functools.reduce(jnp.maximum, [ref[...] for ref in stat_refs[:earlier]], tops[...])
    mass = functools.reduce(jnp.add, [ref[...] for ref in stat_refs[earlier:]], masses[...])
    top = top.reshape(listed, blocks, width)
    mass = mass.reshape(listed, blocks, width)
    highest = jnp.max(top, axis=0)
    factor = jnp.exp2(top - highest[None])
    whole = jnp.sum(factor * mass, axis=0)
    logs_ref[...] = (highest + jnp.log2(whole)) * (1.0 / LOG2E)
    shares[...] = (factor / whole[None]).reshape(listed * blocks, width)
    sum_loop(slots, order_ref, counts_ref, x, shares, acc, totals, tiles, lambda j: None)
    store_sums(acc, totals, out_refs, out_sem)


SMEM = pl.BlockSpec(memory_space=pltpu.SMEM)
ANY = pl.BlockSpec(memory_space=pl.ANY)
HBM = pl.BlockSpec(memory_space=pltpu.HBM)
VMEM = pl.BlockSpec(memory_space=pltpu.VMEM)


class Sizes:
    def __init__(self, rows, blocks, listed, cent):
        self.blocks, self.listed, self.cent = blocks, listed, cent
        self.width = rows.shape[1]
        self.stats = jax.ShapeDtypeStruct((listed * blocks, BLOCK), jnp.float32)
        self.sums = jax.ShapeDtypeStruct((cent + EXTRA, self.width), jnp.float32)
        self.tiles = jax.ShapeDtypeStruct((4 * blocks, cent, BLOCK), jnp.float32)

    def cost(self, members, products):
        pairs = self.blocks * self.listed * 2 * len(members) / 14
        return pl.CostEstimate(
            flops=int(2 * products * pairs * self.cent * BLOCK * self.width),
            bytes_accessed=int(2 * self.blocks * BLOCK * self.width + 4 * pairs * self.cent * BLOCK),
            transcendentals=int(pairs * self.cent * BLOCK),
        )

    def panel_scratch(self, pieces):
        return [
            pltpu.VMEM((pieces, self.cent, self.width), jnp.bfloat16),
            pltpu.VMEM((pieces, self.cent, 128), jnp.float32),
        ]

    def sum_scratch(self, pieces):
        return [
            pltpu.VMEM((pieces, self.cent + EXTRA, self.width), jnp.float32),
            pltpu.VMEM((pieces, self.cent, 128), jnp.float32),
        ]

    def tile_scratch(self, pieces):
        return pltpu.VMEM((pieces * self.blocks, self.cent, BLOCK), jnp.float32)


def score_group(sizes, members, order, counts, rows, pieces):
    count = len(pieces)
    return pl.pallas_call(
        functools.partial(score_kernel, local_slots(members)),
        out_shape=(sizes.tiles, sizes.stats, sizes.stats),
        in_specs=[SMEM, SMEM, VMEM] + [ANY] * count,
        out_specs=(HBM, VMEM, VMEM),
        scratch_shapes=sizes.panel_scratch(count)
        + [
            sizes.tile_scratch(count),
            pltpu.SemaphoreType.DMA((count,)),
            pltpu.SemaphoreType.DMA((count * sizes.blocks,)),
        ],
        compiler_params=pltpu.CompilerParams(vmem_limit_bytes=VMEM_GRANT),
        cost_estimate=sizes.cost(members, 1),
        name="score_group",
    )(order, counts, rows, *pieces)


def sum_group(sizes, members, order, counts, rows, tiles, shares):
    count = 2 * len(members)
    return pl.pallas_call(
        functools.partial(sum_kernel, local_slots(members)),
        out_shape=(sizes.sums,) * count,
        in_specs=[SMEM, SMEM, VMEM, HBM, VMEM],
        out_specs=(ANY,) * count,
        scratch_shapes=sizes.sum_scratch(count)
        + [
            sizes.tile_scratch(count),
            pltpu.SemaphoreType.DMA((count * sizes.blocks,)),
            pltpu.SemaphoreType.DMA((count,)),
        ],
        compiler_params=pltpu.CompilerParams(vmem_limit_bytes=VMEM_GRANT),
        cost_estimate=sizes.cost(members, 1),
        name="sum_group",
    )(order, counts, rows, tiles, shares)


def middle_group(sizes, members, order, counts, rows, tops, masses, pieces):
    count = len(pieces)
    earlier = len(tops)
    return pl.pallas_call(
        functools.partial(middle_kernel, local_slots(members), sizes.listed, earlier),
        out_shape=(jax.ShapeDtypeStruct((sizes.blocks, BLOCK), jnp.float32), sizes.stats)
        + (sizes.sums,) * count,
        in_specs=[SMEM, SMEM, VMEM] + [VMEM] * (2 * earlier) + [ANY] * count,
        out_specs=(VMEM, VMEM) + (ANY,) * count,
        scratch_shapes=sizes.panel_scratch(count)
        + [
            sizes.tile_scratch(count),
            pltpu.VMEM(sizes.stats.shape, jnp.float32),
            pltpu.VMEM(sizes.stats.shape, jnp.float32),
        ]
        + sizes.sum_scratch(count)
        + [pltpu.SemaphoreType.DMA((count,)), pltpu.SemaphoreType.DMA((count,))],
        compiler_params=pltpu.CompilerParams(vmem_limit_bytes=VMEM_GRANT),
        cost_estimate=sizes.cost(members, 2),
        name="middle_group",
    )(order, counts, rows, *tops, *masses, *pieces)


def on_device(rows, centroids, lists):
    count = lax.axis_size("blk")
    device = lax.axis_index("blk")
    cent = centroids.shape[0]
    own, stages = plan_of(count)
    groups = [(own,)] + [tuple(q for q, _, _ in stage) for stage in stages]
    slots = (2 * chip_place(lists, device, count) + ((lists ^ device) & 1)).astype(jnp.int32)
    sizes = Sizes(rows, *slots.shape, cent)
    order, counts = pairs_of(slots, 2 * max(q for members in groups for q in members) + 2)

    near = {own: centroids}
    tiles, tops, masses = [], [], []
    for members, stage in zip(groups, stages):
        arriving = [moved(near[source], shift) for _, source, shift in stage]
        pieces = [v for q in members for v in (near[q], other_core(near[q]))]
        scored = score_group(sizes, members, order, counts, rows, pieces)
        arriving, scored, near = lax.optimization_barrier((arriving, scored, near))
        tiles.append(scored[0])
        tops.append(scored[1])
        masses.append(scored[2])
        for (q, _, _), value in zip(stage, arriving):
            near[q] = value
    members = groups[-1]
    pieces = [v for q in members for v in (near[q], other_core(near[q]))]
    log_totals, shares, *sums = middle_group(sizes, members, order, counts, rows, tops, masses, pieces)

    back = {q: [] for members in groups for q in members}
    sums = {q: pair for q, pair in zip(groups[-1], zip(sums[::2], sums[1::2]))}
    arriving = []
    for at in reversed(range(len(groups))):
        crossed = {q: other_core(theirs) for q, (_, theirs) in sums.items()}
        ahead = []
        if at:
            ahead = sum_group(sizes, groups[at - 1], order, counts, rows, tiles[at - 1], shares)
        crossed, ahead, arriving, shares = lax.optimization_barrier((crossed, ahead, arriving, shares))
        if arriving:
            for value, (_, source, _) in zip(arriving, stages[at]):
                back[source].append(value)
        total = {}
        for q, (mine, _) in sums.items():
            total[q] = (mine + crossed[q]) * LINK_SCALE
            for value in back[q]:
                total[q] = total[q] + value.astype(jnp.float32)
        if at:
            arriving = [
                moved(total[q].astype(jnp.float16), shift if shift is None else -shift)
                for q, _, shift in stages[at - 1]
            ]
            sums = {q: pair for q, pair in zip(groups[at - 1], zip(ahead[::2], ahead[1::2]))}
    own_sums = total[own] * (1.0 / LINK_SCALE)
    updated = (own_sums[:cent] + PRIOR_MASS * centroids.astype(jnp.float32)) / (
        own_sums[cent, :cent][:, None] + PRIOR_MASS
    )
    return updated, log_totals.reshape(-1)


def solution(mesh):
    placed = P(("groups", "blk"), None)
    return jax.shard_map(
        on_device,
        mesh=mesh,
        in_specs=(placed, placed, placed),
        out_specs=(placed, P(("groups", "blk"))),
        check_vma=False,
    )
```

time: 153 us -> 118 us (0.77)
  the two profiles are of different devices: /device:TPU:0 before, /device:TPU:6 now
where the time goes in v1:
time: 118 us
  Pallas kernels  57.4 us (49%)
  waiting for transfers between devices  29 us (25%)
  starting transfers between devices  22.6 us (19%)
  other arithmetic  4.59 us (4%)
  local copies, waits for them, and re-layouts  3.47 us (3%)
    ppermute x6, waiting for transfers between devices, moved(): lax.ppermute(value, 'blk', [(i, (i + shift) % count) for i in range(count)])  23 us
    pallas_call x3, Pallas kernels, score_group(): pl.pallas_call(functools.partial(score_kernel, local_slots(members)), out...  21.7 us
    pallas_call x3, Pallas kernels, sum_group(): pl.pallas_call(functools.partial(sum_kernel, local_slots(members)), out_s...  19.1 us
    pallas_call x1, Pallas kernels, middle_group(): pl.pallas_call(functools.partial(middle_kernel, local_slots(members), siz...  16.7 us
    ppermute x14, starting transfers between devices, other_core(): return lax.ppermute(value, 'blk', [(i, i ^ 1) for i in range(count)])  9.45 us
    ppermute x6, starting transfers between devices, moved(): lax.ppermute(value, 'blk', [(i, (i + shift) % count) for i in range(count)])  9.4 us
    ppermute x6, waiting for transfers between devices, moved(): return lax.ppermute(value, 'blk', [(i, i ^ 2) for i in range(count)])  4.2 us
    ppermute x6, starting transfers between devices, moved(): return lax.ppermute(value, 'blk', [(i, i ^ 2) for i in range(count)])  3.71 us
  transfers between devices with their start and end apart: 26, of which 11 were waited for; matrix products, arithmetic and copies ran while one was open for 2% of the time, Pallas kernels for 35%

profile of v1, /device:TPU:6, one launch (start us, length us, event | category | flops | bytes accessed | tf_op | source)
XLA Modules:
  0.0 117.9 jit_solution(7266306739491689716)
XLA Ops:
  0.7 0.6 collective-permute-start.1
  1.3 1.6 %collective-permute-start = (bf16[256,768]{1,0:T(8,128)(2,1)}, bf16[256,768]{1,0:T(8,128)(2,1)S(1)}, u32[]{:S(2)}, u32[]{:S(2)}) collective-permute-start(bf16[256,768]{1,0:T(8,128)(2,1)} %refs_0_.1), channel_id=1, source_target_pairs={{0,4},{1,5},{2,6},{3,7},{4,8},{5,9},{6,10},{7,11},{8,12},{9,13},{1... | collective-permute-start | bytes 1179656 | tf_op jit(solution)/shard_map/ppermute | solution.py:50
  2.9 0.7 fusion.9
  4.2 2.8 %copy-done = bf16[4096,768]{1,0:T(8,128)(2,1)S(1)} copy-done((bf16[4096,768]{1,0:T(8,128)(2,1)S(1)}, bf16[4096,768]{1,0:T(8,128)(2,1)}, u32[]{:S(2)}) %copy-start) | copy-done | bytes 6291480
  7.0 9.0 %score_group.3 = (f32[64,256,256]{2,1,0:T(8,128)}, f32[96,256]{1,0:T(8,128)S(1)}, f32[96,256]{1,0:T(8,128)S(1)}) custom-call(s32[256]{0:T(256)S(1)} %reshape.57.order_ref, s32[16]{0:T(128)S(1)} %convert_reduce_fusion.counts_ref, bf16[4096,768]{1,0:T(8,128)(2,1)S(1)} %copy-done, bf16[256,768]{1,0:T(8,128)(2,1)} %refs_0_.1, ...), custom_call_target="tpu_custom_call" | custom-call | flops 1380525184 | bytes 9886573 | tf_op jit(solution)/shard_map/score_group/pallas_call | solution.py:291
  16.1 0.5 collective-permute-start.5
  16.8 2.4 %collective-permute-start.4 = (bf16[256,768]{1,0:T(8,128)(2,1)S(1)}, bf16[256,768]{1,0:T(8,128)(2,1)S(1)}, u32[]{:S(2)}, u32[]{:S(2)}) collective-permute-start(bf16[256,768]{1,0:T(8,128)(2,1)S(1)} %collective-permute-done.refs_0_), channel_id=1, source_target_pairs={{0,2},{1,3},{2,0},{3,1},{4,6},{5,7},{6,4},{7,5},{8,10},{9,11},{10,... | collective-permute-start | bytes 1179656 | tf_op jit(solution)/shard_map/ppermute | solution.py:49
  19.2 5.9 %score_group.4 = (f32[64,256,256]{2,1,0:T(8,128)}, f32[96,256]{1,0:T(8,128)S(1)}, f32[96,256]{1,0:T(8,128)S(1)}) custom-call(s32[256]{0:T(256)S(1)} %reshape.57.order_ref, s32[16]{0:T(128)S(1)} %convert_reduce_fusion.counts_ref, bf16[4096,768]{1,0:T(8,128)(2,1)S(1)} %copy-done, bf16[256,768]{1,0:T(8,128)(2,1)S(1)} %collective-permute-done.refs_0_, ...), custom_call_target="tpu_custom_call" | custom-call | flops 2761050368 | bytes 13481691 | tf_op jit(solution)/shard_map/score_group/pallas_call | solution.py:291
  25.1 2.8 %collective-permute-done.3.refs_0_ = bf16[256,768]{1,0:T(8,128)(2,1)S(1)} collective-permute-done((bf16[256,768]{1,0:T(8,128)(2,1)}, bf16[256,768]{1,0:T(8,128)(2,1)S(1)}, u32[]{:S(2)}, u32[]{:S(2)}) %collective-permute-start.3) | collective-permute-done | bytes 393248 | tf_op jit(solution)/shard_map/ppermute | solution.py:50
  28.2 0.5 collective-permute-start.9
  28.7 3.8 %collective-permute-start.7 = (bf16[256,768]{1,0:T(8,128)(2,1)S(1)}, bf16[256,768]{1,0:T(8,128)(2,1)S(1)}, u32[]{:S(2)}, u32[]{:S(2)}) collective-permute-start(bf16[256,768]{1,0:T(8,128)(2,1)S(1)} %collective-permute-done.4.refs_2_), channel_id=1, source_target_pairs={{0,4},{1,5},{2,6},{3,7},{4,8},{5,9},{6,10},{7,11},{8,12},{9,13},{1... | collective-permute-start | bytes 1179656 | tf_op jit(solution)/shard_map/ppermute | solution.py:50
  32.5 6.8 %score_group.5 = (f32[64,256,256]{2,1,0:T(8,128)}, f32[96,256]{1,0:T(8,128)S(1)}, f32[96,256]{1,0:T(8,128)S(1)}) custom-call(s32[256]{0:T(256)S(1)} %reshape.57.order_ref, s32[16]{0:T(128)S(1)} %convert_reduce_fusion.counts_ref, bf16[4096,768]{1,0:T(8,128)(2,1)S(1)} %copy-done, bf16[256,768]{1,0:T(8,128)(2,1)S(1)} %collective-permute-done.3.refs_0_, ...), custom_call_target="tpu_custom_call" | custom-call | flops 2761050368 | bytes 13481691 | tf_op jit(solution)/shard_map/score_group/pallas_call | solution.py:291
  39.4 2.2 %collective-permute-done.7.refs_6_ = bf16[256,768]{1,0:T(8,128)(2,1)S(1)} collective-permute-done((bf16[256,768]{1,0:T(8,128)(2,1)S(1)}, bf16[256,768]{1,0:T(8,128)(2,1)S(1)}, u32[]{:S(2)}, u32[]{:S(2)}) %collective-permute-start.7) | collective-permute-done | bytes 393248 | tf_op jit(solution)/shard_map/ppermute | solution.py:50
  41.6 1.8 %collective-permute-done.8.refs_8_ = bf16[256,768]{1,0:T(8,128)(2,1)S(1)} collective-permute-done((bf16[256,768]{1,0:T(8,128)(2,1)S(1)}, bf16[256,768]{1,0:T(8,128)(2,1)S(1)}, u32[]{:S(2)}, u32[]{:S(2)}) %collective-permute-start.8) | collective-permute-done | bytes 393248 | tf_op jit(solution)/shard_map/ppermute | solution.py:49
  43.3 0.5 collective-permute-start.12
  43.9 1.2 %collective-permute-done.11.refs_7_ = bf16[256,768]{1,0:T(8,128)(2,1)S(1)} collective-permute-done((bf16[256,768]{1,0:T(8,128)(2,1)S(1)}, bf16[256,768]{1,0:T(8,128)(2,1)S(1)}, u32[]{:S(2)}, u32[]{:S(2)}) %collective-permute-start.11) | collective-permute-done | bytes 393248 | tf_op jit(solution)/shard_map/ppermute | solution.py:55
  45.1 0.6 collective-permute-done.12.refs_9_
  45.6 16.7 %middle_group.1 = (f32[16,256]{1,0:T(8,128)S(1)}, f32[96,256]{1,0:T(8,128)S(1)}, f32[264,768]{1,0:T(8,128)S(1)}, f32[264,768]{1,0:T(8,128)S(1)}, f32[264,768]{1,0:T(8,128)S(1)}, /*index=5*/f32[264,768]{1,0:T(8,128)S(1)}) custom-call(s32[256]{0:T(256)S(1)} %reshape.57.order_ref, s32[16]{0:T(128)S(1)} %convert_reduce_fusion.counts_ref, ...), custom_call_target="tpu_custom_call" | custom-call | flops 5522100736 | bytes 13481691 | tf_op jit(solution)/shard_map/middle_group/pallas_call | solution.py:330
  62.3 6.6 %collective-permute-start.13 = (f32[264,768]{1,0:T(8,128)S(1)}, f32[264,768]{1,0:T(8,128)S(1)}, u32[]{:S(2)}, u32[]{:S(2)}) collective-permute-start(f32[264,768]{1,0:T(8,128)S(1)} %get-tuple-element.90), channel_id=1, source_target_pairs={{0,1},{1,0},{2,3},{3,2},{4,5},{5,4},{6,7},{7,6},{8,9},{9,8},{10,11... | collective-permute-start | bytes 2433032 | tf_op jit(solution)/shard_map/ppermute | solution.py:55
  69.0 6.3 %sum_group.3 = (f32[264,768]{1,0:T(8,128)S(1)}, f32[264,768]{1,0:T(8,128)S(1)}, f32[264,768]{1,0:T(8,128)S(1)}, f32[264,768]{1,0:T(8,128)S(1)}) custom-call(s32[256]{0:T(256)S(1)} %reshape.57.order_ref, s32[16]{0:T(128)S(1)} %convert_reduce_fusion.counts_ref, bf16[4096,768]{1,0:T(8,128)(2,1)S(1)} %copy-done, f32[64,256,256]{2,1,0:T(8,128)} %get-tuple-element.92.tiles_ref, ...), custom_call_target="tpu_custom_call" | custom-call | flops 2761050368 | bytes 13481691 | tf_op jit(solution)/shard_map/sum_group/pallas_call | solution.py:310
  75.4 0.5 collective-permute-start.16
  76.3 5.3 %sum_group.4 = (f32[264,768]{1,0:T(8,128)S(1)}, f32[264,768]{1,0:T(8,128)S(1)}, f32[264,768]{1,0:T(8,128)S(1)}, f32[264,768]{1,0:T(8,128)S(1)}) custom-call(s32[256]{0:T(256)S(1)} %reshape.57.order_ref, s32[16]{0:T(128)S(1)} %convert_reduce_fusion.counts_ref, bf16[4096,768]{1,0:T(8,128)(2,1)S(1)} %copy-done, f32[64,256,256]{2,1,0:T(8,128)} %get-tuple-element.100.tiles_ref, ...), custom_call_target="tpu_custom_call" | custom-call | flops 2761050368 | bytes 13481691 | tf_op jit(solution)/shard_map/sum_group/pallas_call | solution.py:310
  81.6 5.8 %collective-permute-done.17 = f16[264,768]{1,0:T(8,128)(2,1)S(1)} collective-permute-done((f16[264,768]{1,0:T(8,128)(2,1)S(1)}, f16[264,768]{1,0:T(8,128)(2,1)S(1)}, u32[]{:S(2)}, u32[]{:S(2)}) %collective-permute-start.17) | collective-permute-done | bytes 405536 | tf_op jit(solution)/shard_map/ppermute | solution.py:50
  87.7 0.5 collective-permute-start.20
  88.4 1.8 %collective-permute-start.21 = (f16[264,768]{1,0:T(8,128)(2,1)S(1)}, f16[264,768]{1,0:T(8,128)(2,1)S(1)}, u32[]{:S(2)}, u32[]{:S(2)}) collective-permute-start(f16[264,768]{1,0:T(8,128)(2,1)S(1)} %add_convert_fusion.2), channel_id=1, source_target_pairs={{0,4},{1,5},{2,6},{3,7},{4,8},{5,9},{6,10},{7,11},{8,12},{9,13},{1... | collective-permute-start | bytes 1216520 | tf_op jit(solution)/shard_map/ppermute | solution.py:50
  90.7 7.5 %sum_group.5 = (f32[264,768]{1,0:T(8,128)S(1)}, f32[264,768]{1,0:T(8,128)S(1)}) custom-call(s32[256]{0:T(256)S(1)} %reshape.57.order_ref, s32[16]{0:T(128)S(1)} %convert_reduce_fusion.counts_ref, bf16[4096,768]{1,0:T(8,128)(2,1)S(1)} %copy-done, f32[64,256,256]{2,1,0:T(8,128)} %get-tuple-element.112.tiles_ref, f32[96,256]{1,0:T(8,128)S(1)} %get-tuple-element.113.shares), custom_call_target="tpu_custom_call" | custom-call | flops 1380525184 | bytes 9886573 | tf_op jit(solution)/shard_map/sum_group/pallas_call | solution.py:310
  98.2 3.4 %collective-permute-done.21 = f16[264,768]{1,0:T(8,128)(2,1)S(1)} collective-permute-done((f16[264,768]{1,0:T(8,128)(2,1)S(1)}, f16[264,768]{1,0:T(8,128)(2,1)S(1)}, u32[]{:S(2)}, u32[]{:S(2)}) %collective-permute-start.21) | collective-permute-done | bytes 405536 | tf_op jit(solution)/shard_map/ppermute | solution.py:50
  101.9 2.0 %collective-permute-start.24 = (f16[264,768]{1,0:T(8,128)(2,1)S(1)}, f16[264,768]{1,0:T(8,128)(2,1)S(1)}, u32[]{:S(2)}, u32[]{:S(2)}) collective-permute-start(f16[264,768]{1,0:T(8,128)(2,1)S(1)} %add_convert_fusion), channel_id=1, source_target_pairs={{0,12},{1,13},{2,14},{3,15},{4,0},{5,1},{6,2},{7,3},{8,4},{9,5},{1... | collective-permute-start | bytes 1216520 | tf_op jit(solution)/shard_map/ppermute | solution.py:50
  104.3 0.6 copy.6
  104.9 8.8 %collective-permute-done.24 = f16[264,768]{1,0:T(8,128)(2,1)S(1)} collective-permute-done((f16[264,768]{1,0:T(8,128)(2,1)S(1)}, f16[264,768]{1,0:T(8,128)(2,1)S(1)}, u32[]{:S(2)}, u32[]{:S(2)}) %collective-permute-start.24) | collective-permute-done | bytes 405536 | tf_op jit(solution)/shard_map/ppermute | solution.py:50
  113.7 1.8 %collective-permute-done.25 = f16[264,768]{1,0:T(8,128)(2,1)S(1)} collective-permute-done((f16[264,768]{1,0:T(8,128)(2,1)S(1)}, f16[264,768]{1,0:T(8,128)(2,1)S(1)}, u32[]{:S(2)}, u32[]{:S(2)}) %collective-permute-start.25) | collective-permute-done | bytes 405536 | tf_op jit(solution)/shard_map/ppermute | solution.py:49
  115.9 2.0 %fusion = f32[256,768]{1,0:T(8,128)} fusion(f32[264,768]{1,0:T(8,128)S(1)} %add_multiply_fusion, bf16[256,768]{1,0:T(8,128)(2,1)} %refs_0_.1, f32[256]{0:T(256)S(1)} %bitcast.5), kind=kLoop, calls=%fused_computation.8 | loop fusion | flops 786432 | bytes 1967104 | tf_op jit(solution)/shard_map/div | solution.py:400
  (49 shorter events, 4.0 us)
Async XLA Ops:
  0.6 3.6 %collective-permute-start.2 = (bf16[256,768]{1,0:T(8,128)(2,1)}, bf16[256,768]{1,0:T(8,128)(2,1)S(1)}, u32[]{:S(2)}, u32[]{:S(2)}) collective-permute-start(bf16[256,768]{1,0:T(8,128)(2,1)} %refs_0_.1), channel_id=1, source_target_pairs={{0,1},{1,0},{2,3},{3,2},{4,5},{5,4},{6,7},{7,6},{8,9},{9,8},{10,11... | collective-permute-start | bytes 1179656 | tf_op jit(solution)/shard_map/ppermute | solution.py:55
  0.7 15.3 %collective-permute-start.1 = (bf16[256,768]{1,0:T(8,128)(2,1)}, bf16[256,768]{1,0:T(8,128)(2,1)S(1)}, u32[]{:S(2)}, u32[]{:S(2)}) collective-permute-start(bf16[256,768]{1,0:T(8,128)(2,1)} %refs_0_.1), channel_id=1, source_target_pairs={{0,2},{1,3},{2,0},{3,1},{4,6},{5,7},{6,4},{7,5},{8,10},{9,11},{10,... | collective-permute-start | bytes 1179656 | tf_op jit(solution)/shard_map/ppermute | solution.py:49
  1.3 14.7 %collective-permute-start = (bf16[256,768]{1,0:T(8,128)(2,1)}, bf16[256,768]{1,0:T(8,128)(2,1)S(1)}, u32[]{:S(2)}, u32[]{:S(2)}) collective-permute-start(bf16[256,768]{1,0:T(8,128)(2,1)} %refs_0_.1), channel_id=1, source_target_pairs={{0,4},{1,5},{2,6},{3,7},{4,8},{5,9},{6,10},{7,11},{8,12},{9,13},{1... | collective-permute-start | bytes 1179656 | tf_op jit(solution)/shard_map/ppermute | solution.py:50
  4.2 2.8 %copy-start = (bf16[4096,768]{1,0:T(8,128)(2,1)S(1)}, bf16[4096,768]{1,0:T(8,128)(2,1)}, u32[]{:S(2)}) copy-start(bf16[4096,768]{1,0:T(8,128)(2,1)} %x.13) | copy-start | bytes 18874372
  16.0 3.2 %collective-permute-start.6 = (bf16[256,768]{1,0:T(8,128)(2,1)S(1)}, bf16[256,768]{1,0:T(8,128)(2,1)S(1)}, u32[]{:S(2)}, u32[]{:S(2)}) collective-permute-start(bf16[256,768]{1,0:T(8,128)(2,1)S(1)} %collective-permute-done.1.refs_2_), channel_id=1, source_target_pairs={{0,1},{1,0},{2,3},{3,2},{4,5},{5,4},{6,7},{7,6},{8,9},{9,8},{10,11... | collective-permute-start | bytes 1179656 | tf_op jit(solution)/shard_map/ppermute | solution.py:55
  16.1 3.1 %collective-permute-start.5 = (bf16[256,768]{1,0:T(8,128)(2,1)S(1)}, bf16[256,768]{1,0:T(8,128)(2,1)S(1)}, u32[]{:S(2)}, u32[]{:S(2)}) collective-permute-start(bf16[256,768]{1,0:T(8,128)(2,1)S(1)} %collective-permute-done.refs_0_), channel_id=1, source_target_pairs={{0,1},{1,0},{2,3},{3,2},{4,5},{5,4},{6,7},{7,6},{8,9},{9,8},{10,11... | collective-permute-start | bytes 1179656 | tf_op jit(solution)/shard_map/ppermute | solution.py:55
  16.6 11.3 %collective-permute-start.3 = (bf16[256,768]{1,0:T(8,128)(2,1)}, bf16[256,768]{1,0:T(8,128)(2,1)S(1)}, u32[]{:S(2)}, u32[]{:S(2)}) collective-permute-start(bf16[256,768]{1,0:T(8,128)(2,1)} %refs_0_.1), channel_id=1, source_target_pairs={{0,12},{1,13},{2,14},{3,15},{4,0},{5,1},{6,2},{7,3},{8,4},{9,5},{1... | collective-permute-start | bytes 1179656 | tf_op jit(solution)/shard_map/ppermute | solution.py:50
  16.8 11.4 %collective-permute-start.4 = (bf16[256,768]{1,0:T(8,128)(2,1)S(1)}, bf16[256,768]{1,0:T(8,128)(2,1)S(1)}, u32[]{:S(2)}, u32[]{:S(2)}) collective-permute-start(bf16[256,768]{1,0:T(8,128)(2,1)S(1)} %collective-permute-done.refs_0_), channel_id=1, source_target_pairs={{0,2},{1,3},{2,0},{3,1},{4,6},{5,7},{6,4},{7,5},{8,10},{9,11},{10,... | collective-permute-start | bytes 1179656 | tf_op jit(solution)/shard_map/ppermute | solution.py:49
  28.2 4.3 %collective-permute-start.10 = (bf16[256,768]{1,0:T(8,128)(2,1)S(1)}, bf16[256,768]{1,0:T(8,128)(2,1)S(1)}, u32[]{:S(2)}, u32[]{:S(2)}) collective-permute-start(bf16[256,768]{1,0:T(8,128)(2,1)S(1)} %collective-permute-done.4.refs_2_), channel_id=1, source_target_pairs={{0,1},{1,0},{2,3},{3,2},{4,5},{5,4},{6,7},{7,6},{8,9},{9,8},{10,11... | collective-permute-start | bytes 1179656 | tf_op jit(solution)/shard_map/ppermute | solution.py:55
  28.2 4.3 %collective-permute-start.9 = (bf16[256,768]{1,0:T(8,128)(2,1)S(1)}, bf16[256,768]{1,0:T(8,128)(2,1)S(1)}, u32[]{:S(2)}, u32[]{:S(2)}) collective-permute-start(bf16[256,768]{1,0:T(8,128)(2,1)S(1)} %collective-permute-done.3.refs_0_), channel_id=1, source_target_pairs={{0,1},{1,0},{2,3},{3,2},{4,5},{5,4},{6,7},{7,6},{8,9},{9,8},{10,11... | collective-permute-start | bytes 1179656 | tf_op jit(solution)/shard_map/ppermute | solution.py:55
  28.7 12.8 %collective-permute-start.7 = (bf16[256,768]{1,0:T(8,128)(2,1)S(1)}, bf16[256,768]{1,0:T(8,128)(2,1)S(1)}, u32[]{:S(2)}, u32[]{:S(2)}) collective-permute-start(bf16[256,768]{1,0:T(8,128)(2,1)S(1)} %collective-permute-done.4.refs_2_), channel_id=1, source_target_pairs={{0,4},{1,5},{2,6},{3,7},{4,8},{5,9},{6,10},{7,11},{8,12},{9,13},{1... | collective-permute-start | bytes 1179656 | tf_op jit(solution)/shard_map/ppermute | solution.py:50
  32.5 10.8 %collective-permute-start.8 = (bf16[256,768]{1,0:T(8,128)(2,1)S(1)}, bf16[256,768]{1,0:T(8,128)(2,1)S(1)}, u32[]{:S(2)}, u32[]{:S(2)}) collective-permute-start(bf16[256,768]{1,0:T(8,128)(2,1)S(1)} %collective-permute-done.3.refs_0_), channel_id=1, source_target_pairs={{0,2},{1,3},{2,0},{3,1},{4,6},{5,7},{6,4},{7,5},{8,10},{9,11},{10,... | collective-permute-start | bytes 1179656 | tf_op jit(solution)/shard_map/ppermute | solution.py:49
  43.3 1.7 %collective-permute-start.11 = (bf16[256,768]{1,0:T(8,128)(2,1)S(1)}, bf16[256,768]{1,0:T(8,128)(2,1)S(1)}, u32[]{:S(2)}, u32[]{:S(2)}) collective-permute-start(bf16[256,768]{1,0:T(8,128)(2,1)S(1)} %collective-permute-done.7.refs_6_), channel_id=1, source_target_pairs={{0,1},{1,0},{2,3},{3,2},{4,5},{5,4},{6,7},{7,6},{8,9},{9,8},{10,11... | collective-permute-start | bytes 1179656 | tf_op jit(solution)/shard_map/ppermute | solution.py:55
  43.3 2.3 %collective-permute-start.12 = (bf16[256,768]{1,0:T(8,128)(2,1)S(1)}, bf16[256,768]{1,0:T(8,128)(2,1)S(1)}, u32[]{:S(2)}, u32[]{:S(2)}) collective-permute-start(bf16[256,768]{1,0:T(8,128)(2,1)S(1)} %collective-permute-done.8.refs_8_), channel_id=1, source_target_pairs={{0,1},{1,0},{2,3},{3,2},{4,5},{5,4},{6,7},{7,6},{8,9},{9,8},{10,11... | collective-permute-start | bytes 1179656 | tf_op jit(solution)/shard_map/ppermute | solution.py:55
  62.3 13.0 %collective-permute-start.13 = (f32[264,768]{1,0:T(8,128)S(1)}, f32[264,768]{1,0:T(8,128)S(1)}, u32[]{:S(2)}, u32[]{:S(2)}) collective-permute-start(f32[264,768]{1,0:T(8,128)S(1)} %get-tuple-element.90), channel_id=1, source_target_pairs={{0,1},{1,0},{2,3},{3,2},{4,5},{5,4},{6,7},{7,6},{8,9},{9,8},{10,11... | collective-permute-start | bytes 2433032 | tf_op jit(solution)/shard_map/ppermute | solution.py:55
  68.9 6.4 %collective-permute-start.14 = (f32[264,768]{1,0:T(8,128)S(1)}, f32[264,768]{1,0:T(8,128)S(1)}, u32[]{:S(2)}, u32[]{:S(2)}) collective-permute-start(f32[264,768]{1,0:T(8,128)S(1)} %get-tuple-element.91), channel_id=1, source_target_pairs={{0,1},{1,0},{2,3},{3,2},{4,5},{5,4},{6,7},{7,6},{8,9},{9,8},{10,11... | collective-permute-start | bytes 2433032 | tf_op jit(solution)/shard_map/ppermute | solution.py:55
  75.3 12.4 %collective-permute-start.15 = (f32[264,768]{1,0:T(8,128)S(1)}, f32[264,768]{1,0:T(8,128)S(1)}, u32[]{:S(2)}, u32[]{:S(2)}) collective-permute-start(f32[264,768]{1,0:T(8,128)S(1)} %get-tuple-element.98), channel_id=1, source_target_pairs={{0,1},{1,0},{2,3},{3,2},{4,5},{5,4},{6,7},{7,6},{8,9},{9,8},{10,11... | collective-permute-start | bytes 2433032 | tf_op jit(solution)/shard_map/ppermute | solution.py:55
  75.4 12.3 %collective-permute-start.16 = (f32[264,768]{1,0:T(8,128)S(1)}, f32[264,768]{1,0:T(8,128)S(1)}, u32[]{:S(2)}, u32[]{:S(2)}) collective-permute-start(f32[264,768]{1,0:T(8,128)S(1)} %get-tuple-element.99), channel_id=1, source_target_pairs={{0,1},{1,0},{2,3},{3,2},{4,5},{5,4},{6,7},{7,6},{8,9},{9,8},{10,11... | collective-permute-start | bytes 2433032 | tf_op jit(solution)/shard_map/ppermute | solution.py:55
  76.0 11.4 %collective-permute-start.17 = (f16[264,768]{1,0:T(8,128)(2,1)S(1)}, f16[264,768]{1,0:T(8,128)(2,1)S(1)}, u32[]{:S(2)}, u32[]{:S(2)}) collective-permute-start(f16[264,768]{1,0:T(8,128)(2,1)S(1)} %multiply_convert_fusion.2), channel_id=1, source_target_pairs={{0,12},{1,13},{2,14},{3,15},{4,0},{5,1},{6,2},{7,3},{8,4},{9,5},{1... | collective-permute-start | bytes 1216520 | tf_op jit(solution)/shard_map/ppermute | solution.py:50
  76.3 11.4 %collective-permute-start.18 = (f16[264,768]{1,0:T(8,128)(2,1)S(1)}, f16[264,768]{1,0:T(8,128)(2,1)S(1)}, u32[]{:S(2)}, u32[]{:S(2)}) collective-permute-start(f16[264,768]{1,0:T(8,128)(2,1)S(1)} %multiply_convert_fusion.1), channel_id=1, source_target_pairs={{0,2},{1,3},{2,0},{3,1},{4,6},{5,7},{6,4},{7,5},{8,10},{9,11},{10,... | collective-permute-start | bytes 1216520 | tf_op jit(solution)/shard_map/ppermute | solution.py:49
  87.7 13.9 %collective-permute-start.19 = (f32[264,768]{1,0:T(8,128)S(1)}, f32[264,768]{1,0:T(8,128)S(1)}, u32[]{:S(2)}, u32[]{:S(2)}) collective-permute-start(f32[264,768]{1,0:T(8,128)S(1)} %get-tuple-element.110), channel_id=1, source_target_pairs={{0,1},{1,0},{2,3},{3,2},{4,5},{5,4},{6,7},{7,6},{8,9},{9,8},{10,11... | collective-permute-start | bytes 2433032 | tf_op jit(solution)/shard_map/ppermute | solution.py:55
  87.7 13.9 %collective-permute-start.20 = (f32[264,768]{1,0:T(8,128)S(1)}, f32[264,768]{1,0:T(8,128)S(1)}, u32[]{:S(2)}, u32[]{:S(2)}) collective-permute-start(f32[264,768]{1,0:T(8,128)S(1)} %get-tuple-element.111), channel_id=1, source_target_pairs={{0,1},{1,0},{2,3},{3,2},{4,5},{5,4},{6,7},{7,6},{8,9},{9,8},{10,11... | collective-permute-start | bytes 2433032 | tf_op jit(solution)/shard_map/ppermute | solution.py:55
  88.4 13.2 %collective-permute-start.21 = (f16[264,768]{1,0:T(8,128)(2,1)S(1)}, f16[264,768]{1,0:T(8,128)(2,1)S(1)}, u32[]{:S(2)}, u32[]{:S(2)}) collective-permute-start(f16[264,768]{1,0:T(8,128)(2,1)S(1)} %add_convert_fusion.2), channel_id=1, source_target_pairs={{0,4},{1,5},{2,6},{3,7},{4,8},{5,9},{6,10},{7,11},{8,12},{9,13},{1... | collective-permute-start | bytes 1216520 | tf_op jit(solution)/shard_map/ppermute | solution.py:50
  90.4 11.2 %collective-permute-start.22 = (f16[264,768]{1,0:T(8,128)(2,1)S(1)}, f16[264,768]{1,0:T(8,128)(2,1)S(1)}, u32[]{:S(2)}, u32[]{:S(2)}) collective-permute-start(f16[264,768]{1,0:T(8,128)(2,1)S(1)} %add_convert_fusion.1), channel_id=1, source_target_pairs={{0,2},{1,3},{2,0},{3,1},{4,6},{5,7},{6,4},{7,5},{8,10},{9,11},{10,... | collective-permute-start | bytes 1216520 | tf_op jit(solution)/shard_map/ppermute | solution.py:49
  101.6 13.9 %collective-permute-start.23 = (f32[264,768]{1,0:T(8,128)S(1)}, f32[264,768]{1,0:T(8,128)S(1)}, u32[]{:S(2)}, u32[]{:S(2)}) collective-permute-start(f32[264,768]{1,0:T(8,128)S(1)} %get-tuple-element.123), channel_id=1, source_target_pairs={{0,1},{1,0},{2,3},{3,2},{4,5},{5,4},{6,7},{7,6},{8,9},{9,8},{10,11... | collective-permute-start | bytes 2433032 | tf_op jit(solution)/shard_map/ppermute | solution.py:55
  101.9 11.8 %collective-permute-start.24 = (f16[264,768]{1,0:T(8,128)(2,1)S(1)}, f16[264,768]{1,0:T(8,128)(2,1)S(1)}, u32[]{:S(2)}, u32[]{:S(2)}) collective-permute-start(f16[264,768]{1,0:T(8,128)(2,1)S(1)} %add_convert_fusion), channel_id=1, source_target_pairs={{0,12},{1,13},{2,14},{3,15},{4,0},{5,1},{6,2},{7,3},{8,4},{9,5},{1... | collective-permute-start | bytes 1216520 | tf_op jit(solution)/shard_map/ppermute | solution.py:50
  104.0 11.6 %collective-permute-start.25 = (f16[264,768]{1,0:T(8,128)(2,1)S(1)}, f16[264,768]{1,0:T(8,128)(2,1)S(1)}, u32[]{:S(2)}, u32[]{:S(2)}) collective-permute-start(f16[264,768]{1,0:T(8,128)(2,1)S(1)} %multiply_convert_fusion), channel_id=1, source_target_pairs={{0,2},{1,3},{2,0},{3,1},{4,6},{5,7},{6,4},{7,5},{8,10},{9,11},{10,... | collective-permute-start | bytes 1216520 | tf_op jit(solution)/shard_map/ppermute | solution.py:49

commit v2 on v1

--- a/solution.py
+++ b/solution.py
@@ -119,7 +119,9 @@
     return powers, top, jnp.sum(powers, axis=0, keepdims=True)
 
 
-def score_loop(slots, order_ref, counts_ref, x, panels, norms, tops, masses, tiles, done):
+def score_loop(
+    slots, order_ref, counts_ref, x, panels, norms, tops, masses, tiles, here, done
+):
     blocks = x.shape[0] // BLOCK
     tops[...] = jnp.full_like(tops, -jnp.inf)
     masses[...] = jnp.zeros_like(masses)
@@ -127,6 +129,7 @@
 
         def some(first, number):
             work = some_pairs(order_ref, counts_ref, slot, blocks, first, number)
+            here(work[-1][1])
             found = [tile_of(panels[p], norms[p], rows_of(x, b)) for _, b, _ in work]
             for (i, _, at), (powers, top, mass) in zip(work, found):
                 tiles[p * blocks + i] = powers
@@ -187,20 +190,43 @@
         lax.fori_loop(0, held, lambda i, _: (act(p * blocks + i), 0)[1], 0)
 
 
-def score_kernel(slots, order_ref, counts_ref, x, *refs):
+def score_kernel(slots, fetch, order_ref, counts_ref, rows_ref, *refs):
     pieces = len(slots)
     piece_refs = refs[:pieces]
-    tiles_ref, tops, masses, panels, norms, tiles, panel_sem, tile_sem = refs[pieces:]
-    load_panels(piece_refs, panels, norms, panel_sem)()
+    tiles_ref, tops, masses = refs[pieces : pieces + 3]
+    refs = refs[pieces + 3 :]
+    x = refs[0] if fetch else rows_ref
+    panels, norms, tiles, panel_sem, tile_sem = refs[1:6] if fetch else refs[:5]
+    blocks = x.shape[0] // BLOCK
+    finish_panels = load_panels(piece_refs, panels, norms, panel_sem)
+    here = lambda b: None
+    if fetch:
+        row_sem, fetched = refs[6:]
+
+        def bring(b):
+            span = pl.ds(pl.multiple_of(b * BLOCK, BLOCK), BLOCK)
+            return pltpu.make_async_copy(rows_ref.at[span], x.at[span], row_sem.at[b])
+
+        for b in range(blocks):
+            bring(b).start()
+        fetched[0] = 0
+
+        def here(b):
+            first = fetched[0]
+            lax.fori_loop(first, b + 1, lambda k, _: (bring(k).wait(), 0)[1], 0)
+            fetched[0] = jnp.maximum(first, b + 1)
+
+    finish_panels()
 
     def outgoing(j):
         return pltpu.make_async_copy(tiles.at[j], tiles_ref.at[j], tile_sem.at[j])
 
     score_loop(
-        slots, order_ref, counts_ref, x, panels, norms, tops, masses, tiles,
+        slots, order_ref, counts_ref, x, panels, norms, tops, masses, tiles, here,
         lambda j: outgoing(j).start(),
     )
-    over_tiles(slots, counts_ref, x.shape[0] // BLOCK, lambda j: outgoing(j).wait())
+    here(blocks - 1)
+    over_tiles(slots, counts_ref, blocks, lambda j: outgoing(j).wait())
 
 
 def sum_kernel(slots, order_ref, counts_ref, x, tiles_ref, shares, *refs):
@@ -232,7 +258,8 @@
     clear_sums(acc, totals)
     finish_panels()
     score_loop(
-        slots, order_ref, counts_ref, x, panels, norms, tops, masses, tiles, lambda j: None
+        slots, order_ref, counts_ref, x, panels, norms, tops, masses, tiles,
+        lambda b: None, lambda j: None,
     )
     width = tops.shape[1]
     top = functools.reduce(jnp.maximum, [ref[...] for ref in stat_refs[:earlier]], tops[...])
@@ -262,8 +289,8 @@
         self.sums = jax.ShapeDtypeStruct((cent + EXTRA, self.width), jnp.float32)
         self.tiles = jax.ShapeDtypeStruct((4 * blocks, cent, BLOCK), jnp.float32)
 
-    def cost(self, members, products):
-        pairs = self.blocks * self.listed * 2 * len(members) / 14
+    def cost(self, slots, products):
+        pairs = self.blocks * self.listed * len(slots) / 14
         return pl.CostEstimate(
             flops=int(2 * products * pairs * self.cent * BLOCK * self.width),
             bytes_accessed=int(2 * self.blocks * BLOCK * self.width + 4 * pairs * self.cent * BLOCK),
@@ -286,29 +313,35 @@
         return pltpu.VMEM((pieces * self.blocks, self.cent, BLOCK), jnp.float32)
 
 
-def score_group(sizes, members, order, counts, rows, pieces):
+def score_group(sizes, slots, order, counts, rows, pieces, fetch):
     count = len(pieces)
+    outs = (sizes.tiles, sizes.stats, sizes.stats)
+    rows_outs, rows_scratch = (), []
+    if fetch:
+        rows_outs = (jax.ShapeDtypeStruct(rows.shape, rows.dtype),)
+        rows_scratch = [pltpu.SemaphoreType.DMA((sizes.blocks,)), pltpu.SMEM((1,), jnp.int32)]
     return pl.pallas_call(
-        functools.partial(score_kernel, local_slots(members)),
-        out_shape=(sizes.tiles, sizes.stats, sizes.stats),
-        in_specs=[SMEM, SMEM, VMEM] + [ANY] * count,
-        out_specs=(HBM, VMEM, VMEM),
+        functools.partial(score_kernel, slots, fetch),
+        out_shape=outs + rows_outs,
+        in_specs=[SMEM, SMEM, HBM if fetch else VMEM] + [ANY] * count,
+        out_specs=(HBM, VMEM, VMEM) + (VMEM,) * len(rows_outs),
         scratch_shapes=sizes.panel_scratch(count)
         + [
             sizes.tile_scratch(count),
             pltpu.SemaphoreType.DMA((count,)),
             pltpu.SemaphoreType.DMA((count * sizes.blocks,)),
-        ],
+        ]
+        + rows_scratch,
         compiler_params=pltpu.CompilerParams(vmem_limit_bytes=VMEM_GRANT),
-        cost_estimate=sizes.cost(members, 1),
+        cost_estimate=sizes.cost(slots, 1),
         name="score_group",
     )(order, counts, rows, *pieces)
 
 
-def sum_group(sizes, members, order, counts, rows, tiles, shares):
-    count = 2 * len(members)
+def sum_group(sizes, slots, order, counts, rows, tiles, shares):
+    count = len(slots)
     return pl.pallas_call(
-        functools.partial(sum_kernel, local_slots(members)),
+        functools.partial(sum_kernel, slots),
         out_shape=(sizes.sums,) * count,
         in_specs=[SMEM, SMEM, VMEM, HBM, VMEM],
         out_specs=(ANY,) * count,
@@ -319,16 +352,16 @@
             pltpu.SemaphoreType.DMA((count,)),
         ],
         compiler_params=pltpu.CompilerParams(vmem_limit_bytes=VMEM_GRANT),
-        cost_estimate=sizes.cost(members, 1),
+        cost_estimate=sizes.cost(slots, 1),
         name="sum_group",
     )(order, counts, rows, tiles, shares)
 
 
-def middle_group(sizes, members, order, counts, rows, tops, masses, pieces):
+def middle_group(sizes, slots, order, counts, rows, tops, masses, pieces):
     count = len(pieces)
     earlier = len(tops)
     return pl.pallas_call(
-        functools.partial(middle_kernel, local_slots(members), sizes.listed, earlier),
+        functools.partial(middle_kernel, slots, sizes.listed, earlier),
         out_shape=(jax.ShapeDtypeStruct((sizes.blocks, BLOCK), jnp.float32), sizes.stats)
         + (sizes.sums,) * count,
         in_specs=[SMEM, SMEM, VMEM] + [VMEM] * (2 * earlier) + [ANY] * count,
@@ -342,9 +375,25 @@
         + sizes.sum_scratch(count)
         + [pltpu.SemaphoreType.DMA((count,)), pltpu.SemaphoreType.DMA((count,))],
         compiler_params=pltpu.CompilerParams(vmem_limit_bytes=VMEM_GRANT),
-        cost_estimate=sizes.cost(members, 2),
+        cost_estimate=sizes.cost(slots, 2),
         name="middle_group",
     )(order, counts, rows, *tops, *masses, *pieces)
+
+
+def add_kernel(mine_ref, back_ref, out_ref):
+    out_ref[...] = mine_ref[...] * LINK_SCALE + back_ref[...]
+
+
+def scaled_sum(mine, back):
+    return pl.pallas_call(
+        add_kernel,
+        out_shape=jax.ShapeDtypeStruct(mine.shape, mine.dtype),
+        in_specs=[VMEM, VMEM],
+        out_specs=VMEM,
+        compiler_params=pltpu.CompilerParams(vmem_limit_bytes=VMEM_GRANT),
+        cost_estimate=pl.CostEstimate(flops=30 * 10**9, bytes_accessed=12 * mine.size, transcendentals=0),
+        name="scaled_sum",
+    )(mine, back)
 
 
 def on_device(rows, centroids, lists):
@@ -362,40 +411,53 @@
     for members, stage in zip(groups, stages):
         arriving = [moved(near[source], shift) for _, source, shift in stage]
         pieces = [v for q in members for v in (near[q], other_core(near[q]))]
-        scored = score_group(sizes, members, order, counts, rows, pieces)
+        scored = score_group(
+            sizes, local_slots(members), order, counts, rows, pieces, fetch=not tiles
+        )
         arriving, scored, near = lax.optimization_barrier((arriving, scored, near))
+        if not tiles:
+            rows = scored[3]
         tiles.append(scored[0])
         tops.append(scored[1])
         masses.append(scored[2])
         for (q, _, _), value in zip(stage, arriving):
             near[q] = value
-    members = groups[-1]
-    pieces = [v for q in members for v in (near[q], other_core(near[q]))]
-    log_totals, shares, *sums = middle_group(sizes, members, order, counts, rows, tops, masses, pieces)
+    last = groups[-1]
+    near_slots, far_slots = [2 * q for q in last], [2 * q + 1 for q in last]
+    far = [other_core(near[q]) for q in last]
+    near_tiles, top, mass = score_group(
+        sizes, near_slots, order, counts, rows, [near[q] for q in last], fetch=False
+    )
+    tops.append(top)
+    masses.append(mass)
+    log_totals, shares, *far_sums = middle_group(
+        sizes, far_slots, order, counts, rows, tops, masses, far
+    )
+    near_sums = sum_group(sizes, near_slots, order, counts, rows, near_tiles, shares)
+    mine = dict(zip(last, near_sums))
+    crossed = {q: other_core(v) for q, v in zip(last, far_sums)}
+    total = {q: (mine[q] + crossed[q]) * LINK_SCALE for q in last}
 
     back = {q: [] for members in groups for q in members}
-    sums = {q: pair for q, pair in zip(groups[-1], zip(sums[::2], sums[1::2]))}
-    arriving = []
-    for at in reversed(range(len(groups))):
-        crossed = {q: other_core(theirs) for q, (_, theirs) in sums.items()}
-        ahead = []
-        if at:
-            ahead = sum_group(sizes, groups[at - 1], order, counts, rows, tiles[at - 1], shares)
-        crossed, ahead, arriving, shares = lax.optimization_barrier((crossed, ahead, arriving, shares))
-        if arriving:
-            for value, (_, source, _) in zip(arriving, stages[at]):
-                back[source].append(value)
-        total = {}
-        for q, (mine, _) in sums.items():
-            total[q] = (mine + crossed[q]) * LINK_SCALE
-            for value in back[q]:
-                total[q] = total[q] + value.astype(jnp.float32)
-        if at:
-            arriving = [
-                moved(total[q].astype(jnp.float16), shift if shift is None else -shift)
-                for q, _, shift in stages[at - 1]
-            ]
-            sums = {q: pair for q, pair in zip(groups[at - 1], zip(ahead[::2], ahead[1::2]))}
+    for members, stage in zip(reversed(groups[:-1]), reversed(stages)):
+        leaving = [total[q].astype(jnp.float16) for q, _, _ in stage]
+        leaving, shares = lax.optimization_barrier((leaving, shares))
+        arriving = [
+            moved(value, shift if shift is None else -shift)
+            for value, (_, _, shift) in zip(leaving, stage)
+        ]
+        at = groups.index(members)
+        sums = sum_group(sizes, local_slots(members), order, counts, rows, tiles[at], shares)
+        crossed = {q: other_core(v) for q, v in zip(members, sums[1::2])}
+        arriving = lax.optimization_barrier(arriving)
+        for value, (_, source, _) in zip(arriving, stage):
+            back[source].append(value.astype(jnp.float32))
+        for q, near_sum in zip(members, sums[::2]):
+            if back[q]:
+                part = scaled_sum(near_sum, functools.reduce(jnp.add, back[q]))
+            else:
+                part = near_sum * LINK_SCALE
+            total[q] = part + crossed[q] * LINK_SCALE
     own_sums = total[own] * (1.0 / LINK_SCALE)
     updated = (own_sums[:cent] + PRIOR_MASS * centroids.astype(jnp.float32)) / (
         own_sums[cent, :cent][:, None] + PRIOR_MASS

time: 118 us -> 113 us (0.958)
  the two profiles are of different devices: /device:TPU:6 before, /device:TPU:0 now
where the time goes in v2:
time: 113 us; the launch traced here: 115 us
  Pallas kernels  61.6 us (55%)
  starting transfers between devices  26 us (23%)
  waiting for transfers between devices  21 us (19%)
  other arithmetic  3.55 us (3%)
  local copies, waits for them, and re-layouts  2.4 us (2%)
    pallas_call x4, Pallas kernels, score_group(): pl.pallas_call(functools.partial(score_kernel, slots, fetch), out_shape=o...  28.7 us
    pallas_call x4, Pallas kernels, sum_group(): pl.pallas_call(functools.partial(sum_kernel, slots), out_shape=(sizes.sum...  25.1 us
    ppermute x6, starting transfers between devices, moved(): return lax.ppermute(value, 'blk', [(i, i ^ 2) for i in range(count)])  12 us
    ppermute x6, waiting for transfers between devices, moved(): lax.ppermute(value, 'blk', [(i, (i + shift) % count) for i in range(count)])  11.7 us
    ppermute x6, starting transfers between devices, moved(): lax.ppermute(value, 'blk', [(i, (i + shift) % count) for i in range(count)])  10 us
    pallas_call x1, Pallas kernels, middle_group(): pl.pallas_call(functools.partial(middle_kernel, slots, sizes.listed, earl...  7.34 us
    ppermute x6, waiting for transfers between devices, moved(): return lax.ppermute(value, 'blk', [(i, i ^ 2) for i in range(count)])  4.9 us
    ppermute x14, waiting for transfers between devices, other_core(): return lax.ppermute(value, 'blk', [(i, i ^ 1) for i in range(count)])  4.46 us
  transfers between devices with their start and end apart: 26, of which 9 were waited for; matrix products, arithmetic and copies ran while one was open for 2% of the time, Pallas kernels for 47%

profile of v2, /device:TPU:0, one launch (start us, length us, event | category | flops | bytes accessed | tf_op | source)
XLA Modules:
  0.0 115.5 jit_solution(16190014700396400167)
XLA Ops:
  0.6 0.5 collective-permute-start.2
  1.1 2.6 %collective-permute-start.1 = (bf16[256,768]{1,0:T(8,128)(2,1)}, bf16[256,768]{1,0:T(8,128)(2,1)S(1)}, u32[]{:S(2)}, u32[]{:S(2)}) collective-permute-start(bf16[256,768]{1,0:T(8,128)(2,1)} %refs_0_.1), channel_id=1, source_target_pairs={{0,2},{1,3},{2,0},{3,1},{4,6},{5,7},{6,4},{7,5},{8,10},{9,11},{10,... | collective-permute-start | bytes 1179656 | tf_op jit(solution)/shard_map/ppermute | solution.py:49
  3.7 1.6 %collective-permute-start = (bf16[256,768]{1,0:T(8,128)(2,1)}, bf16[256,768]{1,0:T(8,128)(2,1)S(1)}, u32[]{:S(2)}, u32[]{:S(2)}) collective-permute-start(bf16[256,768]{1,0:T(8,128)(2,1)} %refs_0_.1), channel_id=1, source_target_pairs={{0,4},{1,5},{2,6},{3,7},{4,8},{5,9},{6,10},{7,11},{8,12},{9,13},{1... | collective-permute-start | bytes 1179656 | tf_op jit(solution)/shard_map/ppermute | solution.py:50
  5.3 0.7 fusion.9
  6.7 1.0 copy-done
  7.7 7.8 %score_group.4 = (f32[64,256,256]{2,1,0:T(8,128)}, f32[96,256]{1,0:T(8,128)S(1)}, f32[96,256]{1,0:T(8,128)S(1)}, bf16[4096,768]{1,0:T(8,128)(2,1)S(1)}) custom-call(s32[256]{0:T(256)S(1)} %reshape.57.order_ref, s32[16]{0:T(128)S(1)} %convert_reduce_fusion.counts_ref, bf16[4096,768]{1,0:T(8,128)(2,1)} %rows_ref.1, bf16[256,768]{1,0:T(8,128)(2,1)S(1)} %copy-done, ...), custom_call_target="tpu_custom_call" | custom-call | flops 1380525184 | bytes 9886573 | tf_op jit(solution)/shard_map/score_group/pallas_call | solution.py:323
  15.5 1.5 %collective-permute-done.refs_0_ = bf16[256,768]{1,0:T(8,128)(2,1)S(1)} collective-permute-done((bf16[256,768]{1,0:T(8,128)(2,1)}, bf16[256,768]{1,0:T(8,128)(2,1)S(1)}, u32[]{:S(2)}, u32[]{:S(2)}) %collective-permute-start) | collective-permute-done | bytes 393248 | tf_op jit(solution)/shard_map/ppermute | solution.py:50
  17.0 0.5 collective-permute-start.5
  17.5 2.7 %collective-permute-start.3 = (bf16[256,768]{1,0:T(8,128)(2,1)S(1)}, bf16[256,768]{1,0:T(8,128)(2,1)S(1)}, u32[]{:S(2)}, u32[]{:S(2)}) collective-permute-start(bf16[256,768]{1,0:T(8,128)(2,1)S(1)} %copy-done), channel_id=1, source_target_pairs={{0,12},{1,13},{2,14},{3,15},{4,0},{5,1},{6,2},{7,3},{8,4},{9,5},{1... | collective-permute-start | bytes 1179656 | tf_op jit(solution)/shard_map/ppermute | solution.py:50
  20.3 12.4 %score_group.5 = (f32[64,256,256]{2,1,0:T(8,128)}, f32[96,256]{1,0:T(8,128)S(1)}, f32[96,256]{1,0:T(8,128)S(1)}) custom-call(s32[256]{0:T(256)S(1)} %reshape.57.order_ref, s32[16]{0:T(128)S(1)} %convert_reduce_fusion.counts_ref, bf16[4096,768]{1,0:T(8,128)(2,1)S(1)} %get-tuple-element.67.rows_ref.x, bf16[256,768]{1,0:T(8,128)(2,1)S(1)} %collective-permute-done.refs_0_, ...), custom_call_target="tpu_custom_call" | custom-call | flops 2761050368 | bytes 13481691 | tf_op jit(solution)/shard_map/score_group/pallas_call | solution.py:323
  33.2 1.2 %collective-permute-done.10.refs_3_ = bf16[256,768]{1,0:T(8,128)(2,1)S(1)} collective-permute-done((bf16[256,768]{1,0:T(8,128)(2,1)S(1)}, bf16[256,768]{1,0:T(8,128)(2,1)S(1)}, u32[]{:S(2)}, u32[]{:S(2)}) %collective-permute-start.10) | collective-permute-done | bytes 393248 | tf_op jit(solution)/shard_map/ppermute | solution.py:55
  34.4 0.6 collective-permute-done.9.refs_1_
  35.0 4.7 %score_group.6 = (f32[64,256,256]{2,1,0:T(8,128)}, f32[96,256]{1,0:T(8,128)S(1)}, f32[96,256]{1,0:T(8,128)S(1)}) custom-call(s32[256]{0:T(256)S(1)} %reshape.57.order_ref, s32[16]{0:T(128)S(1)} %convert_reduce_fusion.counts_ref, bf16[4096,768]{1,0:T(8,128)(2,1)S(1)} %get-tuple-element.67.rows_ref.x, bf16[256,768]{1,0:T(8,128)(2,1)S(1)} %collective-permute-done.3.refs_0_, ...), custom_call_target="tpu_custom_call" | custom-call | flops 2761050368 | bytes 13481691 | tf_op jit(solution)/shard_map/score_group/pallas_call | solution.py:323
  39.8 6.4 %collective-permute-done.7.refs_0_ = bf16[256,768]{1,0:T(8,128)(2,1)S(1)} collective-permute-done((bf16[256,768]{1,0:T(8,128)(2,1)S(1)}, bf16[256,768]{1,0:T(8,128)(2,1)S(1)}, u32[]{:S(2)}, u32[]{:S(2)}) %collective-permute-start.7) | collective-permute-done | bytes 393248 | tf_op jit(solution)/shard_map/ppermute | solution.py:50
  46.1 0.5 collective-permute-start.12
  46.6 3.8 %score_group.7 = (f32[64,256,256]{2,1,0:T(8,128)}, f32[96,256]{1,0:T(8,128)S(1)}, f32[96,256]{1,0:T(8,128)S(1)}) custom-call(s32[256]{0:T(256)S(1)} %reshape.57.order_ref, s32[16]{0:T(128)S(1)} %convert_reduce_fusion.counts_ref, bf16[4096,768]{1,0:T(8,128)(2,1)S(1)} %get-tuple-element.67.rows_ref.x, bf16[256,768]{1,0:T(8,128)(2,1)S(1)} %collective-permute-done.7.refs_0_, ...), custom_call_target="tpu_custom_call" | custom-call | flops 1380525184 | bytes 9886573 | tf_op jit(solution)/shard_map/score_group/pallas_call | solution.py:323
  50.5 7.3 %middle_group.1 = (f32[16,256]{1,0:T(8,128)S(1)}, f32[96,256]{1,0:T(8,128)S(1)}, f32[264,768]{1,0:T(8,128)S(1)}, f32[264,768]{1,0:T(8,128)S(1)}) custom-call(s32[256]{0:T(256)S(1)} %reshape.57.order_ref, s32[16]{0:T(128)S(1)} %convert_reduce_fusion.counts_ref, bf16[4096,768]{1,0:T(8,128)(2,1)S(1)} %get-tuple-element.67.rows_ref.x, ...), custom_call_target="tpu_custom_call" | custom-call | flops 2761050368 | bytes 9886573 | tf_op jit(solution)/shard_map/middle_group/pallas_call | solution.py:363
  58.4 3.5 %sum_group.4 = (f32[264,768]{1,0:T(8,128)S(1)}, f32[264,768]{1,0:T(8,128)S(1)}) custom-call(s32[256]{0:T(256)S(1)} %reshape.57.order_ref, s32[16]{0:T(128)S(1)} %convert_reduce_fusion.counts_ref, bf16[4096,768]{1,0:T(8,128)(2,1)S(1)} %get-tuple-element.67.rows_ref.x, f32[64,256,256]{2,1,0:T(8,128)} %get-tuple-element.84.tiles_ref, ...), custom_call_target="tpu_custom_call" | custom-call | flops 1380525184 | bytes 9886573 | tf_op jit(solution)/shard_map/sum_group/pallas_call | solution.py:343
  62.3 5.6 %collective-permute-start.15 = (f16[264,768]{1,0:T(8,128)(2,1)S(1)}, f16[264,768]{1,0:T(8,128)(2,1)S(1)}, u32[]{:S(2)}, u32[]{:S(2)}) collective-permute-start(f16[264,768]{1,0:T(8,128)(2,1)S(1)} %multiply_convert_fusion.2), channel_id=1, source_target_pairs={{0,12},{1,13},{2,14},{3,15},{4,0},{5,1},{6,2},{7,3},{8,4},{9,5},{1... | collective-permute-start | bytes 1216520 | tf_op jit(solution)/shard_map/ppermute | solution.py:50
  67.9 4.7 %sum_group.5 = (f32[264,768]{1,0:T(8,128)S(1)}, f32[264,768]{1,0:T(8,128)S(1)}, f32[264,768]{1,0:T(8,128)S(1)}, f32[264,768]{1,0:T(8,128)S(1)}) custom-call(s32[256]{0:T(256)S(1)} %reshape.57.order_ref, s32[16]{0:T(128)S(1)} %convert_reduce_fusion.counts_ref, bf16[4096,768]{1,0:T(8,128)(2,1)S(1)} %get-tuple-element.67.rows_ref.x, ...), custom_call_target="tpu_custom_call" | custom-call | flops 2761050368 | bytes 13481691 | tf_op jit(solution)/shard_map/sum_group/pallas_call | solution.py:343
  73.2 3.8 %collective-permute-done.15 = f16[264,768]{1,0:T(8,128)(2,1)S(1)} collective-permute-done((f16[264,768]{1,0:T(8,128)(2,1)S(1)}, f16[264,768]{1,0:T(8,128)(2,1)S(1)}, u32[]{:S(2)}, u32[]{:S(2)}) %collective-permute-start.15) | collective-permute-done | bytes 405536 | tf_op jit(solution)/shard_map/ppermute | solution.py:50
  76.9 2.2 %collective-permute-done.16 = f16[264,768]{1,0:T(8,128)(2,1)S(1)} collective-permute-done((f16[264,768]{1,0:T(8,128)(2,1)S(1)}, f16[264,768]{1,0:T(8,128)(2,1)S(1)}, u32[]{:S(2)}, u32[]{:S(2)}) %collective-permute-start.16) | collective-permute-done | bytes 405536 | tf_op jit(solution)/shard_map/ppermute | solution.py:49
  79.8 4.6 %collective-permute-start.20 = (f16[264,768]{1,0:T(8,128)(2,1)S(1)}, f16[264,768]{1,0:T(8,128)(2,1)S(1)}, u32[]{:S(2)}, u32[]{:S(2)}) collective-permute-start(f16[264,768]{1,0:T(8,128)(2,1)S(1)} %add_convert_fusion.1), channel_id=1, source_target_pairs={{0,2},{1,3},{2,0},{3,1},{4,6},{5,7},{6,4},{7,5},{8,10},{9,11},{10,... | collective-permute-start | bytes 1216520 | tf_op jit(solution)/shard_map/ppermute | solution.py:49
  84.4 10.9 %sum_group.6 = (f32[264,768]{1,0:T(8,128)S(1)}, f32[264,768]{1,0:T(8,128)S(1)}, f32[264,768]{1,0:T(8,128)S(1)}, f32[264,768]{1,0:T(8,128)S(1)}) custom-call(s32[256]{0:T(256)S(1)} %reshape.57.order_ref, s32[16]{0:T(128)S(1)} %convert_reduce_fusion.counts_ref, bf16[4096,768]{1,0:T(8,128)(2,1)S(1)} %get-tuple-element.67.rows_ref.x, ...), custom_call_target="tpu_custom_call" | custom-call | flops 2761050368 | bytes 13481691 | tf_op jit(solution)/shard_map/sum_group/pallas_call | solution.py:343
  96.1 1.6 %collective-permute-done.21 = f32[264,768]{1,0:T(8,128)S(1)} collective-permute-done((f32[264,768]{1,0:T(8,128)S(1)}, f32[264,768]{1,0:T(8,128)S(1)}, u32[]{:S(2)}, u32[]{:S(2)}) %collective-permute-start.21) | collective-permute-done | bytes 811040 | tf_op jit(solution)/shard_map/ppermute | solution.py:55
  97.8 1.0 collective-permute-done.22
  99.1 4.8 %collective-permute-start.24 = (f16[264,768]{1,0:T(8,128)(2,1)S(1)}, f16[264,768]{1,0:T(8,128)(2,1)S(1)}, u32[]{:S(2)}, u32[]{:S(2)}) collective-permute-start(f16[264,768]{1,0:T(8,128)(2,1)S(1)} %multiply_convert_fusion), channel_id=1, source_target_pairs={{0,2},{1,3},{2,0},{3,1},{4,6},{5,7},{6,4},{7,5},{8,10},{9,11},{10,... | collective-permute-start | bytes 1216520 | tf_op jit(solution)/shard_map/ppermute | solution.py:49
  103.9 0.6 copy.6
  104.5 6.0 %sum_group.7 = (f32[264,768]{1,0:T(8,128)S(1)}, f32[264,768]{1,0:T(8,128)S(1)}) custom-call(s32[256]{0:T(256)S(1)} %reshape.57.order_ref, s32[16]{0:T(128)S(1)} %convert_reduce_fusion.counts_ref, bf16[4096,768]{1,0:T(8,128)(2,1)S(1)} %get-tuple-element.67.rows_ref.x, f32[64,256,256]{2,1,0:T(8,128)} %get-tuple-element.68.tiles_ref, ...), custom_call_target="tpu_custom_call" | custom-call | flops 1380525184 | bytes 9886573 | tf_op jit(solution)/shard_map/sum_group/pallas_call | solution.py:343
  110.6 2.7 %collective-permute-done.24 = f16[264,768]{1,0:T(8,128)(2,1)S(1)} collective-permute-done((f16[264,768]{1,0:T(8,128)(2,1)S(1)}, f16[264,768]{1,0:T(8,128)(2,1)S(1)}, u32[]{:S(2)}, u32[]{:S(2)}) %collective-permute-start.24) | collective-permute-done | bytes 405536 | tf_op jit(solution)/shard_map/ppermute | solution.py:49
  113.8 0.7 copy-done.1
  114.5 1.0 fusion
  (61 shorter events, 4.9 us)
Async XLA Ops:
  0.6 6.1 %collective-permute-start.2 = (bf16[256,768]{1,0:T(8,128)(2,1)}, bf16[256,768]{1,0:T(8,128)(2,1)S(1)}, u32[]{:S(2)}, u32[]{:S(2)}) collective-permute-start(bf16[256,768]{1,0:T(8,128)(2,1)} %refs_0_.1), channel_id=1, source_target_pairs={{0,1},{1,0},{2,3},{3,2},{4,5},{5,4},{6,7},{7,6},{8,9},{9,8},{10,11... | collective-permute-start | bytes 1179656 | tf_op jit(solution)/shard_map/ppermute | solution.py:55
  1.1 14.3 %collective-permute-start.1 = (bf16[256,768]{1,0:T(8,128)(2,1)}, bf16[256,768]{1,0:T(8,128)(2,1)S(1)}, u32[]{:S(2)}, u32[]{:S(2)}) collective-permute-start(bf16[256,768]{1,0:T(8,128)(2,1)} %refs_0_.1), channel_id=1, source_target_pairs={{0,2},{1,3},{2,0},{3,1},{4,6},{5,7},{6,4},{7,5},{8,10},{9,11},{10,... | collective-permute-start | bytes 1179656 | tf_op jit(solution)/shard_map/ppermute | solution.py:49
  3.7 13.3 %collective-permute-start = (bf16[256,768]{1,0:T(8,128)(2,1)}, bf16[256,768]{1,0:T(8,128)(2,1)S(1)}, u32[]{:S(2)}, u32[]{:S(2)}) collective-permute-start(bf16[256,768]{1,0:T(8,128)(2,1)} %refs_0_.1), channel_id=1, source_target_pairs={{0,4},{1,5},{2,6},{3,7},{4,8},{5,9},{6,10},{7,11},{8,12},{9,13},{1... | collective-permute-start | bytes 1179656 | tf_op jit(solution)/shard_map/ppermute | solution.py:50
  6.7 1.0 copy-start
  17.0 3.2 %collective-permute-start.6 = (bf16[256,768]{1,0:T(8,128)(2,1)S(1)}, bf16[256,768]{1,0:T(8,128)(2,1)S(1)}, u32[]{:S(2)}, u32[]{:S(2)}) collective-permute-start(bf16[256,768]{1,0:T(8,128)(2,1)S(1)} %collective-permute-done.1.refs_2_), channel_id=1, source_target_pairs={{0,1},{1,0},{2,3},{3,2},{4,5},{5,4},{6,7},{7,6},{8,9},{9,8},{10,11... | collective-permute-start | bytes 1179656 | tf_op jit(solution)/shard_map/ppermute | solution.py:55
  17.0 3.2 %collective-permute-start.5 = (bf16[256,768]{1,0:T(8,128)(2,1)S(1)}, bf16[256,768]{1,0:T(8,128)(2,1)S(1)}, u32[]{:S(2)}, u32[]{:S(2)}) collective-permute-start(bf16[256,768]{1,0:T(8,128)(2,1)S(1)} %collective-permute-done.refs_0_), channel_id=1, source_target_pairs={{0,1},{1,0},{2,3},{3,2},{4,5},{5,4},{6,7},{7,6},{8,9},{9,8},{10,11... | collective-permute-start | bytes 1179656 | tf_op jit(solution)/shard_map/ppermute | solution.py:55
  17.5 15.1 %collective-permute-start.3 = (bf16[256,768]{1,0:T(8,128)(2,1)S(1)}, bf16[256,768]{1,0:T(8,128)(2,1)S(1)}, u32[]{:S(2)}, u32[]{:S(2)}) collective-permute-start(bf16[256,768]{1,0:T(8,128)(2,1)S(1)} %copy-done), channel_id=1, source_target_pairs={{0,12},{1,13},{2,14},{3,15},{4,0},{5,1},{6,2},{7,3},{8,4},{9,5},{1... | collective-permute-start | bytes 1179656 | tf_op jit(solution)/shard_map/ppermute | solution.py:50
  20.3 12.4 %collective-permute-start.4 = (bf16[256,768]{1,0:T(8,128)(2,1)S(1)}, bf16[256,768]{1,0:T(8,128)(2,1)S(1)}, u32[]{:S(2)}, u32[]{:S(2)}) collective-permute-start(bf16[256,768]{1,0:T(8,128)(2,1)S(1)} %collective-permute-done.refs_0_), channel_id=1, source_target_pairs={{0,2},{1,3},{2,0},{3,1},{4,6},{5,7},{6,4},{7,5},{8,10},{9,11},{10,... | collective-permute-start | bytes 1179656 | tf_op jit(solution)/shard_map/ppermute | solution.py:49
  32.7 1.8 %collective-permute-start.10 = (bf16[256,768]{1,0:T(8,128)(2,1)S(1)}, bf16[256,768]{1,0:T(8,128)(2,1)S(1)}, u32[]{:S(2)}, u32[]{:S(2)}) collective-permute-start(bf16[256,768]{1,0:T(8,128)(2,1)S(1)} %collective-permute-done.4.refs_2_), channel_id=1, source_target_pairs={{0,1},{1,0},{2,3},{3,2},{4,5},{5,4},{6,7},{7,6},{8,9},{9,8},{10,11... | collective-permute-start | bytes 1179656 | tf_op jit(solution)/shard_map/ppermute | solution.py:55
  32.7 2.3 %collective-permute-start.9 = (bf16[256,768]{1,0:T(8,128)(2,1)S(1)}, bf16[256,768]{1,0:T(8,128)(2,1)S(1)}, u32[]{:S(2)}, u32[]{:S(2)}) collective-permute-start(bf16[256,768]{1,0:T(8,128)(2,1)S(1)} %collective-permute-done.3.refs_0_), channel_id=1, source_target_pairs={{0,1},{1,0},{2,3},{3,2},{4,5},{5,4},{6,7},{7,6},{8,9},{9,8},{10,11... | collective-permute-start | bytes 1179656 | tf_op jit(solution)/shard_map/ppermute | solution.py:55
  33.2 12.9 %collective-permute-start.7 = (bf16[256,768]{1,0:T(8,128)(2,1)S(1)}, bf16[256,768]{1,0:T(8,128)(2,1)S(1)}, u32[]{:S(2)}, u32[]{:S(2)}) collective-permute-start(bf16[256,768]{1,0:T(8,128)(2,1)S(1)} %collective-permute-done.4.refs_2_), channel_id=1, source_target_pairs={{0,4},{1,5},{2,6},{3,7},{4,8},{5,9},{6,10},{7,11},{8,12},{9,13},{1... | collective-permute-start | bytes 1179656 | tf_op jit(solution)/shard_map/ppermute | solution.py:50
  33.2 12.9 %collective-permute-start.8 = (bf16[256,768]{1,0:T(8,128)(2,1)S(1)}, bf16[256,768]{1,0:T(8,128)(2,1)S(1)}, u32[]{:S(2)}, u32[]{:S(2)}) collective-permute-start(bf16[256,768]{1,0:T(8,128)(2,1)S(1)} %collective-permute-done.3.refs_0_), channel_id=1, source_target_pairs={{0,2},{1,3},{2,0},{3,1},{4,6},{5,7},{6,4},{7,5},{8,10},{9,11},{10,... | collective-permute-start | bytes 1179656 | tf_op jit(solution)/shard_map/ppermute | solution.py:49
  46.1 4.3 %collective-permute-start.11 = (bf16[256,768]{1,0:T(8,128)(2,1)S(1)}, bf16[256,768]{1,0:T(8,128)(2,1)S(1)}, u32[]{:S(2)}, u32[]{:S(2)}) collective-permute-start(bf16[256,768]{1,0:T(8,128)(2,1)S(1)} %collective-permute-done.7.refs_0_), channel_id=1, source_target_pairs={{0,1},{1,0},{2,3},{3,2},{4,5},{5,4},{6,7},{7,6},{8,9},{9,8},{10,11... | collective-permute-start | bytes 1179656 | tf_op jit(solution)/shard_map/ppermute | solution.py:55
  46.1 4.3 %collective-permute-start.12 = (bf16[256,768]{1,0:T(8,128)(2,1)S(1)}, bf16[256,768]{1,0:T(8,128)(2,1)S(1)}, u32[]{:S(2)}, u32[]{:S(2)}) collective-permute-start(bf16[256,768]{1,0:T(8,128)(2,1)S(1)} %collective-permute-done.8.refs_1_), channel_id=1, source_target_pairs={{0,1},{1,0},{2,3},{3,2},{4,5},{5,4},{6,7},{7,6},{8,9},{9,8},{10,11... | collective-permute-start | bytes 1179656 | tf_op jit(solution)/shard_map/ppermute | solution.py:55
  57.8 4.1 %collective-permute-start.13 = (f32[264,768]{1,0:T(8,128)S(1)}, f32[264,768]{1,0:T(8,128)S(1)}, u32[]{:S(2)}, u32[]{:S(2)}) collective-permute-start(f32[264,768]{1,0:T(8,128)S(1)} %get-tuple-element.95), channel_id=1, source_target_pairs={{0,1},{1,0},{2,3},{3,2},{4,5},{5,4},{6,7},{7,6},{8,9},{9,8},{10,11... | collective-permute-start | bytes 2433032 | tf_op jit(solution)/shard_map/ppermute | solution.py:55
  57.9 4.2 %collective-permute-start.14 = (f32[264,768]{1,0:T(8,128)S(1)}, f32[264,768]{1,0:T(8,128)S(1)}, u32[]{:S(2)}, u32[]{:S(2)}) collective-permute-start(f32[264,768]{1,0:T(8,128)S(1)} %get-tuple-element.97), channel_id=1, source_target_pairs={{0,1},{1,0},{2,3},{3,2},{4,5},{5,4},{6,7},{7,6},{8,9},{9,8},{10,11... | collective-permute-start | bytes 2433032 | tf_op jit(solution)/shard_map/ppermute | solution.py:55
  62.3 14.7 %collective-permute-start.15 = (f16[264,768]{1,0:T(8,128)(2,1)S(1)}, f16[264,768]{1,0:T(8,128)(2,1)S(1)}, u32[]{:S(2)}, u32[]{:S(2)}) collective-permute-start(f16[264,768]{1,0:T(8,128)(2,1)S(1)} %multiply_convert_fusion.2), channel_id=1, source_target_pairs={{0,12},{1,13},{2,14},{3,15},{4,0},{5,1},{6,2},{7,3},{8,4},{9,5},{1... | collective-permute-start | bytes 1216520 | tf_op jit(solution)/shard_map/ppermute | solution.py:50
  67.9 11.2 %collective-permute-start.16 = (f16[264,768]{1,0:T(8,128)(2,1)S(1)}, f16[264,768]{1,0:T(8,128)(2,1)S(1)}, u32[]{:S(2)}, u32[]{:S(2)}) collective-permute-start(f16[264,768]{1,0:T(8,128)(2,1)S(1)} %multiply_convert_fusion.1), channel_id=1, source_target_pairs={{0,2},{1,3},{2,0},{3,1},{4,6},{5,7},{6,4},{7,5},{8,10},{9,11},{10,... | collective-permute-start | bytes 1216520 | tf_op jit(solution)/shard_map/ppermute | solution.py:49
  72.6 6.9 %collective-permute-start.17 = (f32[264,768]{1,0:T(8,128)S(1)}, f32[264,768]{1,0:T(8,128)S(1)}, u32[]{:S(2)}, u32[]{:S(2)}) collective-permute-start(f32[264,768]{1,0:T(8,128)S(1)} %get-tuple-element.103), channel_id=1, source_target_pairs={{0,1},{1,0},{2,3},{3,2},{4,5},{5,4},{6,7},{7,6},{8,9},{9,8},{10,11... | collective-permute-start | bytes 2433032 | tf_op jit(solution)/shard_map/ppermute | solution.py:55
  72.7 6.9 %collective-permute-start.18 = (f32[264,768]{1,0:T(8,128)S(1)}, f32[264,768]{1,0:T(8,128)S(1)}, u32[]{:S(2)}, u32[]{:S(2)}) collective-permute-start(f32[264,768]{1,0:T(8,128)S(1)} %get-tuple-element.106), channel_id=1, source_target_pairs={{0,1},{1,0},{2,3},{3,2},{4,5},{5,4},{6,7},{7,6},{8,9},{9,8},{10,11... | collective-permute-start | bytes 2433032 | tf_op jit(solution)/shard_map/ppermute | solution.py:55
  79.7 16.2 %collective-permute-start.19 = (f16[264,768]{1,0:T(8,128)(2,1)S(1)}, f16[264,768]{1,0:T(8,128)(2,1)S(1)}, u32[]{:S(2)}, u32[]{:S(2)}) collective-permute-start(f16[264,768]{1,0:T(8,128)(2,1)S(1)} %add_convert_fusion.2), channel_id=1, source_target_pairs={{0,4},{1,5},{2,6},{3,7},{4,8},{5,9},{6,10},{7,11},{8,12},{9,13},{1... | collective-permute-start | bytes 1216520 | tf_op jit(solution)/shard_map/ppermute | solution.py:50
  79.8 16.1 %collective-permute-start.20 = (f16[264,768]{1,0:T(8,128)(2,1)S(1)}, f16[264,768]{1,0:T(8,128)(2,1)S(1)}, u32[]{:S(2)}, u32[]{:S(2)}) collective-permute-start(f16[264,768]{1,0:T(8,128)(2,1)S(1)} %add_convert_fusion.1), channel_id=1, source_target_pairs={{0,2},{1,3},{2,0},{3,1},{4,6},{5,7},{6,4},{7,5},{8,10},{9,11},{10,... | collective-permute-start | bytes 1216520 | tf_op jit(solution)/shard_map/ppermute | solution.py:49
  95.3 2.4 %collective-permute-start.21 = (f32[264,768]{1,0:T(8,128)S(1)}, f32[264,768]{1,0:T(8,128)S(1)}, u32[]{:S(2)}, u32[]{:S(2)}) collective-permute-start(f32[264,768]{1,0:T(8,128)S(1)} %get-tuple-element.112), channel_id=1, source_target_pairs={{0,1},{1,0},{2,3},{3,2},{4,5},{5,4},{6,7},{7,6},{8,9},{9,8},{10,11... | collective-permute-start | bytes 2433032 | tf_op jit(solution)/shard_map/ppermute | solution.py:55
  95.4 3.5 %collective-permute-start.22 = (f32[264,768]{1,0:T(8,128)S(1)}, f32[264,768]{1,0:T(8,128)S(1)}, u32[]{:S(2)}, u32[]{:S(2)}) collective-permute-start(f32[264,768]{1,0:T(8,128)S(1)} %get-tuple-element.114), channel_id=1, source_target_pairs={{0,1},{1,0},{2,3},{3,2},{4,5},{5,4},{6,7},{7,6},{8,9},{9,8},{10,11... | collective-permute-start | bytes 2433032 | tf_op jit(solution)/shard_map/ppermute | solution.py:55
  99.0 11.6 %collective-permute-start.23 = (f16[264,768]{1,0:T(8,128)(2,1)S(1)}, f16[264,768]{1,0:T(8,128)(2,1)S(1)}, u32[]{:S(2)}, u32[]{:S(2)}) collective-permute-start(f16[264,768]{1,0:T(8,128)(2,1)S(1)} %add_convert_fusion), channel_id=1, source_target_pairs={{0,12},{1,13},{2,14},{3,15},{4,0},{5,1},{6,2},{7,3},{8,4},{9,5},{1... | collective-permute-start | bytes 1216520 | tf_op jit(solution)/shard_map/ppermute | solution.py:50
  99.1 14.2 %collective-permute-start.24 = (f16[264,768]{1,0:T(8,128)(2,1)S(1)}, f16[264,768]{1,0:T(8,128)(2,1)S(1)}, u32[]{:S(2)}, u32[]{:S(2)}) collective-permute-start(f16[264,768]{1,0:T(8,128)(2,1)S(1)} %multiply_convert_fusion), channel_id=1, source_target_pairs={{0,2},{1,3},{2,0},{3,1},{4,6},{5,7},{6,4},{7,5},{8,10},{9,11},{10,... | collective-permute-start | bytes 1216520 | tf_op jit(solution)/shard_map/ppermute | solution.py:49
  110.5 3.1 %collective-permute-start.25 = (f32[264,768]{1,0:T(8,128)S(1)}, f32[264,768]{1,0:T(8,128)S(1)}, u32[]{:S(2)}, u32[]{:S(2)}) collective-permute-start(f32[264,768]{1,0:T(8,128)S(1)} %get-tuple-element.122), channel_id=1, source_target_pairs={{0,1},{1,0},{2,3},{3,2},{4,5},{5,4},{6,7},{7,6},{8,9},{9,8},{10,11... | collective-permute-start | bytes 2433032 | tf_op jit(solution)/shard_map/ppermute | solution.py:55
  113.5 1.0 copy-start.1

commit v3 on v2

--- a/solution.py
+++ b/solution.py
@@ -91,22 +91,11 @@
     return x[pl.ds(pl.multiple_of(block * BLOCK, BLOCK), BLOCK)]
 
 
-def load_panels(piece_refs, panels, norms, sem):
-    copies = [
-        pltpu.make_async_copy(ref, panels.at[p], sem.at[p]) for p, ref in enumerate(piece_refs)
-    ]
-    for copy in copies:
-        copy.start()
-
-    def finish():
-        for copy in copies:
-            copy.wait()
-        for p in range(len(copies)):
-            wide = panels[p].astype(jnp.float32)
-            norm = jnp.sum(wide * wide, axis=1, keepdims=True)
-            norms[p] = jnp.broadcast_to(norm * (0.5 * LOGIT_SCALE * LOG2E), norms.shape[1:])
-
-    return finish
+def find_norms(panels, norms):
+    for p, panel in enumerate(panels):
+        wide = panel[...].astype(jnp.float32)
+        norm = jnp.sum(wide * wide, axis=1, keepdims=True)
+        norms[p] = jnp.broadcast_to(norm * (0.5 * LOGIT_SCALE * LOG2E), norms.shape[1:])
 
 
 def tile_of(panel, norm, block):
@@ -130,7 +119,7 @@
         def some(first, number):
             work = some_pairs(order_ref, counts_ref, slot, blocks, first, number)
             here(work[-1][1])
-            found = [tile_of(panels[p], norms[p], rows_of(x, b)) for _, b, _ in work]
+            found = [tile_of(panels[p][...], norms[p], rows_of(x, b)) for _, b, _ in work]
             for (i, _, at), (powers, top, mass) in zip(work, found):
                 tiles[p * blocks + i] = powers
                 tops[pl.ds(at, 1)] = top
@@ -162,26 +151,22 @@
                 partial = product if partial is None else partial + product
                 count = wide if count is None else count + wide
             totals[p] += count
-            acc[p, pl.ds(0, cent)] += partial
+            acc[p][pl.ds(0, cent)] += partial
 
         by_fours(counts_ref[slot], some)
 
 
 def clear_sums(acc, totals):
-    acc[...] = jnp.zeros_like(acc)
+    for ref in acc:
+        ref[...] = jnp.zeros_like(ref)
     totals[...] = jnp.zeros_like(totals)
 
 
-def store_sums(acc, totals, out_refs, sem):
+def store_totals(acc, totals):
     cent = totals.shape[1]
-    copies = []
-    for p, ref in enumerate(out_refs):
+    for p, ref in enumerate(acc):
         row = jnp.sum(totals[p].T, axis=0, keepdims=True)
-        acc[p, pl.ds(cent, EXTRA), pl.ds(0, cent)] = jnp.broadcast_to(row, (EXTRA, cent))
-        copies.append(pltpu.make_async_copy(acc.at[p], ref, sem.at[p]))
-        copies[-1].start()
-    for copy in copies:
-        copy.wait()
+        ref[pl.ds(cent, EXTRA), pl.ds(0, cent)] = jnp.broadcast_to(row, (EXTRA, cent))
 
 
 def over_tiles(slots, counts_ref, blocks, act):
@@ -196,12 +181,11 @@
     tiles_ref, tops, masses = refs[pieces : pieces + 3]
     refs = refs[pieces + 3 :]
     x = refs[0] if fetch else rows_ref
-    panels, norms, tiles, panel_sem, tile_sem = refs[1:6] if fetch else refs[:5]
+    norms, tiles, tile_sem = refs[1:4] if fetch else refs[:3]
     blocks = x.shape[0] // BLOCK
-    finish_panels = load_panels(piece_refs, panels, norms, panel_sem)
     here = lambda b: None
     if fetch:
-        row_sem, fetched = refs[6:]
+        row_sem, fetched = refs[4:]
 
         def bring(b):
             span = pl.ds(pl.multiple_of(b * BLOCK, BLOCK), BLOCK)
@@ -216,13 +200,13 @@
             lax.fori_loop(first, b + 1, lambda k, _: (bring(k).wait(), 0)[1], 0)
             fetched[0] = jnp.maximum(first, b + 1)
 
-    finish_panels()
+    find_norms(piece_refs, norms)
 
     def outgoing(j):
         return pltpu.make_async_copy(tiles.at[j], tiles_ref.at[j], tile_sem.at[j])
 
     score_loop(
-        slots, order_ref, counts_ref, x, panels, norms, tops, masses, tiles, here,
+        slots, order_ref, counts_ref, x, piece_refs, norms, tops, masses, tiles, here,
         lambda j: outgoing(j).start(),
     )
     here(blocks - 1)
@@ -232,17 +216,18 @@
 def sum_kernel(slots, order_ref, counts_ref, x, tiles_ref, shares, *refs):
     pieces = len(slots)
     out_refs = refs[:pieces]
-    acc, totals, tiles, tile_sem, out_sem = refs[pieces:]
+    totals, tiles, tile_sem = refs[pieces:]
 
     def incoming(j):
         return pltpu.make_async_copy(tiles_ref.at[j], tiles.at[j], tile_sem.at[j])
 
     over_tiles(slots, counts_ref, x.shape[0] // BLOCK, lambda j: incoming(j).start())
-    clear_sums(acc, totals)
+    clear_sums(out_refs, totals)
     sum_loop(
-        slots, order_ref, counts_ref, x, shares, acc, totals, tiles, lambda j: incoming(j).wait()
-    )
-    store_sums(acc, totals, out_refs, out_sem)
+        slots, order_ref, counts_ref, x, shares, out_refs, totals, tiles,
+        lambda j: incoming(j).wait(),
+    )
+    store_totals(out_refs, totals)
 
 
 def middle_kernel(slots, listed, earlier, order_ref, counts_ref, x, *refs):
@@ -252,13 +237,12 @@
     refs = refs[2 * earlier + pieces :]
     logs_ref, shares = refs[:2]
     out_refs = refs[2 : 2 + pieces]
-    panels, norms, tiles, tops, masses, acc, totals, panel_sem, out_sem = refs[2 + pieces :]
+    norms, tiles, tops, masses, totals = refs[2 + pieces :]
     blocks = x.shape[0] // BLOCK
-    finish_panels = load_panels(piece_refs, panels, norms, panel_sem)
-    clear_sums(acc, totals)
-    finish_panels()
+    clear_sums(out_refs, totals)
+    find_norms(piece_refs, norms)
     score_loop(
-        slots, order_ref, counts_ref, x, panels, norms, tops, masses, tiles,
+        slots, order_ref, counts_ref, x, piece_refs, norms, tops, masses, tiles,
         lambda b: None, lambda j: None,
     )
     width = tops.shape[1]
@@ -271,12 +255,11 @@
     whole = jnp.sum(factor * mass, axis=0)
     logs_ref[...] = (highest + jnp.log2(whole)) * (1.0 / LOG2E)
     shares[...] = (factor / whole[None]).reshape(listed * blocks, width)
-    sum_loop(slots, order_ref, counts_ref, x, shares, acc, totals, tiles, lambda j: None)
-    store_sums(acc, totals, out_refs, out_sem)
+    sum_loop(slots, order_ref, counts_ref, x, shares, out_refs, totals, tiles, lambda j: None)
+    store_totals(out_refs, totals)
 
 
 SMEM = pl.BlockSpec(memory_space=pltpu.SMEM)
-ANY = pl.BlockSpec(memory_space=pl.ANY)
 HBM = pl.BlockSpec(memory_space=pltpu.HBM)
 VMEM = pl.BlockSpec(memory_space=pltpu.VMEM)
 
@@ -297,17 +280,8 @@
             transcendentals=int(pairs * self.cent * BLOCK),
         )
 
-    def panel_scratch(self, pieces):
-        return [
-            pltpu.VMEM((pieces, self.cent, self.width), jnp.bfloat16),
-            pltpu.VMEM((pieces, self.cent, 128), jnp.float32),
-        ]
-
-    def sum_scratch(self, pieces):
-        return [
-            pltpu.VMEM((pieces, self.cent + EXTRA, self.width), jnp.float32),
-            pltpu.VMEM((pieces, self.cent, 128), jnp.float32),
-        ]
+    def columns(self, pieces):
+        return pltpu.VMEM((pieces, self.cent, 128), jnp.float32)
 
     def tile_scratch(self, pieces):
         return pltpu.VMEM((pieces * self.blocks, self.cent, BLOCK), jnp.float32)
@@ -323,12 +297,11 @@
     return pl.pallas_call(
         functools.partial(score_kernel, slots, fetch),
         out_shape=outs + rows_outs,
-        in_specs=[SMEM, SMEM, HBM if fetch else VMEM] + [ANY] * count,
+        in_specs=[SMEM, SMEM, HBM if fetch else VMEM] + [VMEM] * count,
         out_specs=(HBM, VMEM, VMEM) + (VMEM,) * len(rows_outs),
-        scratch_shapes=sizes.panel_scratch(count)
-        + [
+        scratch_shapes=[
+            sizes.columns(count),
             sizes.tile_scratch(count),
-            pltpu.SemaphoreType.DMA((count,)),
             pltpu.SemaphoreType.DMA((count * sizes.blocks,)),
         ]
         + rows_scratch,
@@ -344,12 +317,11 @@
         functools.partial(sum_kernel, slots),
         out_shape=(sizes.sums,) * count,
         in_specs=[SMEM, SMEM, VMEM, HBM, VMEM],
-        out_specs=(ANY,) * count,
-        scratch_shapes=sizes.sum_scratch(count)
-        + [
+        out_specs=(VMEM,) * count,
+        scratch_shapes=[
+            sizes.columns(count),
             sizes.tile_scratch(count),
             pltpu.SemaphoreType.DMA((count * sizes.blocks,)),
-            pltpu.SemaphoreType.DMA((count,)),
         ],
         compiler_params=pltpu.CompilerParams(vmem_limit_bytes=VMEM_GRANT),
         cost_estimate=sizes.cost(slots, 1),
@@ -364,16 +336,15 @@
         functools.partial(middle_kernel, slots, sizes.listed, earlier),
         out_shape=(jax.ShapeDtypeStruct((sizes.blocks, BLOCK), jnp.float32), sizes.stats)
         + (sizes.sums,) * count,
-        in_specs=[SMEM, SMEM, VMEM] + [VMEM] * (2 * earlier) + [ANY] * count,
-        out_specs=(VMEM, VMEM) + (ANY,) * count,
-        scratch_shapes=sizes.panel_scratch(count)
-        + [
+        in_specs=[SMEM, SMEM, VMEM] + [VMEM] * (2 * earlier + count),
+        out_specs=(VMEM, VMEM) + (VMEM,) * count,
+        scratch_shapes=[
+            sizes.columns(count),
             sizes.tile_scratch(count),
             pltpu.VMEM(sizes.stats.shape, jnp.float32),
             pltpu.VMEM(sizes.stats.shape, jnp.float32),
-        ]
-        + sizes.sum_scratch(count)
-        + [pltpu.SemaphoreType.DMA((count,)), pltpu.SemaphoreType.DMA((count,))],
+            sizes.columns(count),
+        ],
         compiler_params=pltpu.CompilerParams(vmem_limit_bytes=VMEM_GRANT),
         cost_estimate=sizes.cost(slots, 2),
         name="middle_group",

time: 113 us -> 109 us (0.965)
  the two profiles are of different devices: /device:TPU:0 before, /device:TPU:2 now
where the time goes in v3:
time: 109 us; the launch traced here: 108 us
  Pallas kernels  58.3 us (53%)
  starting transfers between devices  24.8 us (23%)
  waiting for transfers between devices  17.7 us (16%)
  other arithmetic  3.55 us (3%)
  local copies, waits for them, and re-layouts  2.4 us (2%)
    pallas_call x4, Pallas kernels, score_group(): pl.pallas_call(functools.partial(score_kernel, slots, fetch), out_shape=o...  27.6 us
    pallas_call x4, Pallas kernels, sum_group(): pl.pallas_call(functools.partial(sum_kernel, slots), out_shape=(sizes.sum...  24.6 us
    ppermute x6, starting transfers between devices, moved(): return lax.ppermute(value, 'blk', [(i, i ^ 2) for i in range(count)])  12 us
    ppermute x6, waiting for transfers between devices, moved(): lax.ppermute(value, 'blk', [(i, (i + shift) % count) for i in range(count)])  10.7 us
    ppermute x6, starting transfers between devices, moved(): lax.ppermute(value, 'blk', [(i, (i + shift) % count) for i in range(count)])  8.34 us
    pallas_call x1, Pallas kernels, middle_group(): pl.pallas_call(functools.partial(middle_kernel, slots, sizes.listed, earl...  5.75 us
    ppermute x6, waiting for transfers between devices, moved(): return lax.ppermute(value, 'blk', [(i, i ^ 2) for i in range(count)])  5.34 us
    ppermute x14, starting transfers between devices, other_core(): return lax.ppermute(value, 'blk', [(i, i ^ 1) for i in range(count)])  4.49 us
  transfers between devices with their start and end apart: 26, of which 11 were waited for; matrix products, arithmetic and copies ran while one was open for 2% of the time, Pallas kernels for 49%

profile of v3, /device:TPU:2, one launch (start us, length us, event | category | flops | bytes accessed | tf_op | source)
XLA Modules:
  0.0 107.7 jit_solution(13027834187163914312)
XLA Ops:
  0.7 1.6 %collective-permute-start.1 = (bf16[256,768]{1,0:T(8,128)(2,1)}, bf16[256,768]{1,0:T(8,128)(2,1)S(1)}, u32[]{:S(2)}, u32[]{:S(2)}) collective-permute-start(bf16[256,768]{1,0:T(8,128)(2,1)} %refs_0_.1), channel_id=1, source_target_pairs={{0,2},{1,3},{2,0},{3,1},{4,6},{5,7},{6,4},{7,5},{8,10},{9,11},{10,... | collective-permute-start | bytes 1179656 | tf_op jit(solution)/shard_map/ppermute | solution.py:49
  2.3 1.6 %collective-permute-start = (bf16[256,768]{1,0:T(8,128)(2,1)}, bf16[256,768]{1,0:T(8,128)(2,1)S(1)}, u32[]{:S(2)}, u32[]{:S(2)}) collective-permute-start(bf16[256,768]{1,0:T(8,128)(2,1)} %refs_0_.1), channel_id=1, source_target_pairs={{0,4},{1,5},{2,6},{3,7},{4,8},{5,9},{6,10},{7,11},{8,12},{9,13},{1... | collective-permute-start | bytes 1179656 | tf_op jit(solution)/shard_map/ppermute | solution.py:50
  3.9 0.7 fusion.9
  5.3 1.0 copy-done
  6.2 9.4 %score_group.4 = (f32[64,256,256]{2,1,0:T(8,128)}, f32[96,256]{1,0:T(8,128)S(1)}, f32[96,256]{1,0:T(8,128)S(1)}, bf16[4096,768]{1,0:T(8,128)(2,1)S(1)}) custom-call(s32[256]{0:T(256)S(1)} %reshape.57.order_ref, s32[16]{0:T(128)S(1)} %convert_reduce_fusion.counts_ref, bf16[4096,768]{1,0:T(8,128)(2,1)} %rows_ref.1, bf16[256,768]{1,0:T(8,128)(2,1)S(1)} %copy-done, ...), custom_call_target="tpu_custom_call" | custom-call | flops 1380525184 | bytes 9886573 | tf_op jit(solution)/shard_map/score_group/pallas_call | solution.py:297
  16.2 1.6 %collective-permute-start.3 = (bf16[256,768]{1,0:T(8,128)(2,1)S(1)}, bf16[256,768]{1,0:T(8,128)(2,1)S(1)}, u32[]{:S(2)}, u32[]{:S(2)}) collective-permute-start(bf16[256,768]{1,0:T(8,128)(2,1)S(1)} %copy-done), channel_id=1, source_target_pairs={{0,12},{1,13},{2,14},{3,15},{4,0},{5,1},{6,2},{7,3},{8,4},{9,5},{1... | collective-permute-start | bytes 1179656 | tf_op jit(solution)/shard_map/ppermute | solution.py:50
  18.3 7.5 %score_group.5 = (f32[64,256,256]{2,1,0:T(8,128)}, f32[96,256]{1,0:T(8,128)S(1)}, f32[96,256]{1,0:T(8,128)S(1)}) custom-call(s32[256]{0:T(256)S(1)} %reshape.57.order_ref, s32[16]{0:T(128)S(1)} %convert_reduce_fusion.counts_ref, bf16[4096,768]{1,0:T(8,128)(2,1)S(1)} %get-tuple-element.67.rows_ref.x, bf16[256,768]{1,0:T(8,128)(2,1)S(1)} %collective-permute-done.refs_0_, ...), custom_call_target="tpu_custom_call" | custom-call | flops 2761050368 | bytes 13481691 | tf_op jit(solution)/shard_map/score_group/pallas_call | solution.py:297
  25.9 1.5 %collective-permute-done.3.refs_0_ = bf16[256,768]{1,0:T(8,128)(2,1)S(1)} collective-permute-done((bf16[256,768]{1,0:T(8,128)(2,1)S(1)}, bf16[256,768]{1,0:T(8,128)(2,1)S(1)}, u32[]{:S(2)}, u32[]{:S(2)}) %collective-permute-start.3) | collective-permute-done | bytes 393248 | tf_op jit(solution)/shard_map/ppermute | solution.py:50
  27.3 1.2 %collective-permute-done.4.refs_2_ = bf16[256,768]{1,0:T(8,128)(2,1)S(1)} collective-permute-done((bf16[256,768]{1,0:T(8,128)(2,1)S(1)}, bf16[256,768]{1,0:T(8,128)(2,1)S(1)}, u32[]{:S(2)}, u32[]{:S(2)}) %collective-permute-start.4) | collective-permute-done | bytes 393248 | tf_op jit(solution)/shard_map/ppermute | solution.py:49
  29.1 0.5 collective-permute-start.7
  30.3 0.6 collective-permute-done.9.refs_1_
  30.8 5.8 %score_group.6 = (f32[64,256,256]{2,1,0:T(8,128)}, f32[96,256]{1,0:T(8,128)S(1)}, f32[96,256]{1,0:T(8,128)S(1)}) custom-call(s32[256]{0:T(256)S(1)} %reshape.57.order_ref, s32[16]{0:T(128)S(1)} %convert_reduce_fusion.counts_ref, bf16[4096,768]{1,0:T(8,128)(2,1)S(1)} %get-tuple-element.67.rows_ref.x, bf16[256,768]{1,0:T(8,128)(2,1)S(1)} %collective-permute-done.3.refs_0_, ...), custom_call_target="tpu_custom_call" | custom-call | flops 2761050368 | bytes 13481691 | tf_op jit(solution)/shard_map/score_group/pallas_call | solution.py:297
  36.6 5.3 %collective-permute-done.7.refs_0_ = bf16[256,768]{1,0:T(8,128)(2,1)S(1)} collective-permute-done((bf16[256,768]{1,0:T(8,128)(2,1)S(1)}, bf16[256,768]{1,0:T(8,128)(2,1)S(1)}, u32[]{:S(2)}, u32[]{:S(2)}) %collective-permute-start.7) | collective-permute-done | bytes 393248 | tf_op jit(solution)/shard_map/ppermute | solution.py:50
  41.9 0.5 collective-permute-start.12
  42.4 4.9 %score_group.7 = (f32[64,256,256]{2,1,0:T(8,128)}, f32[96,256]{1,0:T(8,128)S(1)}, f32[96,256]{1,0:T(8,128)S(1)}) custom-call(s32[256]{0:T(256)S(1)} %reshape.57.order_ref, s32[16]{0:T(128)S(1)} %convert_reduce_fusion.counts_ref, bf16[4096,768]{1,0:T(8,128)(2,1)S(1)} %get-tuple-element.67.rows_ref.x, bf16[256,768]{1,0:T(8,128)(2,1)S(1)} %collective-permute-done.7.refs_0_, ...), custom_call_target="tpu_custom_call" | custom-call | flops 1380525184 | bytes 9886573 | tf_op jit(solution)/shard_map/score_group/pallas_call | solution.py:297
  47.3 5.7 %middle_group.1 = (f32[16,256]{1,0:T(8,128)S(1)}, f32[96,256]{1,0:T(8,128)S(1)}, f32[264,768]{1,0:T(8,128)S(1)}, f32[264,768]{1,0:T(8,128)S(1)}) custom-call(s32[256]{0:T(256)S(1)} %reshape.57.order_ref, s32[16]{0:T(128)S(1)} %convert_reduce_fusion.counts_ref, bf16[4096,768]{1,0:T(8,128)(2,1)S(1)} %get-tuple-element.67.rows_ref.x, ...), custom_call_target="tpu_custom_call" | custom-call | flops 2761050368 | bytes 9886573 | tf_op jit(solution)/shard_map/middle_group/pallas_call | solution.py:335
  53.6 4.7 %sum_group.4 = (f32[264,768]{1,0:T(8,128)S(1)}, f32[264,768]{1,0:T(8,128)S(1)}) custom-call(s32[256]{0:T(256)S(1)} %reshape.57.order_ref, s32[16]{0:T(128)S(1)} %convert_reduce_fusion.counts_ref, bf16[4096,768]{1,0:T(8,128)(2,1)S(1)} %get-tuple-element.67.rows_ref.x, f32[64,256,256]{2,1,0:T(8,128)} %get-tuple-element.84.tiles_ref, ...), custom_call_target="tpu_custom_call" | custom-call | flops 1380525184 | bytes 9886573 | tf_op jit(solution)/shard_map/sum_group/pallas_call | solution.py:316
  58.7 9.2 %collective-permute-start.16 = (f16[264,768]{1,0:T(8,128)(2,1)S(1)}, f16[264,768]{1,0:T(8,128)(2,1)S(1)}, u32[]{:S(2)}, u32[]{:S(2)}) collective-permute-start(f16[264,768]{1,0:T(8,128)(2,1)S(1)} %multiply_convert_fusion.1), channel_id=1, source_target_pairs={{0,2},{1,3},{2,0},{3,1},{4,6},{5,7},{6,4},{7,5},{8,10},{9,11},{10,... | collective-permute-start | bytes 1216520 | tf_op jit(solution)/shard_map/ppermute | solution.py:49
  68.0 5.7 %sum_group.5 = (f32[264,768]{1,0:T(8,128)S(1)}, f32[264,768]{1,0:T(8,128)S(1)}, f32[264,768]{1,0:T(8,128)S(1)}, f32[264,768]{1,0:T(8,128)S(1)}) custom-call(s32[256]{0:T(256)S(1)} %reshape.57.order_ref, s32[16]{0:T(128)S(1)} %convert_reduce_fusion.counts_ref, bf16[4096,768]{1,0:T(8,128)(2,1)S(1)} %get-tuple-element.67.rows_ref.x, ...), custom_call_target="tpu_custom_call" | custom-call | flops 2761050368 | bytes 13481691 | tf_op jit(solution)/shard_map/sum_group/pallas_call | solution.py:316
  73.7 1.2 %collective-permute-start.17 = (f32[264,768]{1,0:T(8,128)S(1)}, f32[264,768]{1,0:T(8,128)S(1)}, u32[]{:S(2)}, u32[]{:S(2)}) collective-permute-start(f32[264,768]{1,0:T(8,128)S(1)} %get-tuple-element.103), channel_id=1, source_target_pairs={{0,1},{1,0},{2,3},{3,2},{4,5},{5,4},{6,7},{7,6},{8,9},{9,8},{10,11... | collective-permute-start | bytes 2433032 | tf_op jit(solution)/shard_map/ppermute | solution.py:55
  75.0 1.9 %collective-permute-done.16 = f16[264,768]{1,0:T(8,128)(2,1)S(1)} collective-permute-done((f16[264,768]{1,0:T(8,128)(2,1)S(1)}, f16[264,768]{1,0:T(8,128)(2,1)S(1)}, u32[]{:S(2)}, u32[]{:S(2)}) %collective-permute-start.16) | collective-permute-done | bytes 405536 | tf_op jit(solution)/shard_map/ppermute | solution.py:49
  77.3 0.7 collective-permute-done.18
  78.1 4.5 %collective-permute-start.19 = (f16[264,768]{1,0:T(8,128)(2,1)S(1)}, f16[264,768]{1,0:T(8,128)(2,1)S(1)}, u32[]{:S(2)}, u32[]{:S(2)}) collective-permute-start(f16[264,768]{1,0:T(8,128)(2,1)S(1)} %add_convert_fusion.2), channel_id=1, source_target_pairs={{0,4},{1,5},{2,6},{3,7},{4,8},{5,9},{6,10},{7,11},{8,12},{9,13},{1... | collective-permute-start | bytes 1216520 | tf_op jit(solution)/shard_map/ppermute | solution.py:50
  82.7 7.0 %sum_group.6 = (f32[264,768]{1,0:T(8,128)S(1)}, f32[264,768]{1,0:T(8,128)S(1)}, f32[264,768]{1,0:T(8,128)S(1)}, f32[264,768]{1,0:T(8,128)S(1)}) custom-call(s32[256]{0:T(256)S(1)} %reshape.57.order_ref, s32[16]{0:T(128)S(1)} %convert_reduce_fusion.counts_ref, bf16[4096,768]{1,0:T(8,128)(2,1)S(1)} %get-tuple-element.67.rows_ref.x, ...), custom_call_target="tpu_custom_call" | custom-call | flops 2761050368 | bytes 13481691 | tf_op jit(solution)/shard_map/sum_group/pallas_call | solution.py:316
  89.7 0.8 collective-permute-start.21
  90.5 1.1 %collective-permute-done.19 = f16[264,768]{1,0:T(8,128)(2,1)S(1)} collective-permute-done((f16[264,768]{1,0:T(8,128)(2,1)S(1)}, f16[264,768]{1,0:T(8,128)(2,1)S(1)}, u32[]{:S(2)}, u32[]{:S(2)}) %collective-permute-start.19) | collective-permute-done | bytes 405536 | tf_op jit(solution)/shard_map/ppermute | solution.py:50
  91.7 2.2 %collective-permute-done.20 = f16[264,768]{1,0:T(8,128)(2,1)S(1)} collective-permute-done((f16[264,768]{1,0:T(8,128)(2,1)S(1)}, f16[264,768]{1,0:T(8,128)(2,1)S(1)}, u32[]{:S(2)}, u32[]{:S(2)}) %collective-permute-start.20) | collective-permute-done | bytes 405536 | tf_op jit(solution)/shard_map/ppermute | solution.py:49
  94.7 0.6 copy.6
  95.3 7.2 %sum_group.7 = (f32[264,768]{1,0:T(8,128)S(1)}, f32[264,768]{1,0:T(8,128)S(1)}) custom-call(s32[256]{0:T(256)S(1)} %reshape.57.order_ref, s32[16]{0:T(128)S(1)} %convert_reduce_fusion.counts_ref, bf16[4096,768]{1,0:T(8,128)(2,1)S(1)} %get-tuple-element.67.rows_ref.x, f32[64,256,256]{2,1,0:T(8,128)} %get-tuple-element.68.tiles_ref, ...), custom_call_target="tpu_custom_call" | custom-call | flops 1380525184 | bytes 9886573 | tf_op jit(solution)/shard_map/sum_group/pallas_call | solution.py:316
  102.6 2.8 %collective-permute-done.23 = f16[264,768]{1,0:T(8,128)(2,1)S(1)} collective-permute-done((f16[264,768]{1,0:T(8,128)(2,1)S(1)}, f16[264,768]{1,0:T(8,128)(2,1)S(1)}, u32[]{:S(2)}, u32[]{:S(2)}) %collective-permute-start.23) | collective-permute-done | bytes 405536 | tf_op jit(solution)/shard_map/ppermute | solution.py:50
  106.0 0.7 copy-done.1
  106.7 1.0 fusion
  (61 shorter events, 6.1 us)
Async XLA Ops:
  0.6 4.6 %collective-permute-start.2 = (bf16[256,768]{1,0:T(8,128)(2,1)}, bf16[256,768]{1,0:T(8,128)(2,1)S(1)}, u32[]{:S(2)}, u32[]{:S(2)}) collective-permute-start(bf16[256,768]{1,0:T(8,128)(2,1)} %refs_0_.1), channel_id=1, source_target_pairs={{0,1},{1,0},{2,3},{3,2},{4,5},{5,4},{6,7},{7,6},{8,9},{9,8},{10,11... | collective-permute-start | bytes 1179656 | tf_op jit(solution)/shard_map/ppermute | solution.py:55
  0.7 14.9 %collective-permute-start.1 = (bf16[256,768]{1,0:T(8,128)(2,1)}, bf16[256,768]{1,0:T(8,128)(2,1)S(1)}, u32[]{:S(2)}, u32[]{:S(2)}) collective-permute-start(bf16[256,768]{1,0:T(8,128)(2,1)} %refs_0_.1), channel_id=1, source_target_pairs={{0,2},{1,3},{2,0},{3,1},{4,6},{5,7},{6,4},{7,5},{8,10},{9,11},{10,... | collective-permute-start | bytes 1179656 | tf_op jit(solution)/shard_map/ppermute | solution.py:49
  2.3 13.3 %collective-permute-start = (bf16[256,768]{1,0:T(8,128)(2,1)}, bf16[256,768]{1,0:T(8,128)(2,1)S(1)}, u32[]{:S(2)}, u32[]{:S(2)}) collective-permute-start(bf16[256,768]{1,0:T(8,128)(2,1)} %refs_0_.1), channel_id=1, source_target_pairs={{0,4},{1,5},{2,6},{3,7},{4,8},{5,9},{6,10},{7,11},{8,12},{9,13},{1... | collective-permute-start | bytes 1179656 | tf_op jit(solution)/shard_map/ppermute | solution.py:50
  5.2 1.0 copy-start
  15.6 2.7 %collective-permute-start.6 = (bf16[256,768]{1,0:T(8,128)(2,1)S(1)}, bf16[256,768]{1,0:T(8,128)(2,1)S(1)}, u32[]{:S(2)}, u32[]{:S(2)}) collective-permute-start(bf16[256,768]{1,0:T(8,128)(2,1)S(1)} %collective-permute-done.1.refs_2_), channel_id=1, source_target_pairs={{0,1},{1,0},{2,3},{3,2},{4,5},{5,4},{6,7},{7,6},{8,9},{9,8},{10,11... | collective-permute-start | bytes 1179656 | tf_op jit(solution)/shard_map/ppermute | solution.py:55
  15.7 2.6 %collective-permute-start.5 = (bf16[256,768]{1,0:T(8,128)(2,1)S(1)}, bf16[256,768]{1,0:T(8,128)(2,1)S(1)}, u32[]{:S(2)}, u32[]{:S(2)}) collective-permute-start(bf16[256,768]{1,0:T(8,128)(2,1)S(1)} %collective-permute-done.refs_0_), channel_id=1, source_target_pairs={{0,1},{1,0},{2,3},{3,2},{4,5},{5,4},{6,7},{7,6},{8,9},{9,8},{10,11... | collective-permute-start | bytes 1179656 | tf_op jit(solution)/shard_map/ppermute | solution.py:55
  16.2 11.1 %collective-permute-start.3 = (bf16[256,768]{1,0:T(8,128)(2,1)S(1)}, bf16[256,768]{1,0:T(8,128)(2,1)S(1)}, u32[]{:S(2)}, u32[]{:S(2)}) collective-permute-start(bf16[256,768]{1,0:T(8,128)(2,1)S(1)} %copy-done), channel_id=1, source_target_pairs={{0,12},{1,13},{2,14},{3,15},{4,0},{5,1},{6,2},{7,3},{8,4},{9,5},{1... | collective-permute-start | bytes 1179656 | tf_op jit(solution)/shard_map/ppermute | solution.py:50
  17.8 10.7 %collective-permute-start.4 = (bf16[256,768]{1,0:T(8,128)(2,1)S(1)}, bf16[256,768]{1,0:T(8,128)(2,1)S(1)}, u32[]{:S(2)}, u32[]{:S(2)}) collective-permute-start(bf16[256,768]{1,0:T(8,128)(2,1)S(1)} %collective-permute-done.refs_0_), channel_id=1, source_target_pairs={{0,2},{1,3},{2,0},{3,1},{4,6},{5,7},{6,4},{7,5},{8,10},{9,11},{10,... | collective-permute-start | bytes 1179656 | tf_op jit(solution)/shard_map/ppermute | solution.py:49
  28.5 1.7 %collective-permute-start.10 = (bf16[256,768]{1,0:T(8,128)(2,1)S(1)}, bf16[256,768]{1,0:T(8,128)(2,1)S(1)}, u32[]{:S(2)}, u32[]{:S(2)}) collective-permute-start(bf16[256,768]{1,0:T(8,128)(2,1)S(1)} %collective-permute-done.4.refs_2_), channel_id=1, source_target_pairs={{0,1},{1,0},{2,3},{3,2},{4,5},{5,4},{6,7},{7,6},{8,9},{9,8},{10,11... | collective-permute-start | bytes 1179656 | tf_op jit(solution)/shard_map/ppermute | solution.py:55
  28.5 2.3 %collective-permute-start.9 = (bf16[256,768]{1,0:T(8,128)(2,1)S(1)}, bf16[256,768]{1,0:T(8,128)(2,1)S(1)}, u32[]{:S(2)}, u32[]{:S(2)}) collective-permute-start(bf16[256,768]{1,0:T(8,128)(2,1)S(1)} %collective-permute-done.3.refs_0_), channel_id=1, source_target_pairs={{0,1},{1,0},{2,3},{3,2},{4,5},{5,4},{6,7},{7,6},{8,9},{9,8},{10,11... | collective-permute-start | bytes 1179656 | tf_op jit(solution)/shard_map/ppermute | solution.py:55
  29.1 12.8 %collective-permute-start.7 = (bf16[256,768]{1,0:T(8,128)(2,1)S(1)}, bf16[256,768]{1,0:T(8,128)(2,1)S(1)}, u32[]{:S(2)}, u32[]{:S(2)}) collective-permute-start(bf16[256,768]{1,0:T(8,128)(2,1)S(1)} %collective-permute-done.4.refs_2_), channel_id=1, source_target_pairs={{0,4},{1,5},{2,6},{3,7},{4,8},{5,9},{6,10},{7,11},{8,12},{9,13},{1... | collective-permute-start | bytes 1179656 | tf_op jit(solution)/shard_map/ppermute | solution.py:50
  29.6 12.3 %collective-permute-start.8 = (bf16[256,768]{1,0:T(8,128)(2,1)S(1)}, bf16[256,768]{1,0:T(8,128)(2,1)S(1)}, u32[]{:S(2)}, u32[]{:S(2)}) collective-permute-start(bf16[256,768]{1,0:T(8,128)(2,1)S(1)} %collective-permute-done.3.refs_0_), channel_id=1, source_target_pairs={{0,2},{1,3},{2,0},{3,1},{4,6},{5,7},{6,4},{7,5},{8,10},{9,11},{10,... | collective-permute-start | bytes 1179656 | tf_op jit(solution)/shard_map/ppermute | solution.py:49
  41.9 5.4 %collective-permute-start.11 = (bf16[256,768]{1,0:T(8,128)(2,1)S(1)}, bf16[256,768]{1,0:T(8,128)(2,1)S(1)}, u32[]{:S(2)}, u32[]{:S(2)}) collective-permute-start(bf16[256,768]{1,0:T(8,128)(2,1)S(1)} %collective-permute-done.7.refs_0_), channel_id=1, source_target_pairs={{0,1},{1,0},{2,3},{3,2},{4,5},{5,4},{6,7},{7,6},{8,9},{9,8},{10,11... | collective-permute-start | bytes 1179656 | tf_op jit(solution)/shard_map/ppermute | solution.py:55
  41.9 5.4 %collective-permute-start.12 = (bf16[256,768]{1,0:T(8,128)(2,1)S(1)}, bf16[256,768]{1,0:T(8,128)(2,1)S(1)}, u32[]{:S(2)}, u32[]{:S(2)}) collective-permute-start(bf16[256,768]{1,0:T(8,128)(2,1)S(1)} %collective-permute-done.8.refs_1_), channel_id=1, source_target_pairs={{0,1},{1,0},{2,3},{3,2},{4,5},{5,4},{6,7},{7,6},{8,9},{9,8},{10,11... | collective-permute-start | bytes 1179656 | tf_op jit(solution)/shard_map/ppermute | solution.py:55
  53.0 5.3 %collective-permute-start.13 = (f32[264,768]{1,0:T(8,128)S(1)}, f32[264,768]{1,0:T(8,128)S(1)}, u32[]{:S(2)}, u32[]{:S(2)}) collective-permute-start(f32[264,768]{1,0:T(8,128)S(1)} %get-tuple-element.95), channel_id=1, source_target_pairs={{0,1},{1,0},{2,3},{3,2},{4,5},{5,4},{6,7},{7,6},{8,9},{9,8},{10,11... | collective-permute-start | bytes 2433032 | tf_op jit(solution)/shard_map/ppermute | solution.py:55
  53.1 5.4 %collective-permute-start.14 = (f32[264,768]{1,0:T(8,128)S(1)}, f32[264,768]{1,0:T(8,128)S(1)}, u32[]{:S(2)}, u32[]{:S(2)}) collective-permute-start(f32[264,768]{1,0:T(8,128)S(1)} %get-tuple-element.97), channel_id=1, source_target_pairs={{0,1},{1,0},{2,3},{3,2},{4,5},{5,4},{6,7},{7,6},{8,9},{9,8},{10,11... | collective-permute-start | bytes 2433032 | tf_op jit(solution)/shard_map/ppermute | solution.py:55
  58.7 16.4 %collective-permute-start.15 = (f16[264,768]{1,0:T(8,128)(2,1)S(1)}, f16[264,768]{1,0:T(8,128)(2,1)S(1)}, u32[]{:S(2)}, u32[]{:S(2)}) collective-permute-start(f16[264,768]{1,0:T(8,128)(2,1)S(1)} %multiply_convert_fusion.2), channel_id=1, source_target_pairs={{0,12},{1,13},{2,14},{3,15},{4,0},{5,1},{6,2},{7,3},{8,4},{9,5},{1... | collective-permute-start | bytes 1216520 | tf_op jit(solution)/shard_map/ppermute | solution.py:50
  58.7 18.1 %collective-permute-start.16 = (f16[264,768]{1,0:T(8,128)(2,1)S(1)}, f16[264,768]{1,0:T(8,128)(2,1)S(1)}, u32[]{:S(2)}, u32[]{:S(2)}) collective-permute-start(f16[264,768]{1,0:T(8,128)(2,1)S(1)} %multiply_convert_fusion.1), channel_id=1, source_target_pairs={{0,2},{1,3},{2,0},{3,1},{4,6},{5,7},{6,4},{7,5},{8,10},{9,11},{10,... | collective-permute-start | bytes 1216520 | tf_op jit(solution)/shard_map/ppermute | solution.py:49
  73.7 3.5 %collective-permute-start.17 = (f32[264,768]{1,0:T(8,128)S(1)}, f32[264,768]{1,0:T(8,128)S(1)}, u32[]{:S(2)}, u32[]{:S(2)}) collective-permute-start(f32[264,768]{1,0:T(8,128)S(1)} %get-tuple-element.103), channel_id=1, source_target_pairs={{0,1},{1,0},{2,3},{3,2},{4,5},{5,4},{6,7},{7,6},{8,9},{9,8},{10,11... | collective-permute-start | bytes 2433032 | tf_op jit(solution)/shard_map/ppermute | solution.py:55
  74.9 3.1 %collective-permute-start.18 = (f32[264,768]{1,0:T(8,128)S(1)}, f32[264,768]{1,0:T(8,128)S(1)}, u32[]{:S(2)}, u32[]{:S(2)}) collective-permute-start(f32[264,768]{1,0:T(8,128)S(1)} %get-tuple-element.106), channel_id=1, source_target_pairs={{0,1},{1,0},{2,3},{3,2},{4,5},{5,4},{6,7},{7,6},{8,9},{9,8},{10,11... | collective-permute-start | bytes 2433032 | tf_op jit(solution)/shard_map/ppermute | solution.py:55
  78.1 13.5 %collective-permute-start.19 = (f16[264,768]{1,0:T(8,128)(2,1)S(1)}, f16[264,768]{1,0:T(8,128)(2,1)S(1)}, u32[]{:S(2)}, u32[]{:S(2)}) collective-permute-start(f16[264,768]{1,0:T(8,128)(2,1)S(1)} %add_convert_fusion.2), channel_id=1, source_target_pairs={{0,4},{1,5},{2,6},{3,7},{4,8},{5,9},{6,10},{7,11},{8,12},{9,13},{1... | collective-permute-start | bytes 1216520 | tf_op jit(solution)/shard_map/ppermute | solution.py:50
  82.7 11.1 %collective-permute-start.20 = (f16[264,768]{1,0:T(8,128)(2,1)S(1)}, f16[264,768]{1,0:T(8,128)(2,1)S(1)}, u32[]{:S(2)}, u32[]{:S(2)}) collective-permute-start(f16[264,768]{1,0:T(8,128)(2,1)S(1)} %add_convert_fusion.1), channel_id=1, source_target_pairs={{0,2},{1,3},{2,0},{3,1},{4,6},{5,7},{6,4},{7,5},{8,10},{9,11},{10,... | collective-permute-start | bytes 1216520 | tf_op jit(solution)/shard_map/ppermute | solution.py:49
  89.7 4.4 %collective-permute-start.21 = (f32[264,768]{1,0:T(8,128)S(1)}, f32[264,768]{1,0:T(8,128)S(1)}, u32[]{:S(2)}, u32[]{:S(2)}) collective-permute-start(f32[264,768]{1,0:T(8,128)S(1)} %get-tuple-element.112), channel_id=1, source_target_pairs={{0,1},{1,0},{2,3},{3,2},{4,5},{5,4},{6,7},{7,6},{8,9},{9,8},{10,11... | collective-permute-start | bytes 2433032 | tf_op jit(solution)/shard_map/ppermute | solution.py:55
  90.5 3.7 %collective-permute-start.22 = (f32[264,768]{1,0:T(8,128)S(1)}, f32[264,768]{1,0:T(8,128)S(1)}, u32[]{:S(2)}, u32[]{:S(2)}) collective-permute-start(f32[264,768]{1,0:T(8,128)S(1)} %get-tuple-element.114), channel_id=1, source_target_pairs={{0,1},{1,0},{2,3},{3,2},{4,5},{5,4},{6,7},{7,6},{8,9},{9,8},{10,11... | collective-permute-start | bytes 2433032 | tf_op jit(solution)/shard_map/ppermute | solution.py:55
  94.3 11.1 %collective-permute-start.23 = (f16[264,768]{1,0:T(8,128)(2,1)S(1)}, f16[264,768]{1,0:T(8,128)(2,1)S(1)}, u32[]{:S(2)}, u32[]{:S(2)}) collective-permute-start(f16[264,768]{1,0:T(8,128)(2,1)S(1)} %add_convert_fusion), channel_id=1, source_target_pairs={{0,12},{1,13},{2,14},{3,15},{4,0},{5,1},{6,2},{7,3},{8,4},{9,5},{1... | collective-permute-start | bytes 1216520 | tf_op jit(solution)/shard_map/ppermute | solution.py:50
  94.4 11.1 %collective-permute-start.24 = (f16[264,768]{1,0:T(8,128)(2,1)S(1)}, f16[264,768]{1,0:T(8,128)(2,1)S(1)}, u32[]{:S(2)}, u32[]{:S(2)}) collective-permute-start(f16[264,768]{1,0:T(8,128)(2,1)S(1)} %multiply_convert_fusion), channel_id=1, source_target_pairs={{0,2},{1,3},{2,0},{3,1},{4,6},{5,7},{6,4},{7,5},{8,10},{9,11},{10,... | collective-permute-start | bytes 1216520 | tf_op jit(solution)/shard_map/ppermute | solution.py:49
  102.5 3.3 %collective-permute-start.25 = (f32[264,768]{1,0:T(8,128)S(1)}, f32[264,768]{1,0:T(8,128)S(1)}, u32[]{:S(2)}, u32[]{:S(2)}) collective-permute-start(f32[264,768]{1,0:T(8,128)S(1)} %get-tuple-element.122), channel_id=1, source_target_pairs={{0,1},{1,0},{2,3},{3,2},{4,5},{5,4},{6,7},{7,6},{8,9},{9,8},{10,11... | collective-permute-start | bytes 2433032 | tf_op jit(solution)/shard_map/ppermute | solution.py:55
  105.7 1.0 copy-start.1

commit v4 on v3

--- a/solution.py
+++ b/solution.py
@@ -87,13 +87,28 @@
     lax.fori_loop(2 * fours, (count + 1) // 2, lambda k, _: (act(2 * k, 2), 0)[1], 0)
 
 
+def by_eights(count, act):
+    eights = count // 8
+    lax.fori_loop(0, eights, lambda k, _: (act(8 * k, 8), 0)[1], 0)
+    fours = (count - 8 * eights) // 4
+
+    @pl.when(fours == 1)
+    def _():
+        act(8 * eights, 4)
+
+    lax.fori_loop(
+        4 * eights + 2 * fours, (count + 1) // 2, lambda k, _: (act(2 * k, 2), 0)[1], 0
+    )
+
+
 def rows_of(x, block):
     return x[pl.ds(pl.multiple_of(block * BLOCK, BLOCK), BLOCK)]
 
 
-def find_norms(panels, norms):
-    for p, panel in enumerate(panels):
-        wide = panel[...].astype(jnp.float32)
+def find_norms(piece_refs, panels, norms):
+    for p, piece in enumerate(piece_refs):
+        panels[p] = piece[...]
+        wide = piece[...].astype(jnp.float32)
         norm = jnp.sum(wide * wide, axis=1, keepdims=True)
         norms[p] = jnp.broadcast_to(norm * (0.5 * LOGIT_SCALE * LOG2E), norms.shape[1:])
 
@@ -114,20 +129,36 @@
     blocks = x.shape[0] // BLOCK
     tops[...] = jnp.full_like(tops, -jnp.inf)
     masses[...] = jnp.zeros_like(masses)
-    for p, slot in enumerate(slots):
-
-        def some(first, number):
-            work = some_pairs(order_ref, counts_ref, slot, blocks, first, number)
-            here(work[-1][1])
-            found = [tile_of(panels[p][...], norms[p], rows_of(x, b)) for _, b, _ in work]
-            for (i, _, at), (powers, top, mass) in zip(work, found):
-                tiles[p * blocks + i] = powers
-                tops[pl.ds(at, 1)] = top
-                masses[pl.ds(at, 1)] = mass
-            for i, _, _ in work:
-                done(p * blocks + i)
-
-        by_fours(counts_ref[slot], some)
+    starts = [jnp.int32(0)]
+    for slot in slots:
+        starts.append(starts[-1] + counts_ref[slot])
+    count = starts.pop()
+
+    def pair(j):
+        p = functools.reduce(jnp.add, [(j >= start).astype(jnp.int32) for start in starts[1:]])
+        first, slot = starts[0], jnp.int32(slots[0])
+        for later, start in zip(slots[1:], starts[1:]):
+            first = jnp.where(j >= start, start, first)
+            slot = jnp.where(j >= start, later, slot)
+        code = order_ref[slot * blocks + j - first]
+        return p, p * blocks + j - first, code >> 3, (code & 7) * blocks + (code >> 3)
+
+    def some(first, number):
+        work = [pair(jnp.minimum(first + i, count - 1)) for i in range(number)]
+        for _, _, b, _ in work:
+            here(b)
+        found = [tile_of(panels[p], norms[p], rows_of(x, b)) for p, _, b, _ in work]
+        for (_, tile, _, at), (powers, top, mass) in zip(work, found):
+            tiles[tile] = powers
+            tops[pl.ds(at, 1)] = top
+            masses[pl.ds(at, 1)] = mass
+        for i, (_, tile, _, _) in enumerate(work):
+            if number == 2 and i:
+                pl.when(first + i < count)(functools.partial(done, tile))
+            else:
+                done(tile)
+
+    by_eights(count, some)
 
 
 def sum_loop(slots, order_ref, counts_ref, x, shares, acc, totals, tiles, ready):
@@ -137,14 +168,18 @@
 
         def some(first, number):
             work = some_pairs(order_ref, counts_ref, slot, blocks, first, number)
-            for i, _, _ in work:
-                ready(p * blocks + i)
+            for i, (j, _, _) in enumerate(work):
+                if number == 2 and i:
+                    pl.when(j < counts_ref[slot])(functools.partial(ready, p * blocks + j))
+                else:
+                    ready(p * blocks + j)
             partial, count = None, None
-            for i, b, at in work:
+            for i, (j, b, at) in enumerate(work):
                 share = shares[pl.ds(at, 1)]
-                if number == 2:
-                    share = share * (i < counts_ref[slot]).astype(jnp.float32)
-                weights = (tiles[p * blocks + i] * share).astype(jnp.bfloat16)
+                if number == 2 and i:
+                    share = share * (j < counts_ref[slot]).astype(jnp.float32)
+                    j = jnp.minimum(j, counts_ref[slot] - 1)
+                weights = (tiles[p * blocks + j] * share).astype(jnp.bfloat16)
                 wide = weights.astype(jnp.float32)
                 wide = wide[:, :128] + wide[:, 128:]
                 product = jnp.dot(weights, rows_of(x, b), preferred_element_type=jnp.float32)
@@ -171,8 +206,7 @@
 
 def over_tiles(slots, counts_ref, blocks, act):
     for p, slot in enumerate(slots):
-        held = (counts_ref[slot] + 1) // 2 * 2
-        lax.fori_loop(0, held, lambda i, _: (act(p * blocks + i), 0)[1], 0)
+        lax.fori_loop(0, counts_ref[slot], lambda i, _: (act(p * blocks + i), 0)[1], 0)
 
 
 def score_kernel(slots, fetch, order_ref, counts_ref, rows_ref, *refs):
@@ -181,11 +215,11 @@
     tiles_ref, tops, masses = refs[pieces : pieces + 3]
     refs = refs[pieces + 3 :]
     x = refs[0] if fetch else rows_ref
-    norms, tiles, tile_sem = refs[1:4] if fetch else refs[:3]
+    panels, norms, tiles, tile_sem = refs[1:5] if fetch else refs[:4]
     blocks = x.shape[0] // BLOCK
     here = lambda b: None
     if fetch:
-        row_sem, fetched = refs[4:]
+        row_sem, fetched = refs[5:]
 
         def bring(b):
             span = pl.ds(pl.multiple_of(b * BLOCK, BLOCK), BLOCK)
@@ -200,13 +234,13 @@
             lax.fori_loop(first, b + 1, lambda k, _: (bring(k).wait(), 0)[1], 0)
             fetched[0] = jnp.maximum(first, b + 1)
 
-    find_norms(piece_refs, norms)
+    find_norms(piece_refs, panels, norms)
 
     def outgoing(j):
         return pltpu.make_async_copy(tiles.at[j], tiles_ref.at[j], tile_sem.at[j])
 
     score_loop(
-        slots, order_ref, counts_ref, x, piece_refs, norms, tops, masses, tiles, here,
+        slots, order_ref, counts_ref, x, panels, norms, tops, masses, tiles, here,
         lambda j: outgoing(j).start(),
     )
     here(blocks - 1)
@@ -237,12 +271,12 @@
     refs = refs[2 * earlier + pieces :]
     logs_ref, shares = refs[:2]
     out_refs = refs[2 : 2 + pieces]
-    norms, tiles, tops, masses, totals = refs[2 + pieces :]
+    panels, norms, tiles, tops, masses, totals = refs[2 + pieces :]
     blocks = x.shape[0] // BLOCK
     clear_sums(out_refs, totals)
-    find_norms(piece_refs, norms)
+    find_norms(piece_refs, panels, norms)
     score_loop(
-        slots, order_ref, counts_ref, x, piece_refs, norms, tops, masses, tiles,
+        slots, order_ref, counts_ref, x, panels, norms, tops, masses, tiles,
         lambda b: None, lambda j: None,
     )
     width = tops.shape[1]
@@ -279,6 +313,9 @@
             bytes_accessed=int(2 * self.blocks * BLOCK * self.width + 4 * pairs * self.cent * BLOCK),
             transcendentals=int(pairs * self.cent * BLOCK),
         )
+
+    def panels(self, pieces):
+        return pltpu.VMEM((pieces, self.cent, self.width), jnp.bfloat16)
 
     def columns(self, pieces):
         return pltpu.VMEM((pieces, self.cent, 128), jnp.float32)
@@ -300,6 +337,7 @@
         in_specs=[SMEM, SMEM, HBM if fetch else VMEM] + [VMEM] * count,
         out_specs=(HBM, VMEM, VMEM) + (VMEM,) * len(rows_outs),
         scratch_shapes=[
+            sizes.panels(count),
             sizes.columns(count),
             sizes.tile_scratch(count),
             pltpu.SemaphoreType.DMA((count * sizes.blocks,)),
@@ -339,6 +377,7 @@
         in_specs=[SMEM, SMEM, VMEM] + [VMEM] * (2 * earlier + count),
         out_specs=(VMEM, VMEM) + (VMEM,) * count,
         scratch_shapes=[
+            sizes.panels(count),
             sizes.columns(count),
             sizes.tile_scratch(count),
             pltpu.VMEM(sizes.stats.shape, jnp.float32),

time: 109 us -> 107 us (0.982)
  the two profiles are of different devices: /device:TPU:2 before, /device:TPU:0 now
where the time goes in v4:
time: 107 us
  Pallas kernels  53.4 us (50%)
  starting transfers between devices  24.2 us (23%)
  waiting for transfers between devices  22.5 us (21%)
  other arithmetic  3.55 us (3%)
  local copies, waits for them, and re-layouts  2.4 us (2%)
    pallas_call x4, Pallas kernels, score_group(): pl.pallas_call(functools.partial(score_kernel, slots, fetch), out_shape=o...  26.7 us
    pallas_call x4, Pallas kernels, sum_group(): pl.pallas_call(functools.partial(sum_kernel, slots), out_shape=(sizes.sum...  25 us
    ppermute x6, waiting for transfers between devices, moved(): lax.ppermute(value, 'blk', [(i, (i + shift) % count) for i in range(count)])  15.4 us
    ppermute x6, starting transfers between devices, moved(): lax.ppermute(value, 'blk', [(i, (i + shift) % count) for i in range(count)])  13.7 us
    ppermute x14, starting transfers between devices, other_core(): return lax.ppermute(value, 'blk', [(i, i ^ 1) for i in range(count)])  6.66 us
    ppermute x6, waiting for transfers between devices, moved(): return lax.ppermute(value, 'blk', [(i, i ^ 2) for i in range(count)])  5.54 us
    ppermute x6, starting transfers between devices, moved(): return lax.ppermute(value, 'blk', [(i, i ^ 2) for i in range(count)])  3.88 us
    unnamed x5, local copies, waits for them, and re-layouts  2.32 us
  transfers between devices with their start and end apart: 26, of which 12 were waited for; matrix products, arithmetic and copies ran while one was open for 2% of the time, Pallas kernels for 49%

profile of v4, /device:TPU:0, one launch (start us, length us, event | category | flops | bytes accessed | tf_op | source)
XLA Modules:
  0.0 106.9 jit_solution(14140654302028818005)
XLA Ops:
  1.1 2.6 %collective-permute-start.1 = (bf16[256,768]{1,0:T(8,128)(2,1)}, bf16[256,768]{1,0:T(8,128)(2,1)S(1)}, u32[]{:S(2)}, u32[]{:S(2)}) collective-permute-start(bf16[256,768]{1,0:T(8,128)(2,1)} %refs_0_.1), channel_id=1, source_target_pairs={{0,2},{1,3},{2,0},{3,1},{4,6},{5,7},{6,4},{7,5},{8,10},{9,11},{10,... | collective-permute-start | bytes 1179656 | tf_op jit(solution)/shard_map/ppermute | solution.py:49
  3.7 1.6 %collective-permute-start = (bf16[256,768]{1,0:T(8,128)(2,1)}, bf16[256,768]{1,0:T(8,128)(2,1)S(1)}, u32[]{:S(2)}, u32[]{:S(2)}) collective-permute-start(bf16[256,768]{1,0:T(8,128)(2,1)} %refs_0_.1), channel_id=1, source_target_pairs={{0,4},{1,5},{2,6},{3,7},{4,8},{5,9},{6,10},{7,11},{8,12},{9,13},{1... | collective-permute-start | bytes 1179656 | tf_op jit(solution)/shard_map/ppermute | solution.py:50
  5.3 0.7 fusion.9
  6.7 1.0 copy-done
  7.7 6.6 %score_group.4 = (f32[64,256,256]{2,1,0:T(8,128)}, f32[96,256]{1,0:T(8,128)S(1)}, f32[96,256]{1,0:T(8,128)S(1)}, bf16[4096,768]{1,0:T(8,128)(2,1)S(1)}) custom-call(s32[256]{0:T(256)S(1)} %reshape.57.order_ref, s32[16]{0:T(128)S(1)} %convert_reduce_fusion.counts_ref, bf16[4096,768]{1,0:T(8,128)(2,1)} %rows_ref.1, bf16[256,768]{1,0:T(8,128)(2,1)S(1)} %copy-done, ...), custom_call_target="tpu_custom_call" | custom-call | flops 1380525184 | bytes 9886573 | tf_op jit(solution)/shard_map/score_group/pallas_call | solution.py:334
  14.3 2.7 %collective-permute-done.refs_0_ = bf16[256,768]{1,0:T(8,128)(2,1)S(1)} collective-permute-done((bf16[256,768]{1,0:T(8,128)(2,1)}, bf16[256,768]{1,0:T(8,128)(2,1)S(1)}, u32[]{:S(2)}, u32[]{:S(2)}) %collective-permute-start) | collective-permute-done | bytes 393248 | tf_op jit(solution)/shard_map/ppermute | solution.py:50
  17.5 2.2 %collective-permute-start.3 = (bf16[256,768]{1,0:T(8,128)(2,1)S(1)}, bf16[256,768]{1,0:T(8,128)(2,1)S(1)}, u32[]{:S(2)}, u32[]{:S(2)}) collective-permute-start(bf16[256,768]{1,0:T(8,128)(2,1)S(1)} %copy-done), channel_id=1, source_target_pairs={{0,12},{1,13},{2,14},{3,15},{4,0},{5,1},{6,2},{7,3},{8,4},{9,5},{1... | collective-permute-start | bytes 1179656 | tf_op jit(solution)/shard_map/ppermute | solution.py:50
  20.0 7.6 %score_group.5 = (f32[64,256,256]{2,1,0:T(8,128)}, f32[96,256]{1,0:T(8,128)S(1)}, f32[96,256]{1,0:T(8,128)S(1)}) custom-call(s32[256]{0:T(256)S(1)} %reshape.57.order_ref, s32[16]{0:T(128)S(1)} %convert_reduce_fusion.counts_ref, bf16[4096,768]{1,0:T(8,128)(2,1)S(1)} %get-tuple-element.67.rows_ref.x, bf16[256,768]{1,0:T(8,128)(2,1)S(1)} %collective-permute-done.refs_0_, ...), custom_call_target="tpu_custom_call" | custom-call | flops 2761050368 | bytes 13481691 | tf_op jit(solution)/shard_map/score_group/pallas_call | solution.py:334
  27.7 0.9 collective-permute-done.3.refs_0_
  28.6 2.0 %collective-permute-done.4.refs_2_ = bf16[256,768]{1,0:T(8,128)(2,1)S(1)} collective-permute-done((bf16[256,768]{1,0:T(8,128)(2,1)S(1)}, bf16[256,768]{1,0:T(8,128)(2,1)S(1)}, u32[]{:S(2)}, u32[]{:S(2)}) %collective-permute-start.4) | collective-permute-done | bytes 393248 | tf_op jit(solution)/shard_map/ppermute | solution.py:49
  31.5 0.8 collective-permute-done.10.refs_3_
  32.3 0.6 collective-permute-done.9.refs_1_
  32.9 7.6 %score_group.6 = (f32[64,256,256]{2,1,0:T(8,128)}, f32[96,256]{1,0:T(8,128)S(1)}, f32[96,256]{1,0:T(8,128)S(1)}) custom-call(s32[256]{0:T(256)S(1)} %reshape.57.order_ref, s32[16]{0:T(128)S(1)} %convert_reduce_fusion.counts_ref, bf16[4096,768]{1,0:T(8,128)(2,1)S(1)} %get-tuple-element.67.rows_ref.x, bf16[256,768]{1,0:T(8,128)(2,1)S(1)} %collective-permute-done.3.refs_0_, ...), custom_call_target="tpu_custom_call" | custom-call | flops 2761050368 | bytes 13481691 | tf_op jit(solution)/shard_map/score_group/pallas_call | solution.py:334
  40.5 3.4 %collective-permute-done.7.refs_0_ = bf16[256,768]{1,0:T(8,128)(2,1)S(1)} collective-permute-done((bf16[256,768]{1,0:T(8,128)(2,1)S(1)}, bf16[256,768]{1,0:T(8,128)(2,1)S(1)}, u32[]{:S(2)}, u32[]{:S(2)}) %collective-permute-start.7) | collective-permute-done | bytes 393248 | tf_op jit(solution)/shard_map/ppermute | solution.py:50
  44.4 4.8 %score_group.7 = (f32[64,256,256]{2,1,0:T(8,128)}, f32[96,256]{1,0:T(8,128)S(1)}, f32[96,256]{1,0:T(8,128)S(1)}) custom-call(s32[256]{0:T(256)S(1)} %reshape.57.order_ref, s32[16]{0:T(128)S(1)} %convert_reduce_fusion.counts_ref, bf16[4096,768]{1,0:T(8,128)(2,1)S(1)} %get-tuple-element.67.rows_ref.x, bf16[256,768]{1,0:T(8,128)(2,1)S(1)} %collective-permute-done.7.refs_0_, ...), custom_call_target="tpu_custom_call" | custom-call | flops 1380525184 | bytes 9886573 | tf_op jit(solution)/shard_map/score_group/pallas_call | solution.py:334
  49.3 1.2 %middle_group.1 = (f32[16,256]{1,0:T(8,128)S(1)}, f32[96,256]{1,0:T(8,128)S(1)}, f32[264,768]{1,0:T(8,128)S(1)}, f32[264,768]{1,0:T(8,128)S(1)}) custom-call(s32[256]{0:T(256)S(1)} %reshape.57.order_ref, s32[16]{0:T(128)S(1)} %convert_reduce_fusion.counts_ref, bf16[4096,768]{1,0:T(8,128)(2,1)S(1)} %get-tuple-element.67.rows_ref.x, ...), custom_call_target="tpu_custom_call" | custom-call | flops 2761050368 | bytes 9886573 | tf_op jit(solution)/shard_map/middle_group/pallas_call | solution.py:373
  50.5 3.3 %collective-permute-start.13 = (f32[264,768]{1,0:T(8,128)S(1)}, f32[264,768]{1,0:T(8,128)S(1)}, u32[]{:S(2)}, u32[]{:S(2)}) collective-permute-start(f32[264,768]{1,0:T(8,128)S(1)} %get-tuple-element.95), channel_id=1, source_target_pairs={{0,1},{1,0},{2,3},{3,2},{4,5},{5,4},{6,7},{7,6},{8,9},{9,8},{10,11... | collective-permute-start | bytes 2433032 | tf_op jit(solution)/shard_map/ppermute | solution.py:55
  53.9 4.9 %sum_group.4 = (f32[264,768]{1,0:T(8,128)S(1)}, f32[264,768]{1,0:T(8,128)S(1)}) custom-call(s32[256]{0:T(256)S(1)} %reshape.57.order_ref, s32[16]{0:T(128)S(1)} %convert_reduce_fusion.counts_ref, bf16[4096,768]{1,0:T(8,128)(2,1)S(1)} %get-tuple-element.67.rows_ref.x, f32[64,256,256]{2,1,0:T(8,128)} %get-tuple-element.84.tiles_ref, ...), custom_call_target="tpu_custom_call" | custom-call | flops 1380525184 | bytes 9886573 | tf_op jit(solution)/shard_map/sum_group/pallas_call | solution.py:354
  59.3 7.8 %sum_group.5 = (f32[264,768]{1,0:T(8,128)S(1)}, f32[264,768]{1,0:T(8,128)S(1)}, f32[264,768]{1,0:T(8,128)S(1)}, f32[264,768]{1,0:T(8,128)S(1)}) custom-call(s32[256]{0:T(256)S(1)} %reshape.57.order_ref, s32[16]{0:T(128)S(1)} %convert_reduce_fusion.counts_ref, bf16[4096,768]{1,0:T(8,128)(2,1)S(1)} %get-tuple-element.67.rows_ref.x, ...), custom_call_target="tpu_custom_call" | custom-call | flops 2761050368 | bytes 13481691 | tf_op jit(solution)/shard_map/sum_group/pallas_call | solution.py:354
  67.8 3.6 %collective-permute-done.15 = f16[264,768]{1,0:T(8,128)(2,1)S(1)} collective-permute-done((f16[264,768]{1,0:T(8,128)(2,1)S(1)}, f16[264,768]{1,0:T(8,128)(2,1)S(1)}, u32[]{:S(2)}, u32[]{:S(2)}) %collective-permute-start.15) | collective-permute-done | bytes 405536 | tf_op jit(solution)/shard_map/ppermute | solution.py:50
  71.9 3.2 %collective-permute-start.19 = (f16[264,768]{1,0:T(8,128)(2,1)S(1)}, f16[264,768]{1,0:T(8,128)(2,1)S(1)}, u32[]{:S(2)}, u32[]{:S(2)}) collective-permute-start(f16[264,768]{1,0:T(8,128)(2,1)S(1)} %add_convert_fusion.2), channel_id=1, source_target_pairs={{0,4},{1,5},{2,6},{3,7},{4,8},{5,9},{6,10},{7,11},{8,12},{9,13},{1... | collective-permute-start | bytes 1216520 | tf_op jit(solution)/shard_map/ppermute | solution.py:50
  75.1 0.6 collective-permute-start.20
  75.7 7.6 %sum_group.6 = (f32[264,768]{1,0:T(8,128)S(1)}, f32[264,768]{1,0:T(8,128)S(1)}, f32[264,768]{1,0:T(8,128)S(1)}, f32[264,768]{1,0:T(8,128)S(1)}) custom-call(s32[256]{0:T(256)S(1)} %reshape.57.order_ref, s32[16]{0:T(128)S(1)} %convert_reduce_fusion.counts_ref, bf16[4096,768]{1,0:T(8,128)(2,1)S(1)} %get-tuple-element.67.rows_ref.x, ...), custom_call_target="tpu_custom_call" | custom-call | flops 2761050368 | bytes 13481691 | tf_op jit(solution)/shard_map/sum_group/pallas_call | solution.py:354
  83.9 1.2 %collective-permute-done.19 = f16[264,768]{1,0:T(8,128)(2,1)S(1)} collective-permute-done((f16[264,768]{1,0:T(8,128)(2,1)S(1)}, f16[264,768]{1,0:T(8,128)(2,1)S(1)}, u32[]{:S(2)}, u32[]{:S(2)}) %collective-permute-start.19) | collective-permute-done | bytes 405536 | tf_op jit(solution)/shard_map/ppermute | solution.py:50
  85.1 1.4 %collective-permute-done.20 = f16[264,768]{1,0:T(8,128)(2,1)S(1)} collective-permute-done((f16[264,768]{1,0:T(8,128)(2,1)S(1)}, f16[264,768]{1,0:T(8,128)(2,1)S(1)}, u32[]{:S(2)}, u32[]{:S(2)}) %collective-permute-start.20) | collective-permute-done | bytes 405536 | tf_op jit(solution)/shard_map/ppermute | solution.py:49
  87.0 6.6 %collective-permute-start.23 = (f16[264,768]{1,0:T(8,128)(2,1)S(1)}, f16[264,768]{1,0:T(8,128)(2,1)S(1)}, u32[]{:S(2)}, u32[]{:S(2)}) collective-permute-start(f16[264,768]{1,0:T(8,128)(2,1)S(1)} %add_convert_fusion), channel_id=1, source_target_pairs={{0,12},{1,13},{2,14},{3,15},{4,0},{5,1},{6,2},{7,3},{8,4},{9,5},{1... | collective-permute-start | bytes 1216520 | tf_op jit(solution)/shard_map/ppermute | solution.py:50
  93.6 0.6 copy.6
  94.2 4.7 %sum_group.7 = (f32[264,768]{1,0:T(8,128)S(1)}, f32[264,768]{1,0:T(8,128)S(1)}) custom-call(s32[256]{0:T(256)S(1)} %reshape.57.order_ref, s32[16]{0:T(128)S(1)} %convert_reduce_fusion.counts_ref, bf16[4096,768]{1,0:T(8,128)(2,1)S(1)} %get-tuple-element.67.rows_ref.x, f32[64,256,256]{2,1,0:T(8,128)} %get-tuple-element.68.tiles_ref, ...), custom_call_target="tpu_custom_call" | custom-call | flops 1380525184 | bytes 9886573 | tf_op jit(solution)/shard_map/sum_group/pallas_call | solution.py:354
  99.0 3.7 %collective-permute-done.23 = f16[264,768]{1,0:T(8,128)(2,1)S(1)} collective-permute-done((f16[264,768]{1,0:T(8,128)(2,1)S(1)}, f16[264,768]{1,0:T(8,128)(2,1)S(1)}, u32[]{:S(2)}, u32[]{:S(2)}) %collective-permute-start.23) | collective-permute-done | bytes 405536 | tf_op jit(solution)/shard_map/ppermute | solution.py:50
  102.7 2.1 %collective-permute-done.24 = f16[264,768]{1,0:T(8,128)(2,1)S(1)} collective-permute-done((f16[264,768]{1,0:T(8,128)(2,1)S(1)}, f16[264,768]{1,0:T(8,128)(2,1)S(1)}, u32[]{:S(2)}, u32[]{:S(2)}) %collective-permute-start.24) | collective-permute-done | bytes 405536 | tf_op jit(solution)/shard_map/ppermute | solution.py:49
  105.2 0.7 copy-done.1
  105.9 1.0 fusion
  (61 shorter events, 6.6 us)
Async XLA Ops:
  0.6 6.1 %collective-permute-start.2 = (bf16[256,768]{1,0:T(8,128)(2,1)}, bf16[256,768]{1,0:T(8,128)(2,1)S(1)}, u32[]{:S(2)}, u32[]{:S(2)}) collective-permute-start(bf16[256,768]{1,0:T(8,128)(2,1)} %refs_0_.1), channel_id=1, source_target_pairs={{0,1},{1,0},{2,3},{3,2},{4,5},{5,4},{6,7},{7,6},{8,9},{9,8},{10,11... | collective-permute-start | bytes 1179656 | tf_op jit(solution)/shard_map/ppermute | solution.py:55
  1.1 13.1 %collective-permute-start.1 = (bf16[256,768]{1,0:T(8,128)(2,1)}, bf16[256,768]{1,0:T(8,128)(2,1)S(1)}, u32[]{:S(2)}, u32[]{:S(2)}) collective-permute-start(bf16[256,768]{1,0:T(8,128)(2,1)} %refs_0_.1), channel_id=1, source_target_pairs={{0,2},{1,3},{2,0},{3,1},{4,6},{5,7},{6,4},{7,5},{8,10},{9,11},{10,... | collective-permute-start | bytes 1179656 | tf_op jit(solution)/shard_map/ppermute | solution.py:49
  3.7 13.3 %collective-permute-start = (bf16[256,768]{1,0:T(8,128)(2,1)}, bf16[256,768]{1,0:T(8,128)(2,1)S(1)}, u32[]{:S(2)}, u32[]{:S(2)}) collective-permute-start(bf16[256,768]{1,0:T(8,128)(2,1)} %refs_0_.1), channel_id=1, source_target_pairs={{0,4},{1,5},{2,6},{3,7},{4,8},{5,9},{6,10},{7,11},{8,12},{9,13},{1... | collective-permute-start | bytes 1179656 | tf_op jit(solution)/shard_map/ppermute | solution.py:50
  6.7 1.0 copy-start
  17.0 3.0 %collective-permute-start.6 = (bf16[256,768]{1,0:T(8,128)(2,1)S(1)}, bf16[256,768]{1,0:T(8,128)(2,1)S(1)}, u32[]{:S(2)}, u32[]{:S(2)}) collective-permute-start(bf16[256,768]{1,0:T(8,128)(2,1)S(1)} %collective-permute-done.1.refs_2_), channel_id=1, source_target_pairs={{0,1},{1,0},{2,3},{3,2},{4,5},{5,4},{6,7},{7,6},{8,9},{9,8},{10,11... | collective-permute-start | bytes 1179656 | tf_op jit(solution)/shard_map/ppermute | solution.py:55
  17.0 3.0 %collective-permute-start.5 = (bf16[256,768]{1,0:T(8,128)(2,1)S(1)}, bf16[256,768]{1,0:T(8,128)(2,1)S(1)}, u32[]{:S(2)}, u32[]{:S(2)}) collective-permute-start(bf16[256,768]{1,0:T(8,128)(2,1)S(1)} %collective-permute-done.refs_0_), channel_id=1, source_target_pairs={{0,1},{1,0},{2,3},{3,2},{4,5},{5,4},{6,7},{7,6},{8,9},{9,8},{10,11... | collective-permute-start | bytes 1179656 | tf_op jit(solution)/shard_map/ppermute | solution.py:55
  17.5 11.0 %collective-permute-start.3 = (bf16[256,768]{1,0:T(8,128)(2,1)S(1)}, bf16[256,768]{1,0:T(8,128)(2,1)S(1)}, u32[]{:S(2)}, u32[]{:S(2)}) collective-permute-start(bf16[256,768]{1,0:T(8,128)(2,1)S(1)} %copy-done), channel_id=1, source_target_pairs={{0,12},{1,13},{2,14},{3,15},{4,0},{5,1},{6,2},{7,3},{8,4},{9,5},{1... | collective-permute-start | bytes 1179656 | tf_op jit(solution)/shard_map/ppermute | solution.py:50
  19.8 10.8 %collective-permute-start.4 = (bf16[256,768]{1,0:T(8,128)(2,1)S(1)}, bf16[256,768]{1,0:T(8,128)(2,1)S(1)}, u32[]{:S(2)}, u32[]{:S(2)}) collective-permute-start(bf16[256,768]{1,0:T(8,128)(2,1)S(1)} %collective-permute-done.refs_0_), channel_id=1, source_target_pairs={{0,2},{1,3},{2,0},{3,1},{4,6},{5,7},{6,4},{7,5},{8,10},{9,11},{10,... | collective-permute-start | bytes 1179656 | tf_op jit(solution)/shard_map/ppermute | solution.py:49
  30.6 1.7 %collective-permute-start.10 = (bf16[256,768]{1,0:T(8,128)(2,1)S(1)}, bf16[256,768]{1,0:T(8,128)(2,1)S(1)}, u32[]{:S(2)}, u32[]{:S(2)}) collective-permute-start(bf16[256,768]{1,0:T(8,128)(2,1)S(1)} %collective-permute-done.4.refs_2_), channel_id=1, source_target_pairs={{0,1},{1,0},{2,3},{3,2},{4,5},{5,4},{6,7},{7,6},{8,9},{9,8},{10,11... | collective-permute-start | bytes 1179656 | tf_op jit(solution)/shard_map/ppermute | solution.py:55
  30.6 2.3 %collective-permute-start.9 = (bf16[256,768]{1,0:T(8,128)(2,1)S(1)}, bf16[256,768]{1,0:T(8,128)(2,1)S(1)}, u32[]{:S(2)}, u32[]{:S(2)}) collective-permute-start(bf16[256,768]{1,0:T(8,128)(2,1)S(1)} %collective-permute-done.3.refs_0_), channel_id=1, source_target_pairs={{0,1},{1,0},{2,3},{3,2},{4,5},{5,4},{6,7},{7,6},{8,9},{9,8},{10,11... | collective-permute-start | bytes 1179656 | tf_op jit(solution)/shard_map/ppermute | solution.py:55
  31.1 12.8 %collective-permute-start.7 = (bf16[256,768]{1,0:T(8,128)(2,1)S(1)}, bf16[256,768]{1,0:T(8,128)(2,1)S(1)}, u32[]{:S(2)}, u32[]{:S(2)}) collective-permute-start(bf16[256,768]{1,0:T(8,128)(2,1)S(1)} %collective-permute-done.4.refs_2_), channel_id=1, source_target_pairs={{0,4},{1,5},{2,6},{3,7},{4,8},{5,9},{6,10},{7,11},{8,12},{9,13},{1... | collective-permute-start | bytes 1179656 | tf_op jit(solution)/shard_map/ppermute | solution.py:50
  31.1 12.8 %collective-permute-start.8 = (bf16[256,768]{1,0:T(8,128)(2,1)S(1)}, bf16[256,768]{1,0:T(8,128)(2,1)S(1)}, u32[]{:S(2)}, u32[]{:S(2)}) collective-permute-start(bf16[256,768]{1,0:T(8,128)(2,1)S(1)} %collective-permute-done.3.refs_0_), channel_id=1, source_target_pairs={{0,2},{1,3},{2,0},{3,1},{4,6},{5,7},{6,4},{7,5},{8,10},{9,11},{10,... | collective-permute-start | bytes 1179656 | tf_op jit(solution)/shard_map/ppermute | solution.py:49
  43.9 5.4 %collective-permute-start.11 = (bf16[256,768]{1,0:T(8,128)(2,1)S(1)}, bf16[256,768]{1,0:T(8,128)(2,1)S(1)}, u32[]{:S(2)}, u32[]{:S(2)}) collective-permute-start(bf16[256,768]{1,0:T(8,128)(2,1)S(1)} %collective-permute-done.7.refs_0_), channel_id=1, source_target_pairs={{0,1},{1,0},{2,3},{3,2},{4,5},{5,4},{6,7},{7,6},{8,9},{9,8},{10,11... | collective-permute-start | bytes 1179656 | tf_op jit(solution)/shard_map/ppermute | solution.py:55
  43.9 5.4 %collective-permute-start.12 = (bf16[256,768]{1,0:T(8,128)(2,1)S(1)}, bf16[256,768]{1,0:T(8,128)(2,1)S(1)}, u32[]{:S(2)}, u32[]{:S(2)}) collective-permute-start(bf16[256,768]{1,0:T(8,128)(2,1)S(1)} %collective-permute-done.8.refs_1_), channel_id=1, source_target_pairs={{0,1},{1,0},{2,3},{3,2},{4,5},{5,4},{6,7},{7,6},{8,9},{9,8},{10,11... | collective-permute-start | bytes 1179656 | tf_op jit(solution)/shard_map/ppermute | solution.py:55
  50.5 8.3 %collective-permute-start.13 = (f32[264,768]{1,0:T(8,128)S(1)}, f32[264,768]{1,0:T(8,128)S(1)}, u32[]{:S(2)}, u32[]{:S(2)}) collective-permute-start(f32[264,768]{1,0:T(8,128)S(1)} %get-tuple-element.95), channel_id=1, source_target_pairs={{0,1},{1,0},{2,3},{3,2},{4,5},{5,4},{6,7},{7,6},{8,9},{9,8},{10,11... | collective-permute-start | bytes 2433032 | tf_op jit(solution)/shard_map/ppermute | solution.py:55
  53.9 5.2 %collective-permute-start.14 = (f32[264,768]{1,0:T(8,128)S(1)}, f32[264,768]{1,0:T(8,128)S(1)}, u32[]{:S(2)}, u32[]{:S(2)}) collective-permute-start(f32[264,768]{1,0:T(8,128)S(1)} %get-tuple-element.97), channel_id=1, source_target_pairs={{0,1},{1,0},{2,3},{3,2},{4,5},{5,4},{6,7},{7,6},{8,9},{9,8},{10,11... | collective-permute-start | bytes 2433032 | tf_op jit(solution)/shard_map/ppermute | solution.py:55
  59.2 12.1 %collective-permute-start.15 = (f16[264,768]{1,0:T(8,128)(2,1)S(1)}, f16[264,768]{1,0:T(8,128)(2,1)S(1)}, u32[]{:S(2)}, u32[]{:S(2)}) collective-permute-start(f16[264,768]{1,0:T(8,128)(2,1)S(1)} %multiply_convert_fusion.2), channel_id=1, source_target_pairs={{0,12},{1,13},{2,14},{3,15},{4,0},{5,1},{6,2},{7,3},{8,4},{9,5},{1... | collective-permute-start | bytes 1216520 | tf_op jit(solution)/shard_map/ppermute | solution.py:50
  59.3 12.1 %collective-permute-start.16 = (f16[264,768]{1,0:T(8,128)(2,1)S(1)}, f16[264,768]{1,0:T(8,128)(2,1)S(1)}, u32[]{:S(2)}, u32[]{:S(2)}) collective-permute-start(f16[264,768]{1,0:T(8,128)(2,1)S(1)} %multiply_convert_fusion.1), channel_id=1, source_target_pairs={{0,2},{1,3},{2,0},{3,1},{4,6},{5,7},{6,4},{7,5},{8,10},{9,11},{10,... | collective-permute-start | bytes 1216520 | tf_op jit(solution)/shard_map/ppermute | solution.py:49
  67.2 4.5 %collective-permute-start.17 = (f32[264,768]{1,0:T(8,128)S(1)}, f32[264,768]{1,0:T(8,128)S(1)}, u32[]{:S(2)}, u32[]{:S(2)}) collective-permute-start(f32[264,768]{1,0:T(8,128)S(1)} %get-tuple-element.103), channel_id=1, source_target_pairs={{0,1},{1,0},{2,3},{3,2},{4,5},{5,4},{6,7},{7,6},{8,9},{9,8},{10,11... | collective-permute-start | bytes 2433032 | tf_op jit(solution)/shard_map/ppermute | solution.py:55
  67.3 4.5 %collective-permute-start.18 = (f32[264,768]{1,0:T(8,128)S(1)}, f32[264,768]{1,0:T(8,128)S(1)}, u32[]{:S(2)}, u32[]{:S(2)}) collective-permute-start(f32[264,768]{1,0:T(8,128)S(1)} %get-tuple-element.106), channel_id=1, source_target_pairs={{0,1},{1,0},{2,3},{3,2},{4,5},{5,4},{6,7},{7,6},{8,9},{9,8},{10,11... | collective-permute-start | bytes 2433032 | tf_op jit(solution)/shard_map/ppermute | solution.py:55
  71.9 13.2 %collective-permute-start.19 = (f16[264,768]{1,0:T(8,128)(2,1)S(1)}, f16[264,768]{1,0:T(8,128)(2,1)S(1)}, u32[]{:S(2)}, u32[]{:S(2)}) collective-permute-start(f16[264,768]{1,0:T(8,128)(2,1)S(1)} %add_convert_fusion.2), channel_id=1, source_target_pairs={{0,4},{1,5},{2,6},{3,7},{4,8},{5,9},{6,10},{7,11},{8,12},{9,13},{1... | collective-permute-start | bytes 1216520 | tf_op jit(solution)/shard_map/ppermute | solution.py:50
  75.1 11.4 %collective-permute-start.20 = (f16[264,768]{1,0:T(8,128)(2,1)S(1)}, f16[264,768]{1,0:T(8,128)(2,1)S(1)}, u32[]{:S(2)}, u32[]{:S(2)}) collective-permute-start(f16[264,768]{1,0:T(8,128)(2,1)S(1)} %add_convert_fusion.1), channel_id=1, source_target_pairs={{0,2},{1,3},{2,0},{3,1},{4,6},{5,7},{6,4},{7,5},{8,10},{9,11},{10,... | collective-permute-start | bytes 1216520 | tf_op jit(solution)/shard_map/ppermute | solution.py:49
  83.3 3.4 %collective-permute-start.21 = (f32[264,768]{1,0:T(8,128)S(1)}, f32[264,768]{1,0:T(8,128)S(1)}, u32[]{:S(2)}, u32[]{:S(2)}) collective-permute-start(f32[264,768]{1,0:T(8,128)S(1)} %get-tuple-element.112), channel_id=1, source_target_pairs={{0,1},{1,0},{2,3},{3,2},{4,5},{5,4},{6,7},{7,6},{8,9},{9,8},{10,11... | collective-permute-start | bytes 2433032 | tf_op jit(solution)/shard_map/ppermute | solution.py:55
  83.4 3.5 %collective-permute-start.22 = (f32[264,768]{1,0:T(8,128)S(1)}, f32[264,768]{1,0:T(8,128)S(1)}, u32[]{:S(2)}, u32[]{:S(2)}) collective-permute-start(f32[264,768]{1,0:T(8,128)S(1)} %get-tuple-element.114), channel_id=1, source_target_pairs={{0,1},{1,0},{2,3},{3,2},{4,5},{5,4},{6,7},{7,6},{8,9},{9,8},{10,11... | collective-permute-start | bytes 2433032 | tf_op jit(solution)/shard_map/ppermute | solution.py:55
  87.0 15.6 %collective-permute-start.23 = (f16[264,768]{1,0:T(8,128)(2,1)S(1)}, f16[264,768]{1,0:T(8,128)(2,1)S(1)}, u32[]{:S(2)}, u32[]{:S(2)}) collective-permute-start(f16[264,768]{1,0:T(8,128)(2,1)S(1)} %add_convert_fusion), channel_id=1, source_target_pairs={{0,12},{1,13},{2,14},{3,15},{4,0},{5,1},{6,2},{7,3},{8,4},{9,5},{1... | collective-permute-start | bytes 1216520 | tf_op jit(solution)/shard_map/ppermute | solution.py:50
  93.6 11.1 %collective-permute-start.24 = (f16[264,768]{1,0:T(8,128)(2,1)S(1)}, f16[264,768]{1,0:T(8,128)(2,1)S(1)}, u32[]{:S(2)}, u32[]{:S(2)}) collective-permute-start(f16[264,768]{1,0:T(8,128)(2,1)S(1)} %multiply_convert_fusion), channel_id=1, source_target_pairs={{0,2},{1,3},{2,0},{3,1},{4,6},{5,7},{6,4},{7,5},{8,10},{9,11},{10,... | collective-permute-start | bytes 1216520 | tf_op jit(solution)/shard_map/ppermute | solution.py:49
  98.9 6.1 %collective-permute-start.25 = (f32[264,768]{1,0:T(8,128)S(1)}, f32[264,768]{1,0:T(8,128)S(1)}, u32[]{:S(2)}, u32[]{:S(2)}) collective-permute-start(f32[264,768]{1,0:T(8,128)S(1)} %get-tuple-element.122), channel_id=1, source_target_pairs={{0,1},{1,0},{2,3},{3,2},{4,5},{5,4},{6,7},{7,6},{8,9},{9,8},{10,11... | collective-permute-start | bytes 2433032 | tf_op jit(solution)/shard_map/ppermute | solution.py:55
  104.9 1.0 copy-start.1
